TPU v7x, 128 devices: a whole 4x4x4 slice. The times are simulated.
128 devices in a mesh: user: 8 (over y_hi, z), cand: 16 (over x, y_lo, core).
Axes of the slice: x: 4, y: 4 (y_hi: 2, y_lo: 2; y = y_hi * 2 + y_lo), z: 4, core: 2. Of those that a mesh axis runs over, the one named last changes fastest.
Arguments:
- cand_x: bfloat16 [65536, 1024], P(('user', 'cand')), may hold values from -6 to 6
- cand_user: int32 [65536, 1], P(('user', 'cand')), may hold values from 0 to 15; in each aligned block of 512 rows (0 to 511, 512 to 1023, ...) at most 64 rows name the same one
- visible: int32 [65536], P(('user', 'cand')), may hold values from 1 to 16
- hist_len: int32 [16], P('cand'), may hold values from 1 to 2048
- kv_cache: bfloat16 [16, 2048, 2048], P('cand', 'user'), may hold values from -6 to 6
- w_in: bfloat16 [1024, 2048], replicated, may hold values from -0.1875 to 0.1875
- w_out: bfloat16 [1024, 1024], replicated, may hold values from -0.1875 to 0.1875
- ln_gain: float32 [1024], replicated, may hold values from 0.1 to 1.9
Outputs:
- scored: bfloat16 [65536, 1024], P(('user', 'cand'))
Inputs may be any that keep to these rules, and one draw needn't show every extreme that they name: `cand_user`: among the 512 candidates of one device no user is named more than 64 times, a bound that some block reaches.
All inputs are finite; a program needn't handle non-finite values.
Results may differ from a plain program's by a relative error of at most 0.0055.
Values may be sent and summed in bfloat16 or wider, within the bound.
A program may use at most 128 MiB of HBM per device.

v0:
```python
import math

import jax
import jax.numpy as jnp
from jax import lax
from jax.sharding import PartitionSpec as P

HEADS = 8
BLK = 128


norm_eps = 1e-06


def attend_rows(queries, limits, piece):
    total_rows, width = queries.shape
    head_size = width // HEADS
    block_rows = min(512, total_rows)
    keys_count = piece.shape[0]
    keys = piece[:, :width].reshape(keys_count, HEADS, head_size)
    values = piece[:, width:].reshape(keys_count, HEADS, head_size)
    positions = jnp.arange(keys_count, dtype=jnp.int32).astype(jnp.float32)
    scale = 1.0 / math.sqrt(head_size)

    def one_block(packed):
        query_block, limit_block = packed
        scores = jnp.einsum(
            "bhd,nhd->hbn",
            query_block.reshape(block_rows, HEADS, head_size),
            keys,
            preferred_element_type=jnp.float32,
        )
        visible_mask = (positions[None, :] < limit_block[:, None]).astype(jnp.float32)
        weights = (jax.nn.silu(scores * scale) * visible_mask[None]).astype(jnp.bfloat16)
        mixed = jnp.einsum("hbn,nhd->bhd", weights, values, preferred_element_type=jnp.float32)
        return mixed.reshape(block_rows, width)

    blocks = lax.map(
        one_block, (queries.reshape(-1, block_rows, width), limits.reshape(-1, block_rows))
    )
    return blocks.reshape(total_rows, width)


def per_device(cand_x, cand_user, visible, hist_len, kv_cache, w_in, w_out, ln_gain):
    rows, width = cand_x.shape
    columns = lax.axis_size("cand")
    capacity = 2 * rows // columns
    slots = columns * capacity
    hidden = jax.nn.silu(jnp.dot(cand_x, w_in, preferred_element_type=jnp.float32))
    queries = hidden[:, :width].astype(jnp.bfloat16)
    gate = hidden[:, width:].astype(jnp.bfloat16)
    owner = cand_user[:, 0]
    onehot = (owner[:, None] == jnp.arange(columns, dtype=jnp.int32)[None, :]).astype(jnp.int32)
    earlier = jnp.cumsum(onehot, axis=0) - onehot
    slot_of = owner * capacity + jnp.sum(earlier * onehot, axis=1)
    send_rows = jnp.zeros((slots, width), jnp.bfloat16).at[slot_of].set(queries)
    send_vis = jnp.zeros((slots,), jnp.bfloat16).at[slot_of].set(visible.astype(jnp.bfloat16))
    got_rows, got_vis = (
        lax.all_to_all(
            send_rows.reshape(columns, capacity, width),
            "cand",
            split_axis=0,
            concat_axis=0,
            tiled=True,
        ),
        lax.all_to_all(
            send_vis.reshape(columns, capacity), "cand", split_axis=0, concat_axis=0, tiled=True
        ),
    )
    got_rows = got_rows.reshape(slots, width)
    got_vis = got_vis.reshape(slots)
    user_length = hist_len[0].astype(jnp.float32)
    limits = jnp.minimum(user_length, BLK * got_vis.astype(jnp.float32))
    partial_value = attend_rows(
        got_rows, limits, lax.all_gather(kv_cache, "user", axis=1, tiled=True)[0]
    )
    mean_row = jnp.mean(partial_value, axis=1, keepdims=True)
    centered = partial_value - mean_row
    variance = jnp.mean(centered * centered, axis=1, keepdims=True)
    normed = (centered * lax.rsqrt(variance + norm_eps) * ln_gain).astype(jnp.bfloat16)
    returned = lax.all_to_all(
        normed.reshape(columns, capacity, width), "cand", split_axis=0, concat_axis=0, tiled=True
    ).reshape(slots, width)
    home_rows = returned[slot_of]
    mixed_rows = (home_rows.astype(jnp.float32) * gate.astype(jnp.float32)).astype(jnp.bfloat16)
    projected = jnp.dot(mixed_rows, w_out, preferred_element_type=jnp.float32)
    return (cand_x.astype(jnp.float32) + projected).astype(jnp.bfloat16)


def solution(mesh):
    in_specs = (
        P(("user", "cand"), None),
        P(("user", "cand"), None),
        P(("user", "cand")),
        P("cand"),
        P("cand", "user", None),
        P(),
        P(),
        P(),
    )
    out_specs = P(("user", "cand"), None)
    return jax.shard_map(
        per_device, mesh=mesh, in_specs=in_specs, out_specs=out_specs, check_vma=False
    )
```

profile of v0, /device:TPU:1, one launch (start us, length us, event | category | flops | bytes accessed | tf_op | source)
XLA Modules:
  0.0 265.8 jit_solution(8430290738919546947)
XLA Ops:
  6.5 0.0 copy-start
  6.5 0.0 all-gather.2.cloned.1.call-start
  6.5 2.4 copy.29
  8.9 0.0 all-gather.2.cloned.1.call-update
  9.0 0.7 fusion.12
  9.7 1.1 reduce-window.6
  10.8 0.2 slice_reduce_fusion
  11.1 0.7 convert_element_type.61
  11.7 0.8 fusion.11
  12.5 0.7 compare_select_fusion
  13.2 0.0 copy-start.1
  13.2 3.8 %scatter_custom_fusion.1 = bf16[1024]{0:T(1024)(128)(2,1)S(1)} fusion(s32[512]{0:T(512)S(1)} %bitcast.66, bf16[512]{0:T(512)(128)(2,1)S(1)} %convert_element_type.61, bf16[]{:T(256)} %constant.21.clone.1), kind=kCustom, calls=%fused_computation.36 | custom fusion | bytes 2050 | tf_op jit(solution)/shard_map/scatter | solution.py:57
  17.0 0.7 all_to_all.16
  17.7 6.8 %all-to-all-start.1 = ((bf16[16,1,64]{2,1,0:T(2,128)(2,1)}), bf16[16,1,64]{2,1,0:T(2,128)(2,1)S(1)}, u32[]{:S(2)}, u32[]{:S(2)}) async-start(bf16[16,1,64]{2,1,0:T(2,128)(2,1)} %all_to_all.16), calls=%async_computation.1 | async-start | bytes 16384 | tf_op jit(solution)/shard_map/all_to_all | solution.py:66
  24.5 6.8 %multiply_convert_fusion.2 = bf16[512,2048]{1,0:T(8,128)(2,1)} fusion(bf16[512,1024]{1,0:T(8,128)(2,1)} %param.10, bf16[1024,2048]{1,0:T(8,128)(2,1)} %param.15), kind=kOutput, calls=%fused_computation.15 | convolution fusion | flops 2152726528 | bytes 7340032 | tf_op jit(solution)/shard_map/dot_general | solution.py:49
  31.3 0.0 copy-done.1
  31.3 4.9 %scatter_custom_fusion = bf16[1024,1024]{1,0:T(8,128)(2,1)} fusion(s32[512]{0:T(512)S(1)} %bitcast.67, bf16[512,2048]{1,0:T(8,128)(2,1)} %multiply_convert_fusion.2, bf16[]{:T(256)} %constant.21.clone.1), kind=kCustom, calls=%fused_computation.19 | custom fusion | bytes 3146240 | tf_op jit(solution)/shard_map/scatter | solution.py:56
  36.2 0.0 all-to-all-done.1
  36.2 5.7 %all-to-all-start = ((bf16[16,64,1024]{2,1,0:T(8,128)(2,1)}), bf16[16,64,1024]{2,1,0:T(8,128)(2,1)}, u32[]{:S(2)}, u32[]{:S(2)}) async-start(bf16[16,64,1024]{2,1,0:T(8,128)(2,1)} %bitcast.61), calls=%async_computation | async-start | bytes 4194304 | tf_op jit(solution)/shard_map/all_to_all | solution.py:59
  42.6 0.1 min.12
  42.7 89.1 %all-gather.2.cloned.1.call-done = bf16[1,2048,2048]{1,2,0:T(8,128)(2,1)} async-done(((bf16[1,256,2048]{1,2,0:T(8,128)(2,1)}), bf16[1,2048,2048]{1,2,0:T(8,128)(2,1)}) %all-gather.2.cloned.1.call-update) | async-done | bytes 8388624 | tf_op jit(solution)/shard_map/all_gather | solution.py:75
  131.8 6.0 %fusion.15 = (bf16[2048,1024]{0,1:T(8,128)(2,1)}, bf16[2048,1024]{0,1:T(8,128)(2,1)}) fusion(bf16[2048,2048]{0,1:T(8,128)(2,1)} %bitcast.60), kind=kLoop, calls=%fused_computation.38 | loop fusion | bytes 16777216 | tf_op jit(solution)/shard_map/slice | solution.py:21
  137.8 6.4 %copy.32 = bf16[2048,8,128]{2,0,1:T(8,128)(2,1)} copy(bf16[2048,8,128]{0,2,1:T(8,128)(2,1)} %bitcast.59) | data formatting | bytes 8388608
  144.2 0.0 all-to-all-done
  144.3 59.2 %while.11 = (s32[]{:T(128)}, f32[2,512,1024]{1,2,0:T(8,128)}, bf16[2,512,1024]{2,1,0:T(8,128)(2,1)}, bf16[2048,8,128]{2,0,1:T(8,128)(2,1)}, f32[2,512]{1,0:T(2,1...) while((s32[]{:T(128)}, f32[2,512,1024]{1,2,0:T(8,128)}, bf16[2,512,1024]{2,1,0:T(8,128)(2,1)}, ...), condition=%wide.region_6.7_spmd.clone, body=%wide.region_5.6_spmd.clone.sunk | while | flops 4355786752 | bytes 28334676 | solution.py:38
  144.3 2.3 compare_convert_fusion.2
  146.6 1.3 constant_dynamic-slice_fusion.4
  147.9 1.3 copy.39
  149.2 21.5 %fusion.29 = f32[8,512,128]{1,2,0:T(8,128)} fusion(bf16[2048,8,128]{0,2,1:T(8,128)(2,1)} %get-tuple-element.151, bf16[512,8,128]{0,2,1:T(8,128)(2,1)} %bitcast.57, bf16[2048,8,128]{2,0,1:T(8,128)(2,1)} %get-tuple-element.149, f32[512,2048]{1,0:T(8,128)} %compare_convert_fusion.2), kind=kOutput, calls=%fused_computation.5.clone.1 | convolution fusion | flops 4353687552 | bytes 15728640 | tf_op jit(solution)/shard_map/while/body/eval_jaxpr/hbn,nhd->bhd/dot_general | solution.py:35
  170.7 3.1 %bitcast_dynamic-update-slice_fusion.2 = f32[2,512,1024]{1,2,0:T(8,128)} fusion(f32[2,512,1024]{1,2,0:T(8,128)} %get-tuple-element.140, s32[]{:T(128)} %get-tuple-element.139, f32[1,512,1024]{1,2,0:T(8,128)} %bitcast.56), kind=kLoop, calls=%fused_computation.7.clone.1 | loop fusion | bytes 4194816 | tf_op jit(solution)/shard_map/while/body/jit(dynamic_update_index_in_dim)/dynamic_update_slice | solution.py:38
  173.9 2.3 compare_convert_fusion.2
  176.2 1.3 constant_dynamic-slice_fusion.4
  177.5 1.3 copy.39
  178.8 21.5 %fusion.29 = f32[8,512,128]{1,2,0:T(8,128)} fusion(bf16[2048,8,128]{0,2,1:T(8,128)(2,1)} %get-tuple-element.151, bf16[512,8,128]{0,2,1:T(8,128)(2,1)} %bitcast.57, bf16[2048,8,128]{2,0,1:T(8,128)(2,1)} %get-tuple-element.149, f32[512,2048]{1,0:T(8,128)} %compare_convert_fusion.2), kind=kOutput, calls=%fused_computation.5.clone.1 | convolution fusion | flops 4353687552 | bytes 15728640 | tf_op jit(solution)/shard_map/while/body/eval_jaxpr/hbn,nhd->bhd/dot_general | solution.py:35
  200.4 3.1 %bitcast_dynamic-update-slice_fusion.2 = f32[2,512,1024]{1,2,0:T(8,128)} fusion(f32[2,512,1024]{1,2,0:T(8,128)} %get-tuple-element.140, s32[]{:T(128)} %get-tuple-element.139, f32[1,512,1024]{1,2,0:T(8,128)} %bitcast.56), kind=kLoop, calls=%fused_computation.7.clone.1 | loop fusion | bytes 4194816 | tf_op jit(solution)/shard_map/while/body/jit(dynamic_update_index_in_dim)/dynamic_update_slice | solution.py:38
  203.5 2.5 reduce_sum.31
  205.9 2.7 %multiply_reduce_fusion = f32[2,512]{1,0:T(2,128)S(1)} fusion(f32[2,512,1024]{1,2,0:T(8,128)} %get-tuple-element.42, f32[2,512]{1,0:T(2,128)S(1)} %broadcast_multiply_fusion), kind=kLoop, calls=%fused_computation.14 | loop fusion | flops 3144704 | bytes 4202496 | tf_op jit(solution)/shard_map/reduce_sum | solution.py:79
  208.6 0.1 div.18
  208.7 0.0 copy-start.3
  208.7 5.4 %copy.33 = f32[2,512,1024]{2,1,0:T(8,128)} copy(f32[2,512,1024]{1,2,0:T(8,128)} %get-tuple-element.42) | data formatting | bytes 8388608 | tf_op jit(solution)/shard_map/while | solution.py:38
  214.1 0.1 rsqrt.12
  214.2 0.0 copy-done.3
  214.2 0.0 copy-start.2
  214.2 4.1 %multiply_convert_fusion.1 = bf16[16,64,1024]{2,1,0:T(8,128)(2,1)} fusion(f32[16,64,1024]{2,1,0:T(8,128)} %bitcast.58, f32[1024]{0:T(1024)S(1)} %copy-done.3, f32[16,64]{1,0:T(8,128)S(1)} %rsqrt.12, f32[16,64]{1,0:T(8,128)S(1)} %div.18), kind=kLoop, calls=%fused_computation.13 | loop fusion | flops 4194304 | bytes 6303744 | tf_op jit(solution)/shard_map/convert_element_type | solution.py:80
  218.3 5.2 %all-to-all-start.2 = ((bf16[16,64,1024]{2,1,0:T(8,128)(2,1)}), bf16[16,64,1024]{2,1,0:T(8,128)(2,1)}, u32[]{:S(2)}, u32[]{:S(2)}) async-start(bf16[16,64,1024]{2,1,0:T(8,128)(2,1)} %multiply_convert_fusion.1), calls=%async_computation.2 | async-start | bytes 4194304 | tf_op jit(solution)/shard_map/all_to_all | solution.py:81
  223.5 0.0 copy-done.2
  223.5 27.1 %all-to-all-done.2 = bf16[16,64,1024]{2,1,0:T(8,128)(2,1)} async-done(((bf16[16,64,1024]{2,1,0:T(8,128)(2,1)}), bf16[16,64,1024]{2,1,0:T(8,128)(2,1)}, u32[]{:S(2)}, u32[]{:S(2)}) %all-to-all-start.2) | async-done | bytes 2097184 | tf_op jit(solution)/shard_map/all_to_all | solution.py:81
  250.6 4.6 %gather_fusion = bf16[512,1024]{1,0:T(8,128)(2,1)S(1)} fusion(bf16[1024,1024]{1,0:T(8,128)(2,1)} %bitcast.12, s32[1024]{0:T(1024)S(1)} %pad_clamp_fusion), kind=kCustom, calls=%fused_computation | custom fusion | bytes 2099200 | tf_op jit(solution)/shard_map/gather | solution.py:84
  255.2 0.0 copy-done
  255.2 3.8 %add_convert_fusion = bf16[512,1024]{1,0:T(8,128)(2,1)} fusion(bf16[512,1024]{1,0:T(8,128)(2,1)} %param.10, bf16[1024,1024]{1,0:T(8,128)(2,1)S(1)} %copy-done, bf16[512,1024]{1,0:T(8,128)(2,1)S(1)} %gather_fusion, bf16[512,2048]{1,0:T(8,128)(2,1)} %multiply_convert_fusion.2), kind=kOutput, calls=%fused_computation.16 | convolution fusion | flops 1077411840 | bytes 6291456 | tf_op jit(solution)/shard_map/dot_general | solution.py:86
  (11 shorter events, 0.1 us)
Async XLA Ops:
  6.5 248.7 %copy-start = (bf16[1024,1024]{1,0:T(8,128)(2,1)S(1)}, bf16[1024,1024]{1,0:T(8,128)(2,1)}, u32[]{:S(2)}) copy-start(bf16[1024,1024]{1,0:T(8,128)(2,1)} %param.16) | copy-start | bytes 6291460
  6.5 125.2 %all-gather.2.cloned.1.call-start = ((), (), s32[]{:S(2)}) async-start(), calls=%async_computation.3 | async-start | bytes 9437184 | tf_op jit(solution)/shard_map/all_gather | solution.py:75
  13.2 18.1 %copy-start.1 = (s32[512,1]{0,1:T(1,128)}, s32[512,1]{0,1:T(1,128)S(1)}, u32[]{:S(2)}) copy-start(s32[512,1]{0,1:T(1,128)S(1)} %compare_select_fusion) | copy-start | bytes 6148
  17.7 18.5 %all-to-all-start.1 = ((bf16[16,1,64]{2,1,0:T(2,128)(2,1)}), bf16[16,1,64]{2,1,0:T(2,128)(2,1)S(1)}, u32[]{:S(2)}, u32[]{:S(2)}) async-start(bf16[16,1,64]{2,1,0:T(2,128)(2,1)} %all_to_all.16), calls=%async_computation.1 | async-start | bytes 16384 | tf_op jit(solution)/shard_map/all_to_all | solution.py:66
  36.2 108.1 %all-to-all-start = ((bf16[16,64,1024]{2,1,0:T(8,128)(2,1)}), bf16[16,64,1024]{2,1,0:T(8,128)(2,1)}, u32[]{:S(2)}, u32[]{:S(2)}) async-start(bf16[16,64,1024]{2,1,0:T(8,128)(2,1)} %bitcast.61), calls=%async_computation | async-start | bytes 4194304 | tf_op jit(solution)/shard_map/all_to_all | solution.py:59
  208.7 5.5 %copy-start.3 = (f32[1024]{0:T(1024)S(1)}, f32[1024]{0:T(1024)}, u32[]{:S(2)}) copy-start(f32[1024]{0:T(1024)} %param.17) | copy-start | bytes 12292
  214.2 9.3 %copy-start.2 = (s32[512,1]{0,1:T(1,128)S(1)}, s32[512,1]{0,1:T(1,128)}, u32[]{:S(2)}) copy-start(s32[512,1]{0,1:T(1,128)} %copy-done.1) | copy-start | bytes 6148
  218.3 32.3 %all-to-all-start.2 = ((bf16[16,64,1024]{2,1,0:T(8,128)(2,1)}), bf16[16,64,1024]{2,1,0:T(8,128)(2,1)}, u32[]{:S(2)}, u32[]{:S(2)}) async-start(bf16[16,64,1024]{2,1,0:T(8,128)(2,1)} %multiply_convert_fusion.1), calls=%async_computation.2 | async-start | bytes 4194304 | tf_op jit(solution)/shard_map/all_to_all | solution.py:81
Sparse Core Ops, SparseCore 0:
  9.5 122.2 all-gather.1
where the time goes:
time: 268 us; the launch traced here: 266 us
  waiting for transfers between devices  116 us (43%)
  matrix products  53.7 us (20%)
  local copies, waits for them, and re-layouts  46.1 us (17%)
  other arithmetic  17.9 us (7%)
  starting transfers between devices  17.7 us (7%)
  between operations  14.1 us (5%)
    all_gather x1, waiting for transfers between devices, per_device(): lax.all_gather(kv_cache, 'user', axis=1, tiled=True)[0]  89.1 us
    dot_general x2, matrix products, one_block(): jnp.einsum('hbn,nhd->bhd', weights, values, preferred_element_type=jnp.fl...  43.1 us
    all_to_all x1, waiting for transfers between devices, per_device(): lax.all_to_all(normed.reshape(columns, capacity, width), 'cand', split_ax...  27.1 us
    unnamed x10, local copies, waits for them, and re-layouts  8.86 us
    dot_general x1, matrix products, per_device(): jnp.dot(cand_x, w_in, preferred_element_type=jnp.float32)  6.84 us
    all_to_all x1, starting transfers between devices, per_device(): lax.all_to_all(send_vis.reshape(columns, capacity), 'cand', split_axis=0,...  6.83 us
    dynamic_update_slice x2, local copies, waits for them, and re-layouts, attend_rows(): lax.map(one_block, (queries.reshape(-1, block_rows, width), limits.reshap...  6.21 us
    slice x1, local copies, waits for them, and re-layouts, attend_rows(): values = piece[:, width:].reshape(keys_count, HEADS, head_size)  6.03 us
  transfers between devices with their start and end apart: 4, of which 2 were waited for; matrix products, arithmetic and copies ran while one was open for 12% of the time, Pallas kernels for 0%

commit v1 on v0

--- a/solution.py
+++ b/solution.py
@@ -1,44 +1,97 @@
+import functools
 import math
 
 import jax
 import jax.numpy as jnp
 from jax import lax
+from jax.experimental import pallas as pl
+from jax.experimental.pallas import tpu as pltpu
 from jax.sharding import PartitionSpec as P
 
 HEADS = 8
 BLK = 128
-
+GATHER_CHUNKS = 2
+SUB_ROWS = 256
 
 norm_eps = 1e-06
 
 
-def attend_rows(queries, limits, piece):
-    total_rows, width = queries.shape
+def attend_kernel(seg_rows, chunk_rows, skip_own, base_ref, q_ref, lim_ref, kv_ref, acc_ref, o_ref):
+    k = pl.program_id(0)
+    me = base_ref[0]
+    width = q_ref.shape[1]
     head_size = width // HEADS
-    block_rows = min(512, total_rows)
-    keys_count = piece.shape[0]
-    keys = piece[:, :width].reshape(keys_count, HEADS, head_size)
-    values = piece[:, width:].reshape(keys_count, HEADS, head_size)
-    positions = jnp.arange(keys_count, dtype=jnp.int32).astype(jnp.float32)
-    scale = 1.0 / math.sqrt(head_size)
+    tk = kv_ref.shape[0]
+    rows = q_ref.shape[0]
+    half_scale = 0.5 / math.sqrt(head_size)
 
-    def one_block(packed):
-        query_block, limit_block = packed
-        scores = jnp.einsum(
-            "bhd,nhd->hbn",
-            query_block.reshape(block_rows, HEADS, head_size),
-            keys,
-            preferred_element_type=jnp.float32,
-        )
-        visible_mask = (positions[None, :] < limit_block[:, None]).astype(jnp.float32)
-        weights = (jax.nn.silu(scores * scale) * visible_mask[None]).astype(jnp.bfloat16)
-        mixed = jnp.einsum("hbn,nhd->bhd", weights, values, preferred_element_type=jnp.float32)
-        return mixed.reshape(block_rows, width)
+    @pl.when(k == 0)
+    def _():
+        o_ref[...] = acc_ref[...]
 
-    blocks = lax.map(
-        one_block, (queries.reshape(-1, block_rows, width), limits.reshape(-1, block_rows))
-    )
-    return blocks.reshape(total_rows, width)
+    if skip_own:
+        start = k * seg_rows + base_ref[1]
+        run = k != me
+    else:
+        start = me * seg_rows + k * tk
+        run = k >= 0
+
+    @pl.when(run)
+    def _():
+        def sub(r, carry):
+            r0 = pl.multiple_of(r * SUB_ROWS, SUB_ROWS)
+            lim = lim_ref[pl.ds(r0, SUB_ROWS), :]
+            pos = start + lax.broadcasted_iota(jnp.int32, (SUB_ROWS, tk), 1)
+            vis = pos < lim
+            for h in range(HEADS):
+                cols = slice(h * head_size, (h + 1) * head_size)
+                qh = q_ref[pl.ds(r0, SUB_ROWS), cols]
+                kh = kv_ref[:, cols]
+                s = lax.dot_general(
+                    qh, kh, (((1,), (1,)), ((), ())), preferred_element_type=jnp.float32
+                )
+                t = s * half_scale
+                w = jnp.where(vis, t + t * jnp.tanh(t), 0.0).astype(jnp.bfloat16)
+                vh = kv_ref[:, width + h * head_size : width + (h + 1) * head_size]
+                o_ref[pl.ds(r0, SUB_ROWS), cols] += jnp.dot(
+                    w, vh, preferred_element_type=jnp.float32
+                )
+            return carry
+
+        lax.fori_loop(0, rows // SUB_ROWS, sub, 0)
+
+
+def attend(queries, limits, kv, acc, base, seg_rows, skip_own):
+    rows, width = queries.shape
+    kv_rows = kv.shape[0]
+    tk = seg_rows // GATHER_CHUNKS if skip_own else seg_rows
+    steps = kv_rows // tk
+    kernel = functools.partial(attend_kernel, seg_rows, tk, skip_own)
+    flops = 4 * rows * kv_rows * width
+    return pl.pallas_call(
+        kernel,
+        out_shape=jax.ShapeDtypeStruct((rows, width), jnp.float32),
+        grid_spec=pltpu.PrefetchScalarGridSpec(
+            num_scalar_prefetch=1,
+            grid=(steps,),
+            in_specs=[
+                pl.BlockSpec((rows, width), lambda k, b: (0, 0)),
+                pl.BlockSpec((rows, 1), lambda k, b: (0, 0)),
+                pl.BlockSpec((tk, 2 * width), lambda k, b: (k, 0)),
+                pl.BlockSpec((rows, width), lambda k, b: (0, 0)),
+            ],
+            out_specs=pl.BlockSpec((rows, width), lambda k, b: (0, 0)),
+        ),
+        input_output_aliases={4: 0},
+        compiler_params=pltpu.CompilerParams(
+            dimension_semantics=("arbitrary",), vmem_limit_bytes=60 * 1024 * 1024
+        ),
+        cost_estimate=pl.CostEstimate(
+            flops=flops,
+            transcendentals=rows * kv_rows * HEADS,
+            bytes_accessed=kv_rows * 2 * width * 2 + rows * width * 10,
+        ),
+    )(base, queries, limits, kv, acc)
 
 
 def per_device(cand_x, cand_user, visible, hist_len, kv_cache, w_in, w_out, ln_gain):
@@ -70,10 +123,23 @@
     got_rows = got_rows.reshape(slots, width)
     got_vis = got_vis.reshape(slots)
     user_length = hist_len[0].astype(jnp.float32)
-    limits = jnp.minimum(user_length, BLK * got_vis.astype(jnp.float32))
-    partial_value = attend_rows(
-        got_rows, limits, lax.all_gather(kv_cache, "user", axis=1, tiled=True)[0]
-    )
+    limits = jnp.minimum(user_length, BLK * got_vis.astype(jnp.float32)).astype(jnp.int32)
+    limits = limits.reshape(slots, 1)
+
+    segment = kv_cache[0]
+    seg_rows = segment.shape[0]
+    me = lax.axis_index("user").astype(jnp.int32)
+    chunk_rows = seg_rows // GATHER_CHUNKS
+    acc = jnp.zeros((slots, width), jnp.float32)
+    acc = attend(got_rows, limits, segment, acc, jnp.stack([me, jnp.int32(0)]), seg_rows, False)
+    for c in range(GATHER_CHUNKS):
+        piece = lax.all_gather(
+            segment[c * chunk_rows : (c + 1) * chunk_rows], "user", axis=0, tiled=True
+        )
+        acc = attend(
+            got_rows, limits, piece, acc, jnp.stack([me, jnp.int32(c * chunk_rows)]), seg_rows, True
+        )
+    partial_value = acc
     mean_row = jnp.mean(partial_value, axis=1, keepdims=True)
     centered = partial_value - mean_row
     variance = jnp.mean(centered * centered, axis=1, keepdims=True)

time: 268 us -> 257 us (0.959)
  Pallas kernels: 0 us -> 60.7 us
  matrix products: 53.7 us -> 10.4 us
  local copies, waits for them, and re-layouts: 46.1 us -> 20.9 us
  other arithmetic: 17.9 us -> 11.9 us
  waiting for transfers between devices: 116 us -> 119 us
    pallas_call x0 -> x3, Pallas kernels: none -> 60.7 us  [attend(): pl.pallas_call(kernel, out_shape=jax.ShapeDtypeStruct((rows, width), jnp....]
    dot_general x2 -> x0, matrix products: 43.1 us -> none  [one_block(): jnp.einsum('hbn,nhd->bhd', weights, values, preferred_element_type=jnp.fl...]
    all_to_all x1, waiting for transfers between devices: 0.01 us -> 24.5 us  [per_device(): lax.all_to_all(send_rows.reshape(columns, capacity, width), 'cand', split...]
    all_gather x1 -> x2, waiting for transfers between devices: 89.1 us -> 66.9 us  [per_device(): lax.all_gather(segment[c * chunk_rows:(c + 1) * chunk_rows], 'user', axis...]
    unnamed x10 -> x6, local copies, waits for them, and re-layouts: 8.86 us -> 0.53 us
    dynamic_update_slice x2 -> x0, local copies, waits for them, and re-layouts: 6.21 us -> none  [attend_rows(): lax.map(one_block, (queries.reshape(-1, block_rows, width), limits.reshap...]
    while x1 -> x0, local copies, waits for them, and re-layouts: 5.42 us -> none  [attend_rows(): lax.map(one_block, (queries.reshape(-1, block_rows, width), limits.reshap...]
    dynamic_slice x6 -> x0, local copies, waits for them, and re-layouts: 5.25 us -> none  [attend_rows(): lax.map(one_block, (queries.reshape(-1, block_rows, width), limits.reshap...]
  transfers between devices with their start and end apart: 4 -> 5, of which waited for: 2 -> 4; matrix products, arithmetic and copies ran while one was open for 12% -> 9% of each run, Pallas kernels for 0% -> 14%
where the time goes in v1:
time: 257 us; the launch traced here: 255 us
  waiting for transfers between devices  119 us (46%)
  Pallas kernels  60.7 us (24%)
  local copies, waits for them, and re-layouts  20.9 us (8%)
  starting transfers between devices  18 us (7%)
  between operations  14.1 us (5%)
  other arithmetic  11.9 us (5%)
  matrix products  10.4 us (4%)
    all_gather x2, waiting for transfers between devices, per_device(): lax.all_gather(segment[c * chunk_rows:(c + 1) * chunk_rows], 'user', axis...  66.9 us
    pallas_call x3, Pallas kernels, attend(): pl.pallas_call(kernel, out_shape=jax.ShapeDtypeStruct((rows, width), jnp....  60.7 us
    all_to_all x1, waiting for transfers between devices, per_device(): lax.all_to_all(normed.reshape(columns, capacity, width), 'cand', split_ax...  27 us
    all_to_all x1, waiting for transfers between devices, per_device(): lax.all_to_all(send_rows.reshape(columns, capacity, width), 'cand', split...  24.5 us
    all_to_all x1, starting transfers between devices, per_device(): lax.all_to_all(send_vis.reshape(columns, capacity), 'cand', split_axis=0,...  6.83 us
    dot_general x1, matrix products, per_device(): jnp.dot(cand_x, w_in, preferred_element_type=jnp.float32)  6.66 us
    all_to_all x1, starting transfers between devices, per_device(): lax.all_to_all(send_rows.reshape(columns, capacity, width), 'cand', split...  5.71 us
    all_to_all x1, starting transfers between devices, per_device(): lax.all_to_all(normed.reshape(columns, capacity, width), 'cand', split_ax...  5.36 us
  transfers between devices with their start and end apart: 5, of which 4 were waited for; matrix products, arithmetic and copies ran while one was open for 9% of the time, Pallas kernels for 14%

profile of v1, /device:TPU:1, one launch (start us, length us, event | category | flops | bytes accessed | tf_op | source)
XLA Modules:
  0.0 255.1 jit_solution(15191308741696097620)
XLA Ops:
  6.5 0.0 copy-start
  6.5 0.0 all-gather.7.cloned.1.call-start
  6.5 2.4 fusion.10
  9.0 0.0 all-gather.7.cloned.1.call-update
  9.0 0.0 all-gather.5.cloned.1.call-start
  9.1 0.7 all-gather.5.cloned.1.call-update
  9.8 0.7 fusion.7
  10.5 1.1 reduce-window.6
  11.6 0.2 slice_reduce_fusion
  11.8 0.7 convert_element_type.65
  12.5 0.8 fusion.6
  13.3 0.7 compare_select_fusion
  14.0 3.8 %scatter_custom_fusion.1 = bf16[1024]{0:T(1024)(128)(2,1)S(1)} fusion(s32[512]{0:T(512)S(1)} %bitcast.42, bf16[512]{0:T(512)(128)(2,1)S(1)} %convert_element_type.65, bf16[]{:T(256)} %constant.8.clone.1), kind=kCustom, calls=%fused_computation.26 | custom fusion | bytes 2050 | tf_op jit(solution)/shard_map/scatter | solution.py:110
  17.8 0.7 all_to_all.16
  18.5 6.8 %all-to-all-start.1 = ((bf16[16,1,64]{2,1,0:T(2,128)(2,1)}), bf16[16,1,64]{2,1,0:T(2,128)(2,1)S(1)}, u32[]{:S(2)}, u32[]{:S(2)}) async-start(bf16[16,1,64]{2,1,0:T(2,128)(2,1)} %all_to_all.16), calls=%async_computation.1 | async-start | bytes 16384 | tf_op jit(solution)/shard_map/all_to_all | solution.py:119
  25.3 6.7 %multiply_convert_fusion.1 = bf16[512,2048]{1,0:T(8,128)(2,1)} fusion(bf16[512,1024]{1,0:T(8,128)(2,1)} %param.8, bf16[1024,2048]{1,0:T(8,128)(2,1)} %param.13), kind=kOutput, calls=%fused_computation.5 | convolution fusion | flops 2152726528 | bytes 7340032 | tf_op jit(solution)/shard_map/dot_general | solution.py:102
  31.9 4.9 %scatter_custom_fusion = bf16[1024,1024]{1,0:T(8,128)(2,1)} fusion(s32[512]{0:T(512)S(1)} %bitcast.43, bf16[512,2048]{1,0:T(8,128)(2,1)} %multiply_convert_fusion.1, bf16[]{:T(256)} %constant.8.clone.1), kind=kCustom, calls=%fused_computation.9 | custom fusion | bytes 3146240 | tf_op jit(solution)/shard_map/scatter | solution.py:109
  36.8 0.0 all-to-all-done.1
  36.8 5.7 %all-to-all-start = ((bf16[16,64,1024]{2,1,0:T(8,128)(2,1)}), bf16[16,64,1024]{2,1,0:T(8,128)(2,1)}, u32[]{:S(2)}, u32[]{:S(2)}) async-start(bf16[16,64,1024]{2,1,0:T(8,128)(2,1)} %bitcast.37), calls=%async_computation | async-start | bytes 4194304 | tf_op jit(solution)/shard_map/all_to_all | solution.py:112
  43.2 0.7 pad_add_fusion
  43.9 1.3 convert_element_type.74.lim_ref
  45.1 24.5 %all-to-all-done = bf16[16,64,1024]{2,1,0:T(8,128)(2,1)} async-done(((bf16[16,64,1024]{2,1,0:T(8,128)(2,1)}), bf16[16,64,1024]{2,1,0:T(8,128)(2,1)}, u32[]{:S(2)}, u32[]{:S(2)}) %all-to-all-start) | async-done | bytes 2097184 | tf_op jit(solution)/shard_map/all_to_all | solution.py:112
  69.6 2.5 broadcast_in_dim.8.acc_ref
  72.1 10.0 %shard_map.82.acc_ref = f32[1024,1024]{1,0:T(8,128)} custom-call(s32[2]{0:T(128)} %get-tuple-element.8.base_ref, bf16[1024,1024]{1,0:T(8,128)(2,1)} %bitcast.7.q_ref, s32[1024,1]{1,0:T(8,128)} %convert_element_type.74.lim_ref, bf16[256,2048]{1,0:T(8,128)(2,1)} %bitcast.39, f32[1024,1024]{1,0:T(8,128)} %broadcast_in_dim.8.acc_ref), custom_call_target="tpu_custom_call", output_to_operand_aliasing={{}: (4, {})} | custom-call | flops 1073741824 | bytes 11534336 | tf_op jit(solution)/shard_map/pallas_call | solution.py:71
  82.1 20.5 %all-gather.7.cloned.1.call-done = bf16[1,1024,2048]{2,1,0:T(8,128)(2,1)} async-done(((bf16[1,128,2048]{2,1,0:T(8,128)(2,1)}), bf16[1,1024,2048]{2,1,0:T(8,128)(2,1)}) %all-gather.7.cloned.1.call-update) | async-done | bytes 4194320 | tf_op jit(solution)/shard_map/all_gather | solution.py:136
  102.7 25.3 %shard_map.83.acc_ref = f32[1024,1024]{1,0:T(8,128)} custom-call(s32[2]{0:T(128)} %get-tuple-element.8.base_ref, bf16[1024,1024]{1,0:T(8,128)(2,1)} %bitcast.7.q_ref, s32[1024,1]{1,0:T(8,128)} %convert_element_type.74.lim_ref, bf16[1024,2048]{1,0:T(8,128)(2,1)} %bitcast.46, f32[1024,1024]{1,0:T(8,128)} %shard_map.82.acc_ref), custom_call_target="tpu_custom_call", output_to_operand_aliasing={{}: (4, {})} | custom-call | flops 4294967296 | bytes 14680064 | tf_op jit(solution)/shard_map/pallas_call | solution.py:71
  128.0 46.4 %all-gather.5.cloned.1.call-done = bf16[1,1024,2048]{2,1,0:T(8,128)(2,1)} async-done(((bf16[1,128,2048]{2,1,0:T(8,128)(2,1)}), bf16[1,1024,2048]{2,1,0:T(8,128)(2,1)}) %all-gather.5.cloned.1.call-update) | async-done | bytes 4194320 | tf_op jit(solution)/shard_map/all_gather | solution.py:136
  174.4 25.3 %shard_map.84 = f32[1024,1024]{1,0:T(8,128)} custom-call(s32[2]{0:T(128)} %get-tuple-element.7.base_ref, bf16[1024,1024]{1,0:T(8,128)(2,1)} %bitcast.7.q_ref, s32[1024,1]{1,0:T(8,128)} %convert_element_type.74.lim_ref, bf16[1024,2048]{1,0:T(8,128)(2,1)} %bitcast.47, f32[1024,1024]{1,0:T(8,128)} %shard_map.83.acc_ref), custom_call_target="tpu_custom_call", output_to_operand_aliasing={{}: (4, {})} | custom-call | flops 4294967296 | bytes 14680064 | tf_op jit(solution)/shard_map/pallas_call | solution.py:71
  199.7 0.0 copy-start.2
  199.7 2.5 reduce_sum.31
  202.2 0.0 copy-start.1
  202.2 2.9 %multiply_reduce_fusion = f32[1024]{0:T(1024)S(1)} fusion(f32[1024,1024]{1,0:T(8,128)} %shard_map.84, f32[1024]{0:T(1024)S(1)} %broadcast_multiply_fusion), kind=kLoop, calls=%fused_computation.4 | loop fusion | flops 3144704 | bytes 4202496 | tf_op jit(solution)/shard_map/reduce_sum | solution.py:145
  205.1 0.0 copy-done.2
  205.1 0.5 copy-done.1
  205.6 1.9 multiply_convert_fusion
  207.5 5.4 %all-to-all-start.2 = ((bf16[16,64,1024]{2,1,0:T(8,128)(2,1)}), bf16[16,64,1024]{2,1,0:T(8,128)(2,1)}, u32[]{:S(2)}, u32[]{:S(2)}) async-start(bf16[16,64,1024]{2,1,0:T(8,128)(2,1)} %bitcast.38), calls=%async_computation.2 | async-start | bytes 4194304 | tf_op jit(solution)/shard_map/all_to_all | solution.py:147
  212.9 27.0 %all-to-all-done.2 = bf16[16,64,1024]{2,1,0:T(8,128)(2,1)} async-done(((bf16[16,64,1024]{2,1,0:T(8,128)(2,1)}), bf16[16,64,1024]{2,1,0:T(8,128)(2,1)}, u32[]{:S(2)}, u32[]{:S(2)}) %all-to-all-start.2) | async-done | bytes 2097184 | tf_op jit(solution)/shard_map/all_to_all | solution.py:147
  239.9 4.6 %gather_fusion = bf16[512,1024]{1,0:T(8,128)(2,1)S(1)} fusion(bf16[1024,1024]{1,0:T(8,128)(2,1)} %bitcast.13, s32[1024]{0:T(1024)S(1)} %pad_clamp_fusion), kind=kCustom, calls=%fused_computation | custom fusion | bytes 2099200 | tf_op jit(solution)/shard_map/gather | solution.py:150
  244.5 0.0 copy-done
  244.5 3.8 %add_convert_fusion = bf16[512,1024]{1,0:T(8,128)(2,1)} fusion(bf16[512,1024]{1,0:T(8,128)(2,1)} %param.8, bf16[1024,1024]{1,0:T(8,128)(2,1)S(1)} %copy-done, bf16[512,1024]{1,0:T(8,128)(2,1)S(1)} %gather_fusion, bf16[512,2048]{1,0:T(8,128)(2,1)} %multiply_convert_fusion.1), kind=kOutput, calls=%fused_computation.6 | convolution fusion | flops 1077411840 | bytes 6291456 | tf_op jit(solution)/shard_map/dot_general | solution.py:152
  (6 shorter events, 0.1 us)
Async XLA Ops:
  6.5 238.0 %copy-start = (bf16[1024,1024]{1,0:T(8,128)(2,1)S(1)}, bf16[1024,1024]{1,0:T(8,128)(2,1)}, u32[]{:S(2)}) copy-start(bf16[1024,1024]{1,0:T(8,128)(2,1)} %param.14) | copy-start | bytes 6291460
  6.5 96.1 %all-gather.7.cloned.1.call-start = ((), (), s32[]{:S(2)}) async-start(), calls=%async_computation.4 | async-start | bytes 4718592 | tf_op jit(solution)/shard_map/all_gather | solution.py:136
  9.0 165.4 %all-gather.5.cloned.1.call-start = ((), (), s32[]{:S(2)}) async-start(), calls=%async_computation.3 | async-start | bytes 4718592 | tf_op jit(solution)/shard_map/all_gather | solution.py:136
  18.5 18.4 %all-to-all-start.1 = ((bf16[16,1,64]{2,1,0:T(2,128)(2,1)}), bf16[16,1,64]{2,1,0:T(2,128)(2,1)S(1)}, u32[]{:S(2)}, u32[]{:S(2)}) async-start(bf16[16,1,64]{2,1,0:T(2,128)(2,1)} %all_to_all.16), calls=%async_computation.1 | async-start | bytes 16384 | tf_op jit(solution)/shard_map/all_to_all | solution.py:119
  36.8 32.8 %all-to-all-start = ((bf16[16,64,1024]{2,1,0:T(8,128)(2,1)}), bf16[16,64,1024]{2,1,0:T(8,128)(2,1)}, u32[]{:S(2)}, u32[]{:S(2)}) async-start(bf16[16,64,1024]{2,1,0:T(8,128)(2,1)} %bitcast.37), calls=%async_computation | async-start | bytes 4194304 | tf_op jit(solution)/shard_map/all_to_all | solution.py:112
  199.7 5.4 %copy-start.2 = (f32[1024]{0:T(1024)S(1)}, f32[1024]{0:T(1024)}, u32[]{:S(2)}) copy-start(f32[1024]{0:T(1024)} %param.15) | copy-start | bytes 12292
  202.2 3.5 %copy-start.1 = (f32[1024,1024]{1,0:T(8,128)S(1)}, f32[1024,1024]{1,0:T(8,128)}, u32[]{:S(2)}) copy-start(f32[1024,1024]{1,0:T(8,128)} %shard_map.84) | copy-start | bytes 12582916
  207.5 32.4 %all-to-all-start.2 = ((bf16[16,64,1024]{2,1,0:T(8,128)(2,1)}), bf16[16,64,1024]{2,1,0:T(8,128)(2,1)}, u32[]{:S(2)}, u32[]{:S(2)}) async-start(bf16[16,64,1024]{2,1,0:T(8,128)(2,1)} %bitcast.38), calls=%async_computation.2 | async-start | bytes 4194304 | tf_op jit(solution)/shard_map/all_to_all | solution.py:147
Sparse Core Ops, SparseCore 0:
  9.7 92.8 all-gather.6
  105.0 69.3 all-gather.4

commit v2 on v1

--- a/solution.py
+++ b/solution.py
@@ -10,13 +10,12 @@
 
 HEADS = 8
 BLK = 128
-GATHER_CHUNKS = 2
-SUB_ROWS = 256
+SUB_ROWS = 1024
 
 norm_eps = 1e-06
 
 
-def attend_kernel(seg_rows, chunk_rows, skip_own, base_ref, q_ref, lim_ref, kv_ref, acc_ref, o_ref):
+def attend_kernel(seg_rows, skip_own, base_ref, q_ref, lim_ref, kv_ref, acc_ref, o_ref):
     k = pl.program_id(0)
     me = base_ref[0]
     width = q_ref.shape[1]
@@ -30,7 +29,7 @@
         o_ref[...] = acc_ref[...]
 
     if skip_own:
-        start = k * seg_rows + base_ref[1]
+        start = k * seg_rows
         run = k != me
     else:
         start = me * seg_rows + k * tk
@@ -64,9 +63,9 @@
 def attend(queries, limits, kv, acc, base, seg_rows, skip_own):
     rows, width = queries.shape
     kv_rows = kv.shape[0]
-    tk = seg_rows // GATHER_CHUNKS if skip_own else seg_rows
+    tk = seg_rows
     steps = kv_rows // tk
-    kernel = functools.partial(attend_kernel, seg_rows, tk, skip_own)
+    kernel = functools.partial(attend_kernel, seg_rows, skip_own)
     flops = 4 * rows * kv_rows * width
     return pl.pallas_call(
         kernel,
@@ -129,16 +128,10 @@
     segment = kv_cache[0]
     seg_rows = segment.shape[0]
     me = lax.axis_index("user").astype(jnp.int32)
-    chunk_rows = seg_rows // GATHER_CHUNKS
     acc = jnp.zeros((slots, width), jnp.float32)
-    acc = attend(got_rows, limits, segment, acc, jnp.stack([me, jnp.int32(0)]), seg_rows, False)
-    for c in range(GATHER_CHUNKS):
-        piece = lax.all_gather(
-            segment[c * chunk_rows : (c + 1) * chunk_rows], "user", axis=0, tiled=True
-        )
-        acc = attend(
-            got_rows, limits, piece, acc, jnp.stack([me, jnp.int32(c * chunk_rows)]), seg_rows, True
-        )
+    acc = attend(got_rows, limits, segment, acc, me.reshape(1), seg_rows, False)
+    history = lax.all_gather(segment, "user", axis=0, tiled=True)
+    acc = attend(got_rows, limits, history, acc, me.reshape(1), seg_rows, True)
     partial_value = acc
     mean_row = jnp.mean(partial_value, axis=1, keepdims=True)
     centered = partial_value - mean_row

time: 257 us -> 210 us (0.82)
  Pallas kernels: 60.7 us -> 31.1 us
  waiting for transfers between devices: 119 us -> 105 us
    pallas_call x3 -> x2, Pallas kernels: 60.7 us -> 31.1 us  [attend(): pl.pallas_call(kernel, out_shape=jax.ShapeDtypeStruct((rows, width), jnp....]
    all_gather x2 -> x1, waiting for transfers between devices: 66.9 us -> 51.8 us  [per_device(): history = lax.all_gather(segment, 'user', axis=0, tiled=True)]
  transfers between devices with their start and end apart: 5 -> 4, of which waited for: 4 -> 3; matrix products, arithmetic and copies ran while one was open for 9% -> 11% of each run, Pallas kernels for 14% -> 4%
where the time goes in v2:
time: 210 us; the launch traced here: 208 us
  waiting for transfers between devices  105 us (50%)
  Pallas kernels  31.1 us (15%)
  local copies, waits for them, and re-layouts  18.4 us (9%)
  starting transfers between devices  17.5 us (8%)
  between operations  14.1 us (7%)
  other arithmetic  11.2 us (5%)
  matrix products  10.9 us (5%)
    all_gather x1, waiting for transfers between devices, per_device(): history = lax.all_gather(segment, 'user', axis=0, tiled=True)  51.8 us
    pallas_call x2, Pallas kernels, attend(): pl.pallas_call(kernel, out_shape=jax.ShapeDtypeStruct((rows, width), jnp....  31.1 us
    all_to_all x1, waiting for transfers between devices, per_device(): lax.all_to_all(normed.reshape(columns, capacity, width), 'cand', split_ax...  27.1 us
    all_to_all x1, waiting for transfers between devices, per_device(): lax.all_to_all(send_rows.reshape(columns, capacity, width), 'cand', split...  25.1 us
    dot_general x1, matrix products, per_device(): jnp.dot(cand_x, w_in, preferred_element_type=jnp.float32)  7.15 us
    all_to_all x1, starting transfers between devices, per_device(): lax.all_to_all(send_vis.reshape(columns, capacity), 'cand', split_axis=0,...  6.83 us
    all_to_all x1, starting transfers between devices, per_device(): lax.all_to_all(send_rows.reshape(columns, capacity, width), 'cand', split...  5.73 us
    all_to_all x1, starting transfers between devices, per_device(): lax.all_to_all(normed.reshape(columns, capacity, width), 'cand', split_ax...  4.98 us
  transfers between devices with their start and end apart: 4, of which 3 were waited for; matrix products, arithmetic and copies ran while one was open for 11% of the time, Pallas kernels for 4%

profile of v2, /device:TPU:1, one launch (start us, length us, event | category | flops | bytes accessed | tf_op | source)
XLA Modules:
  0.0 208.1 jit_solution(8038061420421417922)
XLA Ops:
  6.5 0.0 copy-start
  6.5 0.0 all-gather.3.cloned.1.call-start
  6.5 0.7 all-gather.3.cloned.1.call-update
  7.3 0.7 fusion.7
  7.9 1.1 reduce-window.6
  9.1 0.2 slice_reduce_fusion
  9.3 0.7 convert_element_type.65
  10.0 0.8 fusion.6
  10.8 0.7 compare_select_fusion
  11.5 3.8 %scatter_custom_fusion.1 = bf16[1024]{0:T(1024)(128)(2,1)S(1)} fusion(s32[512]{0:T(512)S(1)} %bitcast.41, bf16[512]{0:T(512)(128)(2,1)S(1)} %convert_element_type.65, bf16[]{:T(256)} %constant.13.clone.1), kind=kCustom, calls=%fused_computation.26 | custom fusion | bytes 2050 | tf_op jit(solution)/shard_map/scatter | solution.py:109
  15.3 0.7 all_to_all.16
  15.9 6.8 %all-to-all-start.1 = ((bf16[16,1,64]{2,1,0:T(2,128)(2,1)}), bf16[16,1,64]{2,1,0:T(2,128)(2,1)S(1)}, u32[]{:S(2)}, u32[]{:S(2)}) async-start(bf16[16,1,64]{2,1,0:T(2,128)(2,1)} %all_to_all.16), calls=%async_computation.1 | async-start | bytes 16384 | tf_op jit(solution)/shard_map/all_to_all | solution.py:118
  22.8 7.2 %multiply_convert_fusion.1 = bf16[512,2048]{1,0:T(8,128)(2,1)} fusion(bf16[512,1024]{1,0:T(8,128)(2,1)} %param.8, bf16[1024,2048]{1,0:T(8,128)(2,1)} %param.13), kind=kOutput, calls=%fused_computation.5 | convolution fusion | flops 2152726528 | bytes 7340032 | tf_op jit(solution)/shard_map/dot_general | solution.py:101
  29.9 4.9 %scatter_custom_fusion = bf16[1024,1024]{1,0:T(8,128)(2,1)} fusion(s32[512]{0:T(512)S(1)} %bitcast.42, bf16[512,2048]{1,0:T(8,128)(2,1)} %multiply_convert_fusion.1, bf16[]{:T(256)} %constant.13.clone.1), kind=kCustom, calls=%fused_computation.9 | custom fusion | bytes 3146240 | tf_op jit(solution)/shard_map/scatter | solution.py:108
  34.8 0.0 all-to-all-done.1
  34.8 5.7 %all-to-all-start = ((bf16[16,64,1024]{2,1,0:T(8,128)(2,1)}), bf16[16,64,1024]{2,1,0:T(8,128)(2,1)}, u32[]{:S(2)}, u32[]{:S(2)}) async-start(bf16[16,64,1024]{2,1,0:T(8,128)(2,1)} %bitcast.36), calls=%async_computation | async-start | bytes 4194304 | tf_op jit(solution)/shard_map/all_to_all | solution.py:111
  41.2 1.3 convert_element_type.74.lim_ref
  42.5 25.1 %all-to-all-done = bf16[16,64,1024]{2,1,0:T(8,128)(2,1)} async-done(((bf16[16,64,1024]{2,1,0:T(8,128)(2,1)}), bf16[16,64,1024]{2,1,0:T(8,128)(2,1)}, u32[]{:S(2)}, u32[]{:S(2)}) %all-to-all-start) | async-done | bytes 2097184 | tf_op jit(solution)/shard_map/all_to_all | solution.py:111
  67.6 2.5 %broadcast_in_dim.8.acc_ref = f32[1024,1024]{1,0:T(8,128)} broadcast(f32[]{:T(128)} %constant.31.clone.1), dimensions={} | broadcast | bytes 4194308 | tf_op jit(solution)/shard_map/broadcast_in_dim | solution.py:131
  70.1 7.8 %shard_map.82.acc_ref = f32[1024,1024]{1,0:T(8,128)} custom-call(s32[1]{0:T(128)} %bitcast.base_ref, bf16[1024,1024]{1,0:T(8,128)(2,1)} %bitcast.7.q_ref, s32[1024,1]{1,0:T(8,128)} %convert_element_type.74.lim_ref, bf16[256,2048]{1,0:T(8,128)(2,1)} %bitcast.38, f32[1024,1024]{1,0:T(8,128)} %broadcast_in_dim.8.acc_ref), custom_call_target="tpu_custom_call", output_to_operand_aliasing={{}: (4, {})} | custom-call | flops 1073741824 | bytes 11534336 | tf_op jit(solution)/shard_map/pallas_call | solution.py:70
  77.9 51.8 %all-gather.3.cloned.1.call-done = bf16[1,2048,2048]{2,1,0:T(8,128)(2,1)} async-done(((bf16[1,256,2048]{2,1,0:T(8,128)(2,1)}), bf16[1,2048,2048]{2,1,0:T(8,128)(2,1)}) %all-gather.3.cloned.1.call-update) | async-done | bytes 8388624 | tf_op jit(solution)/shard_map/all_gather | solution.py:133
  129.7 23.3 %shard_map.83 = f32[1024,1024]{1,0:T(8,128)} custom-call(s32[1]{0:T(128)} %bitcast.base_ref, bf16[1024,1024]{1,0:T(8,128)(2,1)} %bitcast.7.q_ref, s32[1024,1]{1,0:T(8,128)} %convert_element_type.74.lim_ref, bf16[2048,2048]{1,0:T(8,128)(2,1)} %bitcast.45, f32[1024,1024]{1,0:T(8,128)} %shard_map.82.acc_ref), custom_call_target="tpu_custom_call", output_to_operand_aliasing={{}: (4, {})} | custom-call | flops 8589934592 | bytes 18874368 | tf_op jit(solution)/shard_map/pallas_call | solution.py:70
  153.0 2.4 %reduce_sum.31 = f32[1024]{0:T(1024)S(1)} reduce(f32[1024,1024]{1,0:T(8,128)} %shard_map.83, f32[]{:T(128)} %constant.31.clone.1), dimensions={1}, to_apply=%region_5.6 | reduce | flops 1047552 | bytes 4198404 | tf_op jit(solution)/shard_map/reduce_sum | solution.py:136
  155.4 0.0 copy-start.1
  155.4 0.0 copy-start.2
  155.4 2.9 %multiply_reduce_fusion = f32[1024]{0:T(1024)S(1)} fusion(f32[1024,1024]{1,0:T(8,128)} %shard_map.83, f32[1024]{0:T(1024)S(1)} %broadcast_multiply_fusion), kind=kLoop, calls=%fused_computation.4 | loop fusion | flops 3144704 | bytes 4202496 | tf_op jit(solution)/shard_map/reduce_sum | solution.py:138
  158.4 0.5 copy-done.1
  158.9 0.0 copy-done.2
  158.9 1.9 multiply_convert_fusion
  160.8 5.0 %all-to-all-start.2 = ((bf16[16,64,1024]{2,1,0:T(8,128)(2,1)}), bf16[16,64,1024]{2,1,0:T(8,128)(2,1)}, u32[]{:S(2)}, u32[]{:S(2)}) async-start(bf16[16,64,1024]{2,1,0:T(8,128)(2,1)} %bitcast.37), calls=%async_computation.2 | async-start | bytes 4194304 | tf_op jit(solution)/shard_map/all_to_all | solution.py:140
  165.7 27.1 %all-to-all-done.2 = bf16[16,64,1024]{2,1,0:T(8,128)(2,1)} async-done(((bf16[16,64,1024]{2,1,0:T(8,128)(2,1)}), bf16[16,64,1024]{2,1,0:T(8,128)(2,1)}, u32[]{:S(2)}, u32[]{:S(2)}) %all-to-all-start.2) | async-done | bytes 2097184 | tf_op jit(solution)/shard_map/all_to_all | solution.py:140
  192.9 4.6 %gather_fusion = bf16[512,1024]{1,0:T(8,128)(2,1)S(1)} fusion(bf16[1024,1024]{1,0:T(8,128)(2,1)} %bitcast.12, s32[1024]{0:T(1024)S(1)} %pad_clamp_fusion), kind=kCustom, calls=%fused_computation | custom fusion | bytes 2099200 | tf_op jit(solution)/shard_map/gather | solution.py:143
  197.5 0.0 copy-done
  197.5 3.8 %add_convert_fusion = bf16[512,1024]{1,0:T(8,128)(2,1)} fusion(bf16[512,1024]{1,0:T(8,128)(2,1)} %param.8, bf16[1024,1024]{1,0:T(8,128)(2,1)S(1)} %copy-done, bf16[512,1024]{1,0:T(8,128)(2,1)S(1)} %gather_fusion, bf16[512,2048]{1,0:T(8,128)(2,1)} %multiply_convert_fusion.1), kind=kOutput, calls=%fused_computation.6 | convolution fusion | flops 1077411840 | bytes 6291456 | tf_op jit(solution)/shard_map/dot_general | solution.py:145
  (6 shorter events, 0.1 us)
Async XLA Ops:
  6.5 190.9 %copy-start = (bf16[1024,1024]{1,0:T(8,128)(2,1)S(1)}, bf16[1024,1024]{1,0:T(8,128)(2,1)}, u32[]{:S(2)}) copy-start(bf16[1024,1024]{1,0:T(8,128)(2,1)} %param.14) | copy-start | bytes 6291460
  6.5 123.2 %all-gather.3.cloned.1.call-start = ((), (), s32[]{:S(2)}) async-start(), calls=%async_computation.3 | async-start | bytes 9437184 | tf_op jit(solution)/shard_map/all_gather | solution.py:133
  15.9 18.8 %all-to-all-start.1 = ((bf16[16,1,64]{2,1,0:T(2,128)(2,1)}), bf16[16,1,64]{2,1,0:T(2,128)(2,1)S(1)}, u32[]{:S(2)}, u32[]{:S(2)}) async-start(bf16[16,1,64]{2,1,0:T(2,128)(2,1)} %all_to_all.16), calls=%async_computation.1 | async-start | bytes 16384 | tf_op jit(solution)/shard_map/all_to_all | solution.py:118
  34.8 32.8 %all-to-all-start = ((bf16[16,64,1024]{2,1,0:T(8,128)(2,1)}), bf16[16,64,1024]{2,1,0:T(8,128)(2,1)}, u32[]{:S(2)}, u32[]{:S(2)}) async-start(bf16[16,64,1024]{2,1,0:T(8,128)(2,1)} %bitcast.36), calls=%async_computation | async-start | bytes 4194304 | tf_op jit(solution)/shard_map/all_to_all | solution.py:111
  155.4 3.5 %copy-start.1 = (f32[1024,1024]{1,0:T(8,128)S(1)}, f32[1024,1024]{1,0:T(8,128)}, u32[]{:S(2)}) copy-start(f32[1024,1024]{1,0:T(8,128)} %shard_map.83) | copy-start | bytes 12582916
  155.4 3.4 %copy-start.2 = (f32[1024]{0:T(1024)S(1)}, f32[1024]{0:T(1024)}, u32[]{:S(2)}) copy-start(f32[1024]{0:T(1024)} %param.15) | copy-start | bytes 12292
  160.8 32.1 %all-to-all-start.2 = ((bf16[16,64,1024]{2,1,0:T(8,128)(2,1)}), bf16[16,64,1024]{2,1,0:T(8,128)(2,1)}, u32[]{:S(2)}, u32[]{:S(2)}) async-start(bf16[16,64,1024]{2,1,0:T(8,128)(2,1)} %bitcast.37), calls=%async_computation.2 | async-start | bytes 4194304 | tf_op jit(solution)/shard_map/all_to_all | solution.py:140
Sparse Core Ops, SparseCore 0:
  9.7 119.9 all-gather.2

commit v3 on v2

v3 whole, which is shorter than its diff:
```python
import functools
import math

import jax
import jax.numpy as jnp
from jax import lax
from jax.experimental import pallas as pl
from jax.experimental.pallas import tpu as pltpu
from jax.sharding import PartitionSpec as P

HEADS = 8
BLK = 128
SUB_ROWS = 1024

norm_eps = 1e-06


def attend_kernel(seg_rows, skip_own, final, base_ref, q_ref, lim_ref, kv_ref, acc_ref, *rest):
    if final:
        gain_ref, o_ref, total = rest
    else:
        (o_ref,) = rest
        total = o_ref
    k = pl.program_id(0)
    last = pl.num_programs(0) - 1
    me = base_ref[0]
    rows, width = q_ref.shape
    head_size = width // HEADS
    tk = kv_ref.shape[0]
    half_scale = 0.5 / math.sqrt(head_size)

    @pl.when(k == 0)
    def _():
        total[...] = acc_ref[...]

    if skip_own:
        start = k * seg_rows
        run = k != me
    elif final:
        start = k * seg_rows
        run = k >= 0
    else:
        start = me * seg_rows + k * tk
        run = k >= 0

    @pl.when(run)
    def _():
        pos = start + lax.broadcasted_iota(jnp.int32, (rows, tk), 1)
        vis = pos < lim_ref[...]
        for h in range(HEADS):
            cols = slice(h * head_size, (h + 1) * head_size)
            s = lax.dot_general(
                q_ref[:, cols],
                kv_ref[:, cols],
                (((1,), (1,)), ((), ())),
                preferred_element_type=jnp.float32,
            )
            t = s * half_scale
            w = jnp.where(vis, t + t * jnp.tanh(t), 0.0).astype(jnp.bfloat16)
            vh = kv_ref[:, width + h * head_size : width + (h + 1) * head_size]
            total[:, cols] += jnp.dot(w, vh, preferred_element_type=jnp.float32)

    if final:

        @pl.when(k == last)
        def _():
            value = total[...]
            mean_row = jnp.mean(value, axis=1, keepdims=True)
            centered = value - mean_row
            variance = jnp.mean(centered * centered, axis=1, keepdims=True)
            scale_row = lax.rsqrt(variance + norm_eps)
            o_ref[...] = (centered * scale_row * gain_ref[...]).astype(o_ref.dtype)


def attend(queries, limits, kv, acc, base, seg_rows, skip_own, gain=None):
    rows, width = queries.shape
    kv_rows = kv.shape[0]
    tk = seg_rows
    steps = kv_rows // tk
    final = gain is not None
    kernel = functools.partial(attend_kernel, seg_rows, skip_own, final)
    flops = 4 * rows * kv_rows * width
    in_specs = [
        pl.BlockSpec((rows, width), lambda k, b: (0, 0)),
        pl.BlockSpec((rows, 1), lambda k, b: (0, 0)),
        pl.BlockSpec((tk, 2 * width), lambda k, b: (k, 0)),
        pl.BlockSpec((rows, width), lambda k, b: (0, 0)),
    ]
    operands = [base, queries, limits, kv, acc]
    if final:
        in_specs.append(pl.BlockSpec((1, width), lambda k, b: (0, 0)))
        operands.append(gain.reshape(1, width))
        out_dtype = jnp.bfloat16
        scratch = [pltpu.VMEM((rows, width), jnp.float32)]
        aliases = {}
    else:
        out_dtype = jnp.float32
        scratch = []
        aliases = {4: 0}
    return pl.pallas_call(
        kernel,
        out_shape=jax.ShapeDtypeStruct((rows, width), out_dtype),
        grid_spec=pltpu.PrefetchScalarGridSpec(
            num_scalar_prefetch=1,
            grid=(steps,),
            in_specs=in_specs,
            out_specs=pl.BlockSpec((rows, width), lambda k, b: (0, 0)),
            scratch_shapes=scratch,
        ),
        input_output_aliases=aliases,
        compiler_params=pltpu.CompilerParams(
            dimension_semantics=("arbitrary",), vmem_limit_bytes=60 * 1024 * 1024
        ),
        cost_estimate=pl.CostEstimate(
            flops=flops,
            transcendentals=rows * kv_rows * HEADS,
            bytes_accessed=kv_rows * 2 * width * 2 + rows * width * 10,
        ),
    )(*operands)


def per_device(cand_x, cand_user, visible, hist_len, kv_cache, w_in, w_out, ln_gain):
    rows, width = cand_x.shape
    columns = lax.axis_size("cand")
    capacity = 2 * rows // columns
    slots = columns * capacity
    hidden = jax.nn.silu(jnp.dot(cand_x, w_in, preferred_element_type=jnp.float32))
    queries = hidden[:, :width].astype(jnp.bfloat16)
    gate = hidden[:, width:].astype(jnp.bfloat16)
    owner = cand_user[:, 0]
    onehot = (owner[:, None] == jnp.arange(columns, dtype=jnp.int32)[None, :]).astype(jnp.int32)
    earlier = jnp.cumsum(onehot, axis=0) - onehot
    slot_of = owner * capacity + jnp.sum(earlier * onehot, axis=1)
    send_rows = jnp.zeros((slots, width), jnp.bfloat16).at[slot_of].set(queries)
    send_vis = jnp.zeros((slots,), jnp.bfloat16).at[slot_of].set(visible.astype(jnp.bfloat16))
    send_rows = send_rows.reshape(columns, 2, capacity // 2, width)
    send_vis = send_vis.reshape(columns, 2, capacity // 2)
    half_slots = slots // 2
    user_length = hist_len[0].astype(jnp.float32)
    segment = kv_cache[0]
    seg_rows = segment.shape[0]
    me = lax.axis_index("user").astype(jnp.int32).reshape(1)
    halves = []
    for half in range(2):
        got_rows = lax.all_to_all(
            send_rows[:, half], "cand", split_axis=0, concat_axis=0, tiled=True
        ).reshape(half_slots, width)
        got_vis = lax.all_to_all(
            send_vis[:, half], "cand", split_axis=0, concat_axis=0, tiled=True
        ).reshape(half_slots)
        limits = jnp.minimum(user_length, BLK * got_vis.astype(jnp.float32)).astype(jnp.int32)
        limits = limits.reshape(half_slots, 1)
        acc = jnp.zeros((half_slots, width), jnp.float32)
        halves.append((got_rows, limits, acc))
    history = lax.all_gather(segment, "user", axis=0, tiled=True)
    returned = []
    for got_rows, limits, acc in halves:
        normed = attend(got_rows, limits, history, acc, me, seg_rows, False, ln_gain)
        back = lax.all_to_all(
            normed.reshape(columns, capacity // 2, width),
            "cand",
            split_axis=0,
            concat_axis=0,
            tiled=True,
        )
        returned.append(back)
    returned = jnp.stack(returned, axis=1).reshape(slots, width)
    home_rows = returned[slot_of]
    mixed_rows = (home_rows.astype(jnp.float32) * gate.astype(jnp.float32)).astype(jnp.bfloat16)
    projected = jnp.dot(mixed_rows, w_out, preferred_element_type=jnp.float32)
    return (cand_x.astype(jnp.float32) + projected).astype(jnp.bfloat16)


def solution(mesh):
    in_specs = (
        P(("user", "cand"), None),
        P(("user", "cand"), None),
        P(("user", "cand")),
        P("cand"),
        P("cand", "user", None),
        P(),
        P(),
        P(),
    )
    out_specs = P(("user", "cand"), None)
    return jax.shard_map(
        per_device, mesh=mesh, in_specs=in_specs, out_specs=out_specs, check_vma=False
    )
```

time: 210 us -> 218 us (1.038)
  waiting for transfers between devices: 105 us -> 86 us
  blocking collectives: 0 us -> 18.9 us
  starting transfers between devices: 17.5 us -> 28.1 us
  other arithmetic: 11.2 us -> 5.45 us
  local copies, waits for them, and re-layouts: 18.4 us -> 22.8 us
    all_to_all x3 -> x5, waiting for transfers between devices: 52.2 us -> 18.5 us  [the longest x2 15.8 us: per_device(): lax.all_to_all(normed.reshape(columns, capacity // 2, width), 'cand', spl...]
    all_to_all x0 -> x1, blocking collectives: none -> 18.9 us  [per_device(): lax.all_to_all(send_rows[:, half], 'cand', split_axis=0, concat_axis=0, t...]
    all_gather x1, waiting for transfers between devices: 51.8 us -> 66.8 us  [per_device(): history = lax.all_gather(segment, 'user', axis=0, tiled=True)]
    all_to_all x3 -> x5, starting transfers between devices: 17.5 us -> 28.1 us  [the longest x2 12.6 us: per_device(): lax.all_to_all(send_vis[:, half], 'cand', split_axis=0, concat_axis=0, ti...]
    reduce_sum x2 -> x0, other arithmetic: 5.33 us -> none  [the longest x1 2.89 us: per_device(): variance = jnp.mean(centered * centered, axis=1, keepdims=True)]
    another operation x1 -> x3, local copies, waits for them, and re-layouts: 0.01 us -> 3.08 us
    squeeze x0 -> x1, local copies, waits for them, and re-layouts: none -> 2.76 us  [per_device(): send_rows[:, half]]
    broadcast_in_dim x1 -> x0, local copies, waits for them, and re-layouts: 2.5 us -> none  [per_device(): acc = jnp.zeros((slots, width), jnp.float32)]
  transfers between devices with their start and end apart: 4 -> 6, of which waited for: 3 -> 3; matrix products, arithmetic and copies ran while one was open for 11% -> 12% of each run, Pallas kernels for 4% -> 14%
where the time goes in v3:
time: 218 us; the launch traced here: 217 us
  waiting for transfers between devices  86 us (39%)
  Pallas kernels  30.6 us (14%)
  starting transfers between devices  28.1 us (13%)
  local copies, waits for them, and re-layouts  22.8 us (10%)
  blocking collectives  18.9 us (9%)
  between operations  14.1 us (6%)
  matrix products  10.9 us (5%)
  other arithmetic  5.45 us (2%)
    all_gather x1, waiting for transfers between devices, per_device(): history = lax.all_gather(segment, 'user', axis=0, tiled=True)  66.8 us
    pallas_call x2, Pallas kernels, attend(): pl.pallas_call(kernel, out_shape=jax.ShapeDtypeStruct((rows, width), out_...  30.6 us
    all_to_all x1, blocking collectives, per_device(): lax.all_to_all(send_rows[:, half], 'cand', split_axis=0, concat_axis=0, t...  18.9 us
    all_to_all x2, waiting for transfers between devices, per_device(): lax.all_to_all(normed.reshape(columns, capacity // 2, width), 'cand', spl...  15.8 us
    all_to_all x2, starting transfers between devices, per_device(): lax.all_to_all(send_vis[:, half], 'cand', split_axis=0, concat_axis=0, ti...  12.6 us
    all_to_all x2, starting transfers between devices, per_device(): lax.all_to_all(normed.reshape(columns, capacity // 2, width), 'cand', spl...  10.7 us
    dot_general x1, matrix products, per_device(): jnp.dot(cand_x, w_in, preferred_element_type=jnp.float32)  7.16 us
    all_to_all x1, starting transfers between devices, per_device(): lax.all_to_all(send_rows[:, half], 'cand', split_axis=0, concat_axis=0, t...  4.8 us
  transfers between devices with their start and end apart: 6, of which 3 were waited for; matrix products, arithmetic and copies ran while one was open for 12% of the time, Pallas kernels for 14%

profile of v3, /device:TPU:1, one launch (start us, length us, event | category | flops | bytes accessed | tf_op | source)
XLA Modules:
  0.0 217.0 jit_solution(12131422490617557688)
XLA Ops:
  6.5 0.0 copy-start
  6.5 0.0 all-gather.3.cloned.1.call-start
  6.5 0.7 all-gather.3.cloned.1.call-update
  7.3 0.7 fusion.7
  7.9 1.1 reduce-window.6
  9.1 0.2 slice_reduce_fusion
  9.3 0.7 convert_element_type.86
  10.0 0.8 fusion.6
  10.8 0.7 compare_select_fusion
  11.5 3.8 %scatter_custom_fusion.1 = bf16[1024]{0:T(1024)(128)(2,1)S(1)} fusion(s32[512]{0:T(512)S(1)} %bitcast.55, bf16[512]{0:T(512)(128)(2,1)S(1)} %convert_element_type.86, bf16[]{:T(256)} %constant.6.clone.1), kind=kCustom, calls=%fused_computation.26 | custom fusion | bytes 2050 | tf_op jit(solution)/shard_map/scatter | solution.py:135
  15.3 0.1 reshape.112
  15.3 0.6 fusion.10
  16.0 6.8 %all-to-all-start.1 = ((bf16[16,1,32]{2,1,0:T(2,128)(2,1)}), bf16[16,1,32]{2,1,0:T(2,128)(2,1)S(1)}, u32[]{:S(2)}, u32[]{:S(2)}) async-start(bf16[16,1,32]{2,1,0:T(2,128)(2,1)} %get-tuple-element.7), calls=%async_computation.1 | async-start | bytes 16384 | tf_op jit(solution)/shard_map/all_to_all | solution.py:148
  22.8 7.2 %multiply_convert_fusion = bf16[512,2048]{1,0:T(8,128)(2,1)} fusion(bf16[512,1024]{1,0:T(8,128)(2,1)} %param.8, bf16[1024,2048]{1,0:T(8,128)(2,1)} %param.13), kind=kOutput, calls=%fused_computation.3 | convolution fusion | flops 2152726528 | bytes 7340032 | tf_op jit(solution)/shard_map/dot_general | solution.py:127
  30.0 4.8 %scatter_custom_fusion = bf16[1024,1024]{1,0:T(8,128)(2,1)} fusion(s32[512]{0:T(512)S(1)} %bitcast.56, bf16[512,2048]{1,0:T(8,128)(2,1)} %multiply_convert_fusion, bf16[]{:T(256)} %constant.6.clone.1), kind=kCustom, calls=%fused_computation.10 | custom fusion | bytes 3146240 | tf_op jit(solution)/shard_map/scatter | solution.py:134
  34.7 0.0 all-to-all-done.1
  34.7 5.7 %all-to-all-start.4 = ((bf16[16,1,32]{2,1,0:T(2,128)(2,1)}), bf16[16,1,32]{2,1,0:T(2,128)(2,1)S(1)}, u32[]{:S(2)}, u32[]{:S(2)}) async-start(bf16[16,1,32]{2,1,0:T(2,128)(2,1)} %get-tuple-element.8), calls=%async_computation.4 | async-start | bytes 16384 | tf_op jit(solution)/shard_map/all_to_all | solution.py:148
  40.5 2.8 %slice_bitcast_fusion.1 = (bf16[16,32,1024]{2,1,0:T(8,128)(2,1)S(1)}, bf16[16,32,1024]{2,1,0:T(8,128)(2,1)}) fusion(bf16[16,2,32,1024]{3,2,1,0:T(8,128)(2,1)} %bitcast.47), kind=kLoop, calls=%fused_computation.9 | loop fusion | bytes 4194304 | tf_op jit(solution)/shard_map/squeeze | solution.py:146
  43.2 2.7 %all-to-all-done.4 = bf16[16,1,32]{2,1,0:T(2,128)(2,1)S(1)} async-done(((bf16[16,1,32]{2,1,0:T(2,128)(2,1)}), bf16[16,1,32]{2,1,0:T(2,128)(2,1)S(1)}, u32[]{:S(2)}, u32[]{:S(2)}) %all-to-all-start.4) | async-done | bytes 1056 | tf_op jit(solution)/shard_map/all_to_all | solution.py:148
  46.0 18.9 %all_to_all.32 = bf16[16,32,1024]{2,1,0:T(8,128)(2,1)} all-to-all(bf16[16,32,1024]{2,1,0:T(8,128)(2,1)S(1)} %get-tuple-element.5), channel_id=1, replica_groups=mesh['user'=8,'cand'=16] {'cand'}, dimensions={0} | all-to-all | bytes 2097152 | tf_op jit(solution)/shard_map/all_to_all | solution.py:145
  64.9 4.8 %all-to-all-start.3 = ((bf16[16,32,1024]{2,1,0:T(8,128)(2,1)}), bf16[16,32,1024]{2,1,0:T(8,128)(2,1)S(1)}, u32[]{:S(2)}, u32[]{:S(2)}) async-start(bf16[16,32,1024]{2,1,0:T(8,128)(2,1)} %get-tuple-element.6), calls=%async_computation.3 | async-start | bytes 2097152 | tf_op jit(solution)/shard_map/all_to_all | solution.py:145
  70.4 1.0 convert_element_type.97.lim_ref
  71.3 66.8 %all-gather.3.cloned.1.call-done = bf16[1,2048,2048]{2,1,0:T(8,128)(2,1)} async-done(((bf16[1,256,2048]{2,1,0:T(8,128)(2,1)}), bf16[1,2048,2048]{2,1,0:T(8,128)(2,1)}) %all-gather.3.cloned.1.call-update) | async-done | bytes 8388624 | tf_op jit(solution)/shard_map/all_gather | solution.py:155
  138.1 1.6 broadcast_6_acc_ref.2.acc_ref
  139.7 15.4 %shard_map.82 = bf16[512,1024]{1,0:T(8,128)(2,1)} custom-call(s32[1]{0:T(128)} %bitcast.base_ref, bf16[512,1024]{1,0:T(8,128)(2,1)} %bitcast.50, s32[512,1]{1,0:T(8,128)} %convert_element_type.97.lim_ref, bf16[2048,2048]{1,0:T(8,128)(2,1)} %bitcast.59, f32[512,1024]{1,0:T(8,128)} %broadcast_6_acc_ref.2.acc_ref, f32[1,1024]{1,0:T(1,128)} %bitcast.61), custom_call_target="tpu_custom_call" | custom-call | flops 4294967296 | bytes 13631488 | tf_op jit(solution)/shard_map/pallas_call | solution.py:100
  155.0 0.0 all-to-all-done.3
  155.0 0.0 copy-start.1
  155.1 1.0 copy-done.1
  156.0 5.0 %all-to-all-start.2 = ((bf16[16,32,1024]{2,1,0:T(8,128)(2,1)}), bf16[16,32,1024]{2,1,0:T(8,128)(2,1)S(1)}, u32[]{:S(2)}, u32[]{:S(2)}) async-start(bf16[16,32,1024]{2,1,0:T(8,128)(2,1)} %bitcast.51), calls=%async_computation.2 | async-start | bytes 2097152 | tf_op jit(solution)/shard_map/all_to_all | solution.py:159
  161.0 1.0 convert_element_type.98.lim_ref
  162.0 15.3 %shard_map.83 = bf16[512,1024]{1,0:T(8,128)(2,1)} custom-call(s32[1]{0:T(128)} %bitcast.base_ref, bf16[512,1024]{1,0:T(8,128)(2,1)} %bitcast.49, s32[512,1]{1,0:T(8,128)} %convert_element_type.98.lim_ref, bf16[2048,2048]{1,0:T(8,128)(2,1)} %bitcast.60, f32[512,1024]{1,0:T(8,128)} %broadcast_6_acc_ref.2.acc_ref, f32[1,1024]{1,0:T(1,128)} %bitcast.62), custom_call_target="tpu_custom_call" | custom-call | flops 4294967296 | bytes 13631488 | tf_op jit(solution)/shard_map/pallas_call | solution.py:100
  177.3 0.0 all-to-all-done.2
  177.3 5.7 %all-to-all-start.5 = ((bf16[16,32,1024]{2,1,0:T(8,128)(2,1)}), bf16[16,32,1024]{2,1,0:T(8,128)(2,1)}, u32[]{:S(2)}, u32[]{:S(2)}) async-start(bf16[16,32,1024]{2,1,0:T(8,128)(2,1)} %bitcast.52), calls=%async_computation.5 | async-start | bytes 2097152 | tf_op jit(solution)/shard_map/all_to_all | solution.py:159
  183.0 15.8 %all-to-all-done.5 = bf16[16,32,1024]{2,1,0:T(8,128)(2,1)} async-done(((bf16[16,32,1024]{2,1,0:T(8,128)(2,1)}), bf16[16,32,1024]{2,1,0:T(8,128)(2,1)}, u32[]{:S(2)}, u32[]{:S(2)}) %all-to-all-start.5) | async-done | bytes 1048608 | tf_op jit(solution)/shard_map/all_to_all | solution.py:159
  198.8 1.4 pad_maximum_fusion
  200.3 1.5 copy.25
  201.8 4.6 %gather_fusion = bf16[512,1024]{1,0:T(8,128)(2,1)S(1)} fusion(bf16[1024,1024]{1,0:T(8,128)(2,1)} %bitcast.46, s32[1024]{0:T(1024)S(1)} %pad_clamp_fusion), kind=kCustom, calls=%fused_computation | custom fusion | bytes 2099200 | tf_op jit(solution)/shard_map/gather | solution.py:168
  206.4 0.0 copy-done
  206.4 3.8 %add_convert_fusion = bf16[512,1024]{1,0:T(8,128)(2,1)} fusion(bf16[512,1024]{1,0:T(8,128)(2,1)} %param.8, bf16[1024,1024]{1,0:T(8,128)(2,1)S(1)} %copy-done, bf16[512,1024]{1,0:T(8,128)(2,1)S(1)} %gather_fusion, bf16[512,2048]{1,0:T(8,128)(2,1)} %multiply_convert_fusion), kind=kOutput, calls=%fused_computation.5 | convolution fusion | flops 1077411840 | bytes 6291456 | tf_op jit(solution)/shard_map/dot_general | solution.py:170
  (5 shorter events, 0.1 us)
Async XLA Ops:
  6.5 199.8 %copy-start = (bf16[1024,1024]{1,0:T(8,128)(2,1)S(1)}, bf16[1024,1024]{1,0:T(8,128)(2,1)}, u32[]{:S(2)}) copy-start(bf16[1024,1024]{1,0:T(8,128)(2,1)} %param.14) | copy-start | bytes 6291460
  6.5 131.6 %all-gather.3.cloned.1.call-start = ((), (), s32[]{:S(2)}) async-start(), calls=%async_computation.6 | async-start | bytes 9437184 | tf_op jit(solution)/shard_map/all_gather | solution.py:155
  16.0 18.8 %all-to-all-start.1 = ((bf16[16,1,32]{2,1,0:T(2,128)(2,1)}), bf16[16,1,32]{2,1,0:T(2,128)(2,1)S(1)}, u32[]{:S(2)}, u32[]{:S(2)}) async-start(bf16[16,1,32]{2,1,0:T(2,128)(2,1)} %get-tuple-element.7), calls=%async_computation.1 | async-start | bytes 16384 | tf_op jit(solution)/shard_map/all_to_all | solution.py:148
  34.7 11.2 %all-to-all-start.4 = ((bf16[16,1,32]{2,1,0:T(2,128)(2,1)}), bf16[16,1,32]{2,1,0:T(2,128)(2,1)S(1)}, u32[]{:S(2)}, u32[]{:S(2)}) async-start(bf16[16,1,32]{2,1,0:T(2,128)(2,1)} %get-tuple-element.8), calls=%async_computation.4 | async-start | bytes 16384 | tf_op jit(solution)/shard_map/all_to_all | solution.py:148
  64.9 90.2 %all-to-all-start.3 = ((bf16[16,32,1024]{2,1,0:T(8,128)(2,1)}), bf16[16,32,1024]{2,1,0:T(8,128)(2,1)S(1)}, u32[]{:S(2)}, u32[]{:S(2)}) async-start(bf16[16,32,1024]{2,1,0:T(8,128)(2,1)} %get-tuple-element.6), calls=%async_computation.3 | async-start | bytes 2097152 | tf_op jit(solution)/shard_map/all_to_all | solution.py:145
  155.0 1.0 copy-start.1
  156.0 21.3 %all-to-all-start.2 = ((bf16[16,32,1024]{2,1,0:T(8,128)(2,1)}), bf16[16,32,1024]{2,1,0:T(8,128)(2,1)S(1)}, u32[]{:S(2)}, u32[]{:S(2)}) async-start(bf16[16,32,1024]{2,1,0:T(8,128)(2,1)} %bitcast.51), calls=%async_computation.2 | async-start | bytes 2097152 | tf_op jit(solution)/shard_map/all_to_all | solution.py:159
  177.3 21.5 %all-to-all-start.5 = ((bf16[16,32,1024]{2,1,0:T(8,128)(2,1)}), bf16[16,32,1024]{2,1,0:T(8,128)(2,1)}, u32[]{:S(2)}, u32[]{:S(2)}) async-start(bf16[16,32,1024]{2,1,0:T(8,128)(2,1)} %bitcast.52), calls=%async_computation.5 | async-start | bytes 2097152 | tf_op jit(solution)/shard_map/all_to_all | solution.py:159
Sparse Core Ops, SparseCore 0:
  9.7 128.3 all-gather.2

commit v4 on v2

--- a/solution.py
+++ b/solution.py
@@ -93,6 +93,152 @@
     )(base, queries, limits, kv, acc)
 
 
+def fused_kernel(peers, key_rows, q_ref, lim_ref, gain_ref, hist_hbm, out_hbm,
+                 kv_buf, kv_sem, acc, normed, send_sem, recv_sem, local_sem):
+    me = lax.axis_index("cand")
+    uid = lax.axis_index("user")
+    rows, width = q_ref.shape
+    half_rows = rows // 2
+    blk = half_rows // peers
+    cap = 2 * blk
+    head_size = width // HEADS
+    half_scale = 0.5 / math.sqrt(head_size)
+    segments = hist_hbm.shape[0] // key_rows
+    steps = 2 * segments
+
+    barrier = pltpu.get_barrier_semaphore()
+    for j in range(1, peers):
+        pl.semaphore_signal(
+            barrier, inc=1, device_id=(uid, lax.rem(me + j, peers)), device_id_type=pl.DeviceIdType.MESH
+        )
+    pl.semaphore_wait(barrier, peers - 1)
+
+    def kv_copy(s, slot):
+        k = lax.rem(s, segments)
+        return pltpu.make_async_copy(
+            hist_hbm.at[pl.ds(pl.multiple_of(k * key_rows, key_rows), key_rows)],
+            kv_buf.at[slot],
+            kv_sem.at[slot],
+        )
+
+    def remote(half, j):
+        p = lax.rem(me + j, peers)
+        return pltpu.make_async_remote_copy(
+            src_ref=normed.at[half, pl.ds(pl.multiple_of(p * blk, blk), blk)],
+            dst_ref=out_hbm.at[pl.ds(pl.multiple_of(me * cap + half * blk, blk), blk)],
+            send_sem=send_sem.at[half, j],
+            recv_sem=recv_sem.at[half, j],
+            device_id=(uid, p),
+            device_id_type=pl.DeviceIdType.MESH,
+        )
+
+    def incoming(half, j):
+        src = lax.rem(me + peers - j, peers)
+        return pltpu.make_async_remote_copy(
+            src_ref=normed.at[half, pl.ds(pl.multiple_of(me * blk, blk), blk)],
+            dst_ref=out_hbm.at[pl.ds(pl.multiple_of(src * cap + half * blk, blk), blk)],
+            send_sem=send_sem.at[half, j],
+            recv_sem=recv_sem.at[half, j],
+            device_id=(uid, src),
+            device_id_type=pl.DeviceIdType.MESH,
+        )
+
+    def local(half):
+        return pltpu.make_async_copy(
+            normed.at[half, pl.ds(pl.multiple_of(me * blk, blk), blk)],
+            out_hbm.at[pl.ds(pl.multiple_of(me * cap + half * blk, blk), blk)],
+            local_sem.at[half],
+        )
+
+    kv_copy(0, 0).start()
+
+    def step(s, carry):
+        slot = lax.rem(s, 2)
+        half = s // segments
+        k = lax.rem(s, segments)
+        kv_copy(s, slot).wait()
+
+        @pl.when(s + 1 < steps)
+        def _():
+            kv_copy(s + 1, 1 - slot).start()
+
+        @pl.when(k == 0)
+        def _():
+            acc[...] = jnp.zeros_like(acc)
+
+        q_rows = pl.ds(pl.multiple_of(half * half_rows, half_rows), half_rows)
+        pos = k * key_rows + lax.broadcasted_iota(jnp.int32, (half_rows, key_rows), 1)
+        vis = pos < lim_ref[q_rows, :]
+        block = kv_buf.at[slot]
+        for h in range(HEADS):
+            cols = slice(h * head_size, (h + 1) * head_size)
+            scores = lax.dot_general(
+                q_ref[q_rows, cols],
+                block[:, cols],
+                (((1,), (1,)), ((), ())),
+                preferred_element_type=jnp.float32,
+            )
+            t = scores * half_scale
+            w = jnp.where(vis, t + t * jnp.tanh(t), 0.0).astype(jnp.bfloat16)
+            vh = block[:, width + h * head_size : width + (h + 1) * head_size]
+            acc[:, cols] += jnp.dot(w, vh, preferred_element_type=jnp.float32)
+
+        @pl.when(k == segments - 1)
+        def _():
+            value = acc[...]
+            mean_row = jnp.mean(value, axis=1, keepdims=True)
+            centered = value - mean_row
+            variance = jnp.mean(centered * centered, axis=1, keepdims=True)
+            scale_row = lax.rsqrt(variance + norm_eps)
+            normed[half] = (centered * scale_row * gain_ref[...]).astype(jnp.bfloat16)
+            local(half).start()
+            for j in range(1, peers):
+                remote(half, j).start()
+
+        return carry
+
+    lax.fori_loop(0, steps, step, 0)
+
+    for half in range(2):
+        local(half).wait()
+        for j in range(1, peers):
+            remote(half, j).wait_send()
+            incoming(half, j).wait_recv()
+
+
+def attend_and_return(queries, limits, history, gain, peers, key_rows):
+    rows, width = queries.shape
+    kernel = functools.partial(fused_kernel, peers, key_rows)
+    return pl.pallas_call(
+        kernel,
+        out_shape=jax.ShapeDtypeStruct((rows, width), jnp.bfloat16),
+        in_specs=[
+            pl.BlockSpec(memory_space=pltpu.VMEM),
+            pl.BlockSpec(memory_space=pltpu.VMEM),
+            pl.BlockSpec(memory_space=pltpu.VMEM),
+            pl.BlockSpec(memory_space=pl.ANY),
+        ],
+        out_specs=pl.BlockSpec(memory_space=pl.ANY),
+        scratch_shapes=[
+            pltpu.VMEM((2, key_rows, 2 * width), jnp.bfloat16),
+            pltpu.SemaphoreType.DMA((2,)),
+            pltpu.VMEM((rows // 2, width), jnp.float32),
+            pltpu.VMEM((2, rows // 2, width), jnp.bfloat16),
+            pltpu.SemaphoreType.DMA((2, peers)),
+            pltpu.SemaphoreType.DMA((2, peers)),
+            pltpu.SemaphoreType.DMA((2,)),
+        ],
+        compiler_params=pltpu.CompilerParams(
+            collective_id=0, has_side_effects=True, vmem_limit_bytes=60 * 1024 * 1024
+        ),
+        cost_estimate=pl.CostEstimate(
+            flops=8 * rows * history.shape[0] * width,
+            transcendentals=rows * history.shape[0] * HEADS,
+            bytes_accessed=2 * history.size * 2 + rows * width * 6,
+        ),
+    )(queries, limits, gain.reshape(1, width), history)
+
+
 def per_device(cand_x, cand_user, visible, hist_len, kv_cache, w_in, w_out, ln_gain):
     rows, width = cand_x.shape
     columns = lax.axis_size("cand")
@@ -123,23 +269,12 @@
     got_vis = got_vis.reshape(slots)
     user_length = hist_len[0].astype(jnp.float32)
     limits = jnp.minimum(user_length, BLK * got_vis.astype(jnp.float32)).astype(jnp.int32)
-    limits = limits.reshape(slots, 1)
-
+    halves = lambda x: jnp.swapaxes(x.reshape(columns, 2, capacity // 2, -1), 0, 1).reshape(slots, -1)
     segment = kv_cache[0]
-    seg_rows = segment.shape[0]
-    me = lax.axis_index("user").astype(jnp.int32)
-    acc = jnp.zeros((slots, width), jnp.float32)
-    acc = attend(got_rows, limits, segment, acc, me.reshape(1), seg_rows, False)
     history = lax.all_gather(segment, "user", axis=0, tiled=True)
-    acc = attend(got_rows, limits, history, acc, me.reshape(1), seg_rows, True)
-    partial_value = acc
-    mean_row = jnp.mean(partial_value, axis=1, keepdims=True)
-    centered = partial_value - mean_row
-    variance = jnp.mean(centered * centered, axis=1, keepdims=True)
-    normed = (centered * lax.rsqrt(variance + norm_eps) * ln_gain).astype(jnp.bfloat16)
-    returned = lax.all_to_all(
-        normed.reshape(columns, capacity, width), "cand", split_axis=0, concat_axis=0, tiled=True
-    ).reshape(slots, width)
+    returned = attend_and_return(
+        halves(got_rows), halves(limits.reshape(slots, 1)), history, ln_gain, columns, segment.shape[0]
+    )
     home_rows = returned[slot_of]
     mixed_rows = (home_rows.astype(jnp.float32) * gate.astype(jnp.float32)).astype(jnp.bfloat16)
     projected = jnp.dot(mixed_rows, w_out, preferred_element_type=jnp.float32)

time: 210 us -> 191 us (0.910)
  waiting for transfers between devices: 105 us -> 84.6 us
  Pallas kernels: 31.1 us -> 44 us
  other arithmetic: 11.2 us -> 4.03 us
  starting transfers between devices: 17.5 us -> 12.6 us
    all_to_all x1 -> x0, waiting for transfers between devices: 27.1 us -> none  [per_device(): lax.all_to_all(normed.reshape(columns, capacity, width), 'cand', split_ax...]
    pallas_call x2 -> x1, Pallas kernels: 31.1 us -> 44 us  [attend_and_return(): pl.pallas_call(kernel, out_shape=jax.ShapeDtypeStruct((rows, width), jnp....]
    all_gather x1, waiting for transfers between devices: 51.8 us -> 59 us  [per_device(): history = lax.all_gather(segment, 'user', axis=0, tiled=True)]
    reduce_sum x2 -> x0, other arithmetic: 5.33 us -> none  [the longest x1 2.89 us: per_device(): variance = jnp.mean(centered * centered, axis=1, keepdims=True)]
    all_to_all x1 -> x0, starting transfers between devices: 4.98 us -> none  [per_device(): lax.all_to_all(normed.reshape(columns, capacity, width), 'cand', split_ax...]
    transpose x0 -> x2, local copies, waits for them, and re-layouts: none -> 3.17 us  [per_device(): jnp.swapaxes(x.reshape(columns, 2, capacity // 2, -1), 0, 1)]
    broadcast_in_dim x1 -> x0, local copies, waits for them, and re-layouts: 2.5 us -> none  [per_device(): acc = jnp.zeros((slots, width), jnp.float32)]
  transfers between devices with their start and end apart: 4 -> 3, of which waited for: 3 -> 2; matrix products, arithmetic and copies ran while one was open for 11% -> 13% of each run, Pallas kernels for 4% -> 0%
where the time goes in v4:
time: 191 us; the launch traced here: 189 us
  waiting for transfers between devices  84.6 us (44%)
  Pallas kernels  44 us (23%)
  local copies, waits for them, and re-layouts  18.6 us (10%)
  between operations  14.1 us (7%)
  starting transfers between devices  12.6 us (7%)
  matrix products  11 us (6%)
  other arithmetic  4.03 us (2%)
    all_gather x1, waiting for transfers between devices, per_device(): history = lax.all_gather(segment, 'user', axis=0, tiled=True)  59 us
    pallas_call x1, Pallas kernels, attend_and_return(): pl.pallas_call(kernel, out_shape=jax.ShapeDtypeStruct((rows, width), jnp....  44 us
    all_to_all x1, waiting for transfers between devices, per_device(): lax.all_to_all(send_rows.reshape(columns, capacity, width), 'cand', split...  24.9 us
    dot_general x1, matrix products, per_device(): jnp.dot(cand_x, w_in, preferred_element_type=jnp.float32)  7.18 us
    all_to_all x1, starting transfers between devices, per_device(): lax.all_to_all(send_vis.reshape(columns, capacity), 'cand', split_axis=0,...  6.83 us
    all_to_all x1, starting transfers between devices, per_device(): lax.all_to_all(send_rows.reshape(columns, capacity, width), 'cand', split...  5.73 us
    scatter x1, local copies, waits for them, and re-layouts, per_device(): send_rows = jnp.zeros((slots, width), jnp.bfloat16).at[slot_of].set(queries)  4.77 us
    gather x1, local copies, waits for them, and re-layouts, per_device(): home_rows = returned[slot_of]  4.59 us
  transfers between devices with their start and end apart: 3, of which 2 were waited for; matrix products, arithmetic and copies ran while one was open for 13% of the time, Pallas kernels for 0%

profile of v4, /device:TPU:1, one launch (start us, length us, event | category | flops | bytes accessed | tf_op | source)
XLA Modules:
  0.0 188.9 jit_solution(15776064331373614827)
XLA Ops:
  6.5 0.0 copy-start
  6.5 0.0 all-gather.3.cloned.1.call-start
  6.5 0.7 all-gather.3.cloned.1.call-update
  7.3 0.7 fusion.7
  7.9 1.1 reduce-window.6
  9.1 0.2 slice_reduce_fusion
  9.3 0.7 convert_element_type.62
  10.0 0.8 fusion.6
  10.8 0.7 compare_select_fusion
  11.5 3.8 %scatter_custom_fusion.1 = bf16[1024]{0:T(1024)(128)(2,1)S(1)} fusion(s32[512]{0:T(512)S(1)} %bitcast.46, bf16[512]{0:T(512)(128)(2,1)S(1)} %convert_element_type.62, bf16[]{:T(256)} %constant.6.clone.1), kind=kCustom, calls=%fused_computation.22 | custom fusion | bytes 2050 | tf_op jit(solution)/shard_map/scatter | solution.py:255
  15.3 0.7 all_to_all.12
  15.9 6.8 %all-to-all-start.1 = ((bf16[16,1,64]{2,1,0:T(2,128)(2,1)}), bf16[16,1,64]{2,1,0:T(2,128)(2,1)S(1)}, u32[]{:S(2)}, u32[]{:S(2)}) async-start(bf16[16,1,64]{2,1,0:T(2,128)(2,1)} %all_to_all.12), calls=%async_computation.1 | async-start | bytes 16384 | tf_op jit(solution)/shard_map/all_to_all | solution.py:264
  22.8 7.2 %multiply_convert_fusion = bf16[512,2048]{1,0:T(8,128)(2,1)} fusion(bf16[512,1024]{1,0:T(8,128)(2,1)} %param.8, bf16[1024,2048]{1,0:T(8,128)(2,1)} %param.13), kind=kOutput, calls=%fused_computation.3 | convolution fusion | flops 2152726528 | bytes 7340032 | tf_op jit(solution)/shard_map/dot_general | solution.py:247
  30.0 4.8 %scatter_custom_fusion = bf16[1024,1024]{1,0:T(8,128)(2,1)} fusion(s32[512]{0:T(512)S(1)} %bitcast.47, bf16[512,2048]{1,0:T(8,128)(2,1)} %multiply_convert_fusion, bf16[]{:T(256)} %constant.6.clone.1), kind=kCustom, calls=%fused_computation.7 | custom fusion | bytes 3146240 | tf_op jit(solution)/shard_map/scatter | solution.py:254
  34.7 0.0 all-to-all-done.1
  34.7 5.7 %all-to-all-start = ((bf16[16,64,1024]{2,1,0:T(8,128)(2,1)}), bf16[16,64,1024]{2,1,0:T(8,128)(2,1)}, u32[]{:S(2)}, u32[]{:S(2)}) async-start(bf16[16,64,1024]{2,1,0:T(8,128)(2,1)} %bitcast.41), calls=%async_computation | async-start | bytes 4194304 | tf_op jit(solution)/shard_map/all_to_all | solution.py:257
  41.1 0.1 convert_element_type.65
  41.2 1.3 reshape.91.lim_ref
  42.6 24.9 %all-to-all-done = bf16[16,64,1024]{2,1,0:T(8,128)(2,1)} async-done(((bf16[16,64,1024]{2,1,0:T(8,128)(2,1)}), bf16[16,64,1024]{2,1,0:T(8,128)(2,1)}, u32[]{:S(2)}, u32[]{:S(2)}) %all-to-all-start) | async-done | bytes 2097184 | tf_op jit(solution)/shard_map/all_to_all | solution.py:257
  67.5 3.2 %copy.19 = bf16[2,16,32,1024]{3,2,1,0:T(8,128)(2,1)} copy(bf16[2,16,32,1024]{3,2,0,1:T(8,128)(2,1)} %bitcast.7) | data formatting | bytes 4194304 | tf_op jit(solution)/shard_map/transpose | solution.py:272
  70.7 59.0 %all-gather.3.cloned.1.call-done = bf16[1,2048,2048]{2,1,0:T(8,128)(2,1)} async-done(((bf16[1,256,2048]{2,1,0:T(8,128)(2,1)}), bf16[1,2048,2048]{2,1,0:T(8,128)(2,1)}) %all-gather.3.cloned.1.call-update) | async-done | bytes 8388624 | tf_op jit(solution)/shard_map/all_gather | solution.py:274
  129.6 44.0 %shard_map.82 = bf16[1024,1024]{1,0:T(8,128)(2,1)} custom-call(bf16[1024,1024]{1,0:T(8,128)(2,1)} %bitcast.42, s32[1024,1]{1,0:T(8,128)} %reshape.91.lim_ref, f32[1,1024]{1,0:T(1,128)} %bitcast.51, bf16[2048,2048]{1,0:T(8,128)(2,1)} %bitcast.50), custom_call_target="tpu_custom_call" | custom-call | flops 17179869184 | bytes 23068672 | tf_op jit(solution)/shard_map/pallas_call | solution.py:212
  173.6 4.6 %gather_fusion = bf16[512,1024]{1,0:T(8,128)(2,1)S(1)} fusion(bf16[1024,1024]{1,0:T(8,128)(2,1)} %shard_map.82, s32[1024]{0:T(1024)S(1)} %pad_clamp_fusion), kind=kCustom, calls=%fused_computation | custom fusion | bytes 2099200 | tf_op jit(solution)/shard_map/gather | solution.py:278
  178.2 0.0 copy-done
  178.2 3.8 %add_convert_fusion = bf16[512,1024]{1,0:T(8,128)(2,1)} fusion(bf16[512,1024]{1,0:T(8,128)(2,1)} %param.8, bf16[1024,1024]{1,0:T(8,128)(2,1)S(1)} %copy-done, bf16[512,1024]{1,0:T(8,128)(2,1)S(1)} %gather_fusion, bf16[512,2048]{1,0:T(8,128)(2,1)} %multiply_convert_fusion), kind=kOutput, calls=%fused_computation.4 | convolution fusion | flops 1077411840 | bytes 6291456 | tf_op jit(solution)/shard_map/dot_general | solution.py:280
  (5 shorter events, 0.1 us)
Async XLA Ops:
  6.5 171.7 %copy-start = (bf16[1024,1024]{1,0:T(8,128)(2,1)S(1)}, bf16[1024,1024]{1,0:T(8,128)(2,1)}, u32[]{:S(2)}) copy-start(bf16[1024,1024]{1,0:T(8,128)(2,1)} %param.14) | copy-start | bytes 6291460
  6.5 123.1 %all-gather.3.cloned.1.call-start = ((), (), s32[]{:S(2)}) async-start(), calls=%async_computation.2 | async-start | bytes 9437184 | tf_op jit(solution)/shard_map/all_gather | solution.py:274
  15.9 18.8 %all-to-all-start.1 = ((bf16[16,1,64]{2,1,0:T(2,128)(2,1)}), bf16[16,1,64]{2,1,0:T(2,128)(2,1)S(1)}, u32[]{:S(2)}, u32[]{:S(2)}) async-start(bf16[16,1,64]{2,1,0:T(2,128)(2,1)} %all_to_all.12), calls=%async_computation.1 | async-start | bytes 16384 | tf_op jit(solution)/shard_map/all_to_all | solution.py:264
  34.7 32.8 %all-to-all-start = ((bf16[16,64,1024]{2,1,0:T(8,128)(2,1)}), bf16[16,64,1024]{2,1,0:T(8,128)(2,1)}, u32[]{:S(2)}, u32[]{:S(2)}) async-start(bf16[16,64,1024]{2,1,0:T(8,128)(2,1)} %bitcast.41), calls=%async_computation | async-start | bytes 4194304 | tf_op jit(solution)/shard_map/all_to_all | solution.py:257
Sparse Core Ops, SparseCore 0:
  9.7 119.8 all-gather.2

commit v5 on v4

--- a/solution.py
+++ b/solution.py
@@ -275,7 +275,8 @@
     returned = attend_and_return(
         halves(got_rows), halves(limits.reshape(slots, 1)), history, ln_gain, columns, segment.shape[0]
     )
-    home_rows = returned[slot_of]
+    pick = (slot_of[:, None] == jnp.arange(slots, dtype=jnp.int32)[None, :]).astype(jnp.bfloat16)
+    home_rows = jnp.dot(pick, returned, preferred_element_type=jnp.float32)
     mixed_rows = (home_rows.astype(jnp.float32) * gate.astype(jnp.float32)).astype(jnp.bfloat16)
     projected = jnp.dot(mixed_rows, w_out, preferred_element_type=jnp.float32)
     return (cand_x.astype(jnp.float32) + projected).astype(jnp.bfloat16)

time: 191 us -> 188 us (0.984)
  local copies, waits for them, and re-layouts: 18.6 us -> 14 us
    gather x1 -> x0, local copies, waits for them, and re-layouts: 4.59 us -> none  [per_device(): home_rows = returned[slot_of]]
where the time goes in v5:
time: 188 us; the launch traced here: 186 us
  waiting for transfers between devices  84.6 us (45%)
  Pallas kernels  44 us (23%)
  between operations  14.1 us (8%)
  local copies, waits for them, and re-layouts  14 us (7%)
  starting transfers between devices  12.6 us (7%)
  matrix products  12.4 us (7%)
  other arithmetic  4.02 us (2%)
    all_gather x1, waiting for transfers between devices, per_device(): history = lax.all_gather(segment, 'user', axis=0, tiled=True)  59 us
    pallas_call x1, Pallas kernels, attend_and_return(): pl.pallas_call(kernel, out_shape=jax.ShapeDtypeStruct((rows, width), jnp....  44 us
    all_to_all x1, waiting for transfers between devices, per_device(): lax.all_to_all(send_rows.reshape(columns, capacity, width), 'cand', split...  25 us
    dot_general x1, matrix products, per_device(): jnp.dot(cand_x, w_in, preferred_element_type=jnp.float32)  7.18 us
    all_to_all x1, starting transfers between devices, per_device(): lax.all_to_all(send_vis.reshape(columns, capacity), 'cand', split_axis=0,...  6.83 us
    all_to_all x1, starting transfers between devices, per_device(): lax.all_to_all(send_rows.reshape(columns, capacity, width), 'cand', split...  5.74 us
    dot_general x1, matrix products, per_device(): projected = jnp.dot(mixed_rows, w_out, preferred_element_type=jnp.float32)  5.22 us
    scatter x1, local copies, waits for them, and re-layouts, per_device(): send_rows = jnp.zeros((slots, width), jnp.bfloat16).at[slot_of].set(queries)  4.77 us
  transfers between devices with their start and end apart: 3, of which 2 were waited for; matrix products, arithmetic and copies ran while one was open for 13% of the time, Pallas kernels for 0%

profile of v5, /device:TPU:1, one launch (start us, length us, event | category | flops | bytes accessed | tf_op | source)
XLA Modules:
  0.0 185.7 jit_solution(6940755698024924057)
XLA Ops:
  6.5 0.0 copy-start
  6.5 0.0 all-gather.3.cloned.1.call-start
  6.5 0.7 all-gather.3.cloned.1.call-update
  7.3 0.7 fusion.8
  7.9 1.1 reduce-window.6
  9.1 0.2 slice_reduce_fusion
  9.3 0.7 convert_element_type.60
  10.0 0.8 fusion.7
  10.8 0.7 compare_select_fusion
  11.5 3.8 %scatter_custom_fusion.1 = bf16[1024]{0:T(1024)(128)(2,1)S(1)} fusion(s32[512]{0:T(512)S(1)} %bitcast.50, bf16[512]{0:T(512)(128)(2,1)S(1)} %convert_element_type.60, bf16[]{:T(256)} %constant.4.clone.1), kind=kCustom, calls=%fused_computation.23 | custom fusion | bytes 2050 | tf_op jit(solution)/shard_map/scatter | solution.py:255
  15.3 0.7 all_to_all.12
  15.9 6.8 %all-to-all-start.1 = ((bf16[16,1,64]{2,1,0:T(2,128)(2,1)}), bf16[16,1,64]{2,1,0:T(2,128)(2,1)S(1)}, u32[]{:S(2)}, u32[]{:S(2)}) async-start(bf16[16,1,64]{2,1,0:T(2,128)(2,1)} %all_to_all.12), calls=%async_computation.1 | async-start | bytes 16384 | tf_op jit(solution)/shard_map/all_to_all | solution.py:264
  22.8 7.2 %multiply_convert_fusion = bf16[512,2048]{1,0:T(8,128)(2,1)} fusion(bf16[512,1024]{1,0:T(8,128)(2,1)} %param.8, bf16[1024,2048]{1,0:T(8,128)(2,1)} %param.13), kind=kOutput, calls=%fused_computation.2 | convolution fusion | flops 2152726528 | bytes 7340032 | tf_op jit(solution)/shard_map/dot_general | solution.py:247
  30.0 4.8 %scatter_custom_fusion = bf16[1024,1024]{1,0:T(8,128)(2,1)} fusion(s32[512]{0:T(512)S(1)} %bitcast.51, bf16[512,2048]{1,0:T(8,128)(2,1)} %multiply_convert_fusion, bf16[]{:T(256)} %constant.4.clone.1), kind=kCustom, calls=%fused_computation.7 | custom fusion | bytes 3146240 | tf_op jit(solution)/shard_map/scatter | solution.py:254
  34.7 0.0 all-to-all-done.1
  34.7 5.7 %all-to-all-start = ((bf16[16,64,1024]{2,1,0:T(8,128)(2,1)}), bf16[16,64,1024]{2,1,0:T(8,128)(2,1)}, u32[]{:S(2)}, u32[]{:S(2)}) async-start(bf16[16,64,1024]{2,1,0:T(8,128)(2,1)} %bitcast.43), calls=%async_computation | async-start | bytes 4194304 | tf_op jit(solution)/shard_map/all_to_all | solution.py:257
  41.1 0.1 convert_element_type.63
  41.2 1.3 reshape.84.lim_ref
  42.5 25.0 %all-to-all-done = bf16[16,64,1024]{2,1,0:T(8,128)(2,1)} async-done(((bf16[16,64,1024]{2,1,0:T(8,128)(2,1)}), bf16[16,64,1024]{2,1,0:T(8,128)(2,1)}, u32[]{:S(2)}, u32[]{:S(2)}) %all-to-all-start) | async-done | bytes 2097184 | tf_op jit(solution)/shard_map/all_to_all | solution.py:257
  67.5 3.2 %copy.19 = bf16[2,16,32,1024]{3,2,1,0:T(8,128)(2,1)} copy(bf16[2,16,32,1024]{3,2,0,1:T(8,128)(2,1)} %bitcast.8) | data formatting | bytes 4194304 | tf_op jit(solution)/shard_map/transpose | solution.py:272
  70.7 59.0 %all-gather.3.cloned.1.call-done = bf16[1,2048,2048]{2,1,0:T(8,128)(2,1)} async-done(((bf16[1,256,2048]{2,1,0:T(8,128)(2,1)}), bf16[1,2048,2048]{2,1,0:T(8,128)(2,1)}) %all-gather.3.cloned.1.call-update) | async-done | bytes 8388624 | tf_op jit(solution)/shard_map/all_gather | solution.py:274
  129.6 0.0 copy-start.1
  129.6 44.0 %shard_map.82 = bf16[1024,1024]{1,0:T(8,128)(2,1)} custom-call(bf16[1024,1024]{1,0:T(8,128)(2,1)} %bitcast.44, s32[1024,1]{1,0:T(8,128)} %reshape.84.lim_ref, f32[1,1024]{1,0:T(1,128)} %bitcast.53, bf16[2048,2048]{1,0:T(8,128)(2,1)} %bitcast.52), custom_call_target="tpu_custom_call" | custom-call | flops 17179869184 | bytes 23068672 | tf_op jit(solution)/shard_map/pallas_call | solution.py:212
  173.6 0.0 copy-done
  173.6 0.0 copy-done.1
  173.6 5.2 %add_convert_fusion = bf16[512,1024]{1,0:T(8,128)(2,1)} fusion(bf16[512,1024]{1,0:T(8,128)(2,1)S(1)} %copy-done.1, bf16[1024,1024]{1,0:T(8,128)(2,1)S(1)} %copy-done, bf16[1024,1024]{1,0:T(8,128)(2,1)} %shard_map.82, bf16[512,2048]{1,0:T(8,128)(2,1)} %multiply_convert_fusion, s32[512]{0:T(512)S(1)} %bitcast.49), kind=kOutput, calls=%fused_computation.3 | convolution fusion | flops 2151153664 | bytes 7342080 | tf_op jit(solution)/shard_map/dot_general | solution.py:281
  (4 shorter events, 0.1 us)
Async XLA Ops:
  6.5 167.1 %copy-start = (bf16[1024,1024]{1,0:T(8,128)(2,1)S(1)}, bf16[1024,1024]{1,0:T(8,128)(2,1)}, u32[]{:S(2)}) copy-start(bf16[1024,1024]{1,0:T(8,128)(2,1)} %param.14) | copy-start | bytes 6291460
  6.5 123.1 %all-gather.3.cloned.1.call-start = ((), (), s32[]{:S(2)}) async-start(), calls=%async_computation.2 | async-start | bytes 9437184 | tf_op jit(solution)/shard_map/all_gather | solution.py:274
  15.9 18.8 %all-to-all-start.1 = ((bf16[16,1,64]{2,1,0:T(2,128)(2,1)}), bf16[16,1,64]{2,1,0:T(2,128)(2,1)S(1)}, u32[]{:S(2)}, u32[]{:S(2)}) async-start(bf16[16,1,64]{2,1,0:T(2,128)(2,1)} %all_to_all.12), calls=%async_computation.1 | async-start | bytes 16384 | tf_op jit(solution)/shard_map/all_to_all | solution.py:264
  34.7 32.8 %all-to-all-start = ((bf16[16,64,1024]{2,1,0:T(8,128)(2,1)}), bf16[16,64,1024]{2,1,0:T(8,128)(2,1)}, u32[]{:S(2)}, u32[]{:S(2)}) async-start(bf16[16,64,1024]{2,1,0:T(8,128)(2,1)} %bitcast.43), calls=%async_computation | async-start | bytes 4194304 | tf_op jit(solution)/shard_map/all_to_all | solution.py:257
  129.6 44.0 %copy-start.1 = (bf16[512,1024]{1,0:T(8,128)(2,1)S(1)}, bf16[512,1024]{1,0:T(8,128)(2,1)}, u32[]{:S(2)}) copy-start(bf16[512,1024]{1,0:T(8,128)(2,1)} %param.8) | copy-start | bytes 3145732
Sparse Core Ops, SparseCore 0:
  9.7 119.8 all-gather.2

commit v6 on v5

--- a/solution.py
+++ b/solution.py
@@ -93,8 +93,8 @@
     )(base, queries, limits, kv, acc)
 
 
-def fused_kernel(peers, key_rows, q_ref, lim_ref, gain_ref, hist_hbm, out_hbm,
-                 kv_buf, kv_sem, acc, normed, send_sem, recv_sem, local_sem):
+def fused_kernel(peers, key_rows, q_ref, lim_ref, gain_ref, hist_hbm, start_hbm, out_hbm,
+                 kv_buf, kv_sem, acc, normed, send_sem, recv_sem, local_sem, start_sem):
     me = lax.axis_index("cand")
     uid = lax.axis_index("user")
     rows, width = q_ref.shape
@@ -103,8 +103,9 @@
     cap = 2 * blk
     head_size = width // HEADS
     half_scale = 0.5 / math.sqrt(head_size)
-    segments = hist_hbm.shape[0] // key_rows
+    segments = hist_hbm.shape[0] // key_rows - 1
     steps = 2 * segments
+    own = lax.axis_index("user")
 
     barrier = pltpu.get_barrier_semaphore()
     for j in range(1, peers):
@@ -113,8 +114,13 @@
         )
     pl.semaphore_wait(barrier, peers - 1)
 
+    def start_copy(half):
+        return pltpu.make_async_copy(
+            start_hbm.at[pl.ds(half * half_rows, half_rows)], acc.at[half], start_sem.at[half]
+        )
+
     def kv_copy(s, slot):
-        k = lax.rem(s, segments)
+        k = lax.rem(own + 1 + lax.rem(s, segments), segments + 1)
         return pltpu.make_async_copy(
             hist_hbm.at[pl.ds(pl.multiple_of(k * key_rows, key_rows), key_rows)],
             kv_buf.at[slot],
@@ -151,21 +157,29 @@
         )
 
     kv_copy(0, 0).start()
+    start_copy(0).start()
+    start_copy(1).start()
 
     def step(s, carry):
         slot = lax.rem(s, 2)
         half = s // segments
-        k = lax.rem(s, segments)
+        i = lax.rem(s, segments)
+        k = lax.rem(own + 1 + i, segments + 1)
         kv_copy(s, slot).wait()
 
         @pl.when(s + 1 < steps)
         def _():
             kv_copy(s + 1, 1 - slot).start()
 
-        @pl.when(k == 0)
+        @pl.when(s == 0)
         def _():
-            acc[...] = jnp.zeros_like(acc)
-
+            start_copy(0).wait()
+
+        @pl.when(s == segments)
+        def _():
+            start_copy(1).wait()
+
+        total = acc.at[half]
         q_rows = pl.ds(pl.multiple_of(half * half_rows, half_rows), half_rows)
         pos = k * key_rows + lax.broadcasted_iota(jnp.int32, (half_rows, key_rows), 1)
         vis = pos < lim_ref[q_rows, :]
@@ -181,11 +195,11 @@
             t = scores * half_scale
             w = jnp.where(vis, t + t * jnp.tanh(t), 0.0).astype(jnp.bfloat16)
             vh = block[:, width + h * head_size : width + (h + 1) * head_size]
-            acc[:, cols] += jnp.dot(w, vh, preferred_element_type=jnp.float32)
-
-        @pl.when(k == segments - 1)
+            total[:, cols] += jnp.dot(w, vh, preferred_element_type=jnp.float32)
+
+        @pl.when(i == segments - 1)
         def _():
-            value = acc[...]
+            value = total[...]
             mean_row = jnp.mean(value, axis=1, keepdims=True)
             centered = value - mean_row
             variance = jnp.mean(centered * centered, axis=1, keepdims=True)
@@ -206,7 +220,7 @@
             incoming(half, j).wait_recv()
 
 
-def attend_and_return(queries, limits, history, gain, peers, key_rows):
+def attend_and_return(queries, limits, history, start, gain, peers, key_rows):
     rows, width = queries.shape
     kernel = functools.partial(fused_kernel, peers, key_rows)
     return pl.pallas_call(
@@ -217,16 +231,18 @@
             pl.BlockSpec(memory_space=pltpu.VMEM),
             pl.BlockSpec(memory_space=pltpu.VMEM),
             pl.BlockSpec(memory_space=pl.ANY),
+            pl.BlockSpec(memory_space=pl.ANY),
         ],
         out_specs=pl.BlockSpec(memory_space=pl.ANY),
         scratch_shapes=[
             pltpu.VMEM((2, key_rows, 2 * width), jnp.bfloat16),
             pltpu.SemaphoreType.DMA((2,)),
-            pltpu.VMEM((rows // 2, width), jnp.float32),
+            pltpu.VMEM((2, rows // 2, width), jnp.float32),
             pltpu.VMEM((2, rows // 2, width), jnp.bfloat16),
             pltpu.SemaphoreType.DMA((2, peers)),
             pltpu.SemaphoreType.DMA((2, peers)),
             pltpu.SemaphoreType.DMA((2,)),
+            pltpu.SemaphoreType.DMA((2,)),
         ],
         compiler_params=pltpu.CompilerParams(
             collective_id=0, has_side_effects=True, vmem_limit_bytes=60 * 1024 * 1024
@@ -236,7 +252,7 @@
             transcendentals=rows * history.shape[0] * HEADS,
             bytes_accessed=2 * history.size * 2 + rows * width * 6,
         ),
-    )(queries, limits, gain.reshape(1, width), history)
+    )(queries, limits, gain.reshape(1, width), history, start)
 
 
 def per_device(cand_x, cand_user, visible, hist_len, kv_cache, w_in, w_out, ln_gain):
@@ -271,9 +287,15 @@
     limits = jnp.minimum(user_length, BLK * got_vis.astype(jnp.float32)).astype(jnp.int32)
     halves = lambda x: jnp.swapaxes(x.reshape(columns, 2, capacity // 2, -1), 0, 1).reshape(slots, -1)
     segment = kv_cache[0]
+    me = lax.axis_index("user").astype(jnp.int32).reshape(1)
+    queries_h = halves(got_rows)
+    limits_h = halves(limits.reshape(slots, 1))
+    start = attend(
+        queries_h, limits_h, segment, jnp.zeros((slots, width), jnp.float32), me, segment.shape[0], False
+    )
     history = lax.all_gather(segment, "user", axis=0, tiled=True)
     returned = attend_and_return(
-        halves(got_rows), halves(limits.reshape(slots, 1)), history, ln_gain, columns, segment.shape[0]
+        queries_h, limits_h, history, start, ln_gain, columns, segment.shape[0]
     )
     pick = (slot_of[:, None] == jnp.arange(slots, dtype=jnp.int32)[None, :]).astype(jnp.bfloat16)
     home_rows = jnp.dot(pick, returned, preferred_element_type=jnp.float32)

time: 188 us -> 187 us (level)
  waiting for transfers between devices: 84.6 us -> 74.3 us
  Pallas kernels: 44 us -> 51.2 us
  local copies, waits for them, and re-layouts: 14 us -> 16.6 us
    all_gather x1, waiting for transfers between devices: 59 us -> 48.6 us  [per_device(): history = lax.all_gather(segment, 'user', axis=0, tiled=True)]
    pallas_call x0 -> x1, Pallas kernels: none -> 7.8 us  [attend(): pl.pallas_call(kernel, out_shape=jax.ShapeDtypeStruct((rows, width), jnp....]
    broadcast_in_dim x0 -> x1, local copies, waits for them, and re-layouts: none -> 2.5 us  [per_device(): jnp.zeros((slots, width), jnp.float32)]
  transfers between devices with their start and end apart: 3 -> 3, of which waited for: 2 -> 2; matrix products, arithmetic and copies ran while one was open for 13% -> 15% of each run, Pallas kernels for 0% -> 4%
where the time goes in v6:
time: 187 us; the launch traced here: 185 us
  waiting for transfers between devices  74.3 us (40%)
  Pallas kernels  51.2 us (27%)
  local copies, waits for them, and re-layouts  16.6 us (9%)
  between operations  14.1 us (8%)
  starting transfers between devices  12.6 us (7%)
  matrix products  12.4 us (7%)
  other arithmetic  4.02 us (2%)
    all_gather x1, waiting for transfers between devices, per_device(): history = lax.all_gather(segment, 'user', axis=0, tiled=True)  48.6 us
    pallas_call x1, Pallas kernels, attend_and_return(): pl.pallas_call(kernel, out_shape=jax.ShapeDtypeStruct((rows, width), jnp....  43.4 us
    all_to_all x1, waiting for transfers between devices, per_device(): lax.all_to_all(send_rows.reshape(columns, capacity, width), 'cand', split...  25 us
    pallas_call x1, Pallas kernels, attend(): pl.pallas_call(kernel, out_shape=jax.ShapeDtypeStruct((rows, width), jnp....  7.8 us
    dot_general x1, matrix products, per_device(): jnp.dot(cand_x, w_in, preferred_element_type=jnp.float32)  7.15 us
    all_to_all x1, starting transfers between devices, per_device(): lax.all_to_all(send_vis.reshape(columns, capacity), 'cand', split_axis=0,...  6.83 us
    all_to_all x1, starting transfers between devices, per_device(): lax.all_to_all(send_rows.reshape(columns, capacity, width), 'cand', split...  5.74 us
    dot_general x1, matrix products, per_device(): projected = jnp.dot(mixed_rows, w_out, preferred_element_type=jnp.float32)  5.22 us
  transfers between devices with their start and end apart: 3, of which 2 were waited for; matrix products, arithmetic and copies ran while one was open for 15% of the time, Pallas kernels for 4%

profile of v6, /device:TPU:1, one launch (start us, length us, event | category | flops | bytes accessed | tf_op | source)
XLA Modules:
  0.0 185.1 jit_solution(7373310289083250965)
XLA Ops:
  6.5 0.0 copy-start
  6.5 0.0 all-gather.3.cloned.1.call-start
  6.5 0.7 all-gather.3.cloned.1.call-update
  7.3 0.7 fusion.8
  7.9 1.1 reduce-window.6
  9.1 0.2 slice_reduce_fusion
  9.3 0.7 convert_element_type.60
  10.0 0.8 fusion.7
  10.8 0.7 compare_select_fusion
  11.5 3.8 %scatter_custom_fusion.1 = bf16[1024]{0:T(1024)(128)(2,1)S(1)} fusion(s32[512]{0:T(512)S(1)} %bitcast.54, bf16[512]{0:T(512)(128)(2,1)S(1)} %convert_element_type.60, bf16[]{:T(256)} %constant.6.clone.1), kind=kCustom, calls=%fused_computation.23 | custom fusion | bytes 2050 | tf_op jit(solution)/shard_map/scatter | solution.py:271
  15.3 0.7 all_to_all.12
  15.9 6.8 %all-to-all-start.1 = ((bf16[16,1,64]{2,1,0:T(2,128)(2,1)}), bf16[16,1,64]{2,1,0:T(2,128)(2,1)S(1)}, u32[]{:S(2)}, u32[]{:S(2)}) async-start(bf16[16,1,64]{2,1,0:T(2,128)(2,1)} %all_to_all.12), calls=%async_computation.1 | async-start | bytes 16384 | tf_op jit(solution)/shard_map/all_to_all | solution.py:280
  22.8 7.1 %multiply_convert_fusion = bf16[512,2048]{1,0:T(8,128)(2,1)} fusion(bf16[512,1024]{1,0:T(8,128)(2,1)} %param.8, bf16[1024,2048]{1,0:T(8,128)(2,1)} %param.13), kind=kOutput, calls=%fused_computation.2 | convolution fusion | flops 2152726528 | bytes 7340032 | tf_op jit(solution)/shard_map/dot_general | solution.py:263
  29.9 4.8 %scatter_custom_fusion = bf16[1024,1024]{1,0:T(8,128)(2,1)} fusion(s32[512]{0:T(512)S(1)} %bitcast.55, bf16[512,2048]{1,0:T(8,128)(2,1)} %multiply_convert_fusion, bf16[]{:T(256)} %constant.6.clone.1), kind=kCustom, calls=%fused_computation.7 | custom fusion | bytes 3146240 | tf_op jit(solution)/shard_map/scatter | solution.py:270
  34.7 0.0 all-to-all-done.1
  34.7 5.7 %all-to-all-start = ((bf16[16,64,1024]{2,1,0:T(8,128)(2,1)}), bf16[16,64,1024]{2,1,0:T(8,128)(2,1)}, u32[]{:S(2)}, u32[]{:S(2)}) async-start(bf16[16,64,1024]{2,1,0:T(8,128)(2,1)} %bitcast.45), calls=%async_computation | async-start | bytes 4194304 | tf_op jit(solution)/shard_map/all_to_all | solution.py:273
  41.1 0.1 convert_element_type.63
  41.2 1.3 reshape.88.lim_ref
  42.5 25.0 %all-to-all-done = bf16[16,64,1024]{2,1,0:T(8,128)(2,1)} async-done(((bf16[16,64,1024]{2,1,0:T(8,128)(2,1)}), bf16[16,64,1024]{2,1,0:T(8,128)(2,1)}, u32[]{:S(2)}, u32[]{:S(2)}) %all-to-all-start) | async-done | bytes 2097184 | tf_op jit(solution)/shard_map/all_to_all | solution.py:273
  67.5 3.2 %copy.22 = bf16[2,16,32,1024]{3,2,1,0:T(8,128)(2,1)} copy(bf16[2,16,32,1024]{3,2,0,1:T(8,128)(2,1)} %bitcast.8) | data formatting | bytes 4194304 | tf_op jit(solution)/shard_map/transpose | solution.py:288
  70.7 2.5 %broadcast_in_dim.16.acc_ref = f32[1024,1024]{1,0:T(8,128)} broadcast(f32[]{:T(128)} %constant.26.clone.1), dimensions={} | broadcast | bytes 4194308 | tf_op jit(solution)/shard_map/broadcast_in_dim | solution.py:294
  73.2 7.8 %shard_map.82.start_hbm = f32[1024,1024]{1,0:T(8,128)} custom-call(s32[1]{0:T(128)} %bitcast.14.base_ref, bf16[1024,1024]{1,0:T(8,128)(2,1)} %bitcast.46, s32[1024,1]{1,0:T(8,128)} %reshape.88.lim_ref, bf16[256,2048]{1,0:T(8,128)(2,1)} %bitcast.48, f32[1024,1024]{1,0:T(8,128)} %broadcast_in_dim.16.acc_ref), custom_call_target="tpu_custom_call", output_to_operand_aliasing={{}: (4, {})} | custom-call | flops 1073741824 | bytes 11534336 | tf_op jit(solution)/shard_map/pallas_call | solution.py:70
  81.0 48.6 %all-gather.3.cloned.1.call-done = bf16[1,2048,2048]{2,1,0:T(8,128)(2,1)} async-done(((bf16[1,256,2048]{2,1,0:T(8,128)(2,1)}), bf16[1,2048,2048]{2,1,0:T(8,128)(2,1)}) %all-gather.3.cloned.1.call-update) | async-done | bytes 8388624 | tf_op jit(solution)/shard_map/all_gather | solution.py:296
  129.6 0.0 copy-start.1
  129.6 43.4 %shard_map.83 = bf16[1024,1024]{1,0:T(8,128)(2,1)} custom-call(bf16[1024,1024]{1,0:T(8,128)(2,1)} %bitcast.47, s32[1024,1]{1,0:T(8,128)} %reshape.88.lim_ref, f32[1,1024]{1,0:T(1,128)} %bitcast.57, bf16[2048,2048]{1,0:T(8,128)(2,1)} %bitcast.56, f32[1024,1024]{1,0:T(8,128)} %shard_map.82.start_hbm), custom_call_target="tpu_custom_call" | custom-call | flops 17179869184 | bytes 23068672 | tf_op jit(solution)/shard_map/pallas_call | solution.py:226
  173.0 0.0 copy-done
  173.0 0.0 copy-done.1
  173.0 5.2 %add_convert_fusion = bf16[512,1024]{1,0:T(8,128)(2,1)} fusion(bf16[512,1024]{1,0:T(8,128)(2,1)S(1)} %copy-done.1, bf16[1024,1024]{1,0:T(8,128)(2,1)S(1)} %copy-done, bf16[1024,1024]{1,0:T(8,128)(2,1)} %shard_map.83, bf16[512,2048]{1,0:T(8,128)(2,1)} %multiply_convert_fusion, s32[512]{0:T(512)S(1)} %bitcast.53), kind=kOutput, calls=%fused_computation.3 | convolution fusion | flops 2151153664 | bytes 7342080 | tf_op jit(solution)/shard_map/dot_general | solution.py:303
  (4 shorter events, 0.1 us)
Async XLA Ops:
  6.5 166.5 %copy-start = (bf16[1024,1024]{1,0:T(8,128)(2,1)S(1)}, bf16[1024,1024]{1,0:T(8,128)(2,1)}, u32[]{:S(2)}) copy-start(bf16[1024,1024]{1,0:T(8,128)(2,1)} %param.14) | copy-start | bytes 6291460
  6.5 123.1 %all-gather.3.cloned.1.call-start = ((), (), s32[]{:S(2)}) async-start(), calls=%async_computation.2 | async-start | bytes 9437184 | tf_op jit(solution)/shard_map/all_gather | solution.py:296
  15.9 18.7 %all-to-all-start.1 = ((bf16[16,1,64]{2,1,0:T(2,128)(2,1)}), bf16[16,1,64]{2,1,0:T(2,128)(2,1)S(1)}, u32[]{:S(2)}, u32[]{:S(2)}) async-start(bf16[16,1,64]{2,1,0:T(2,128)(2,1)} %all_to_all.12), calls=%async_computation.1 | async-start | bytes 16384 | tf_op jit(solution)/shard_map/all_to_all | solution.py:280
  34.7 32.8 %all-to-all-start = ((bf16[16,64,1024]{2,1,0:T(8,128)(2,1)}), bf16[16,64,1024]{2,1,0:T(8,128)(2,1)}, u32[]{:S(2)}, u32[]{:S(2)}) async-start(bf16[16,64,1024]{2,1,0:T(8,128)(2,1)} %bitcast.45), calls=%async_computation | async-start | bytes 4194304 | tf_op jit(solution)/shard_map/all_to_all | solution.py:273
  129.6 43.4 %copy-start.1 = (bf16[512,1024]{1,0:T(8,128)(2,1)S(1)}, bf16[512,1024]{1,0:T(8,128)(2,1)}, u32[]{:S(2)}) copy-start(bf16[512,1024]{1,0:T(8,128)(2,1)} %param.8) | copy-start | bytes 3145732
Sparse Core Ops, SparseCore 0:
  9.7 119.8 all-gather.2

commit v7 on v2

--- a/solution.py
+++ b/solution.py
@@ -93,6 +93,154 @@
     )(base, queries, limits, kv, acc)
 
 
+def fused_kernel(peers, key_rows, parts, q_ref, lim_ref, gain_ref, hist_hbm, start_hbm, out_hbm,
+                 kv_buf, kv_sem, acc, normed, send_sem, recv_sem, local_sem, start_sem):
+    me = lax.axis_index("cand")
+    uid = lax.axis_index("user")
+    rows, width = q_ref.shape
+    cap = rows // peers
+    head_size = width // HEADS
+    half_scale = 0.5 / math.sqrt(head_size)
+    segments = hist_hbm.shape[0] // key_rows - 1
+    steps = len(parts) * segments
+
+    barrier = pltpu.get_barrier_semaphore()
+    for j in range(1, peers):
+        pl.semaphore_signal(
+            barrier, inc=1, device_id=(uid, lax.rem(me + j, peers)), device_id_type=pl.DeviceIdType.MESH
+        )
+    pl.semaphore_wait(barrier, peers - 1)
+
+    def part_rows(n):
+        first, count = parts[n]
+        return first * peers, count * peers
+
+    def start_copy(n):
+        r0, nr = part_rows(n)
+        return pltpu.make_async_copy(
+            start_hbm.at[pl.ds(r0, nr)], acc.at[pl.ds(r0, nr)], start_sem.at[n]
+        )
+
+    def kv_copy(s, slot):
+        k = lax.rem(uid + 1 + lax.rem(s, segments), segments + 1)
+        return pltpu.make_async_copy(
+            hist_hbm.at[pl.ds(pl.multiple_of(k * key_rows, key_rows), key_rows)],
+            kv_buf.at[slot],
+            kv_sem.at[slot],
+        )
+
+    def remote(n, j, dest, src):
+        first, count = parts[n]
+        r0 = first * peers
+        return pltpu.make_async_remote_copy(
+            src_ref=normed.at[pl.ds(r0 + dest * count, count)],
+            dst_ref=out_hbm.at[pl.ds(src * cap + first, count)],
+            send_sem=send_sem.at[n, j],
+            recv_sem=recv_sem.at[n, j],
+            device_id=(uid, dest),
+            device_id_type=pl.DeviceIdType.MESH,
+        )
+
+    def local(n):
+        first, count = parts[n]
+        return pltpu.make_async_copy(
+            normed.at[pl.ds(first * peers + me * count, count)],
+            out_hbm.at[pl.ds(me * cap + first, count)],
+            local_sem.at[n],
+        )
+
+    kv_copy(0, 0).start()
+    for n in range(len(parts)):
+        start_copy(n).start()
+
+    for n in range(len(parts)):
+        r0, nr = part_rows(n)
+        start_copy(n).wait()
+        lim = lim_ref[r0 : r0 + nr, :]
+
+        def step(i, carry, n=n, r0=r0, nr=nr, lim=lim):
+            s = n * segments + i
+            slot = lax.rem(s, 2)
+            k = lax.rem(uid + 1 + i, segments + 1)
+            kv_copy(s, slot).wait()
+
+            @pl.when(s + 1 < steps)
+            def _():
+                kv_copy(s + 1, 1 - slot).start()
+
+            pos = k * key_rows + lax.broadcasted_iota(jnp.int32, (nr, key_rows), 1)
+            vis = pos < lim
+            block = kv_buf.at[slot]
+            for h in range(HEADS):
+                cols = slice(h * head_size, (h + 1) * head_size)
+                scores = lax.dot_general(
+                    q_ref[r0 : r0 + nr, cols],
+                    block[:, cols],
+                    (((1,), (1,)), ((), ())),
+                    preferred_element_type=jnp.float32,
+                )
+                t = scores * half_scale
+                w = jnp.where(vis, t + t * jnp.tanh(t), 0.0).astype(jnp.bfloat16)
+                vh = block[:, width + h * head_size : width + (h + 1) * head_size]
+                acc[r0 : r0 + nr, cols] += jnp.dot(w, vh, preferred_element_type=jnp.float32)
+            return carry
+
+        lax.fori_loop(0, segments, step, 0)
+        value = acc[r0 : r0 + nr, :]
+        mean_row = jnp.mean(value, axis=1, keepdims=True)
+        centered = value - mean_row
+        variance = jnp.mean(centered * centered, axis=1, keepdims=True)
+        scale_row = lax.rsqrt(variance + norm_eps)
+        normed[r0 : r0 + nr, :] = (centered * scale_row * gain_ref[...]).astype(jnp.bfloat16)
+        local(n).start()
+        for j in range(1, peers):
+            remote(n, j, lax.rem(me + j, peers), me).start()
+
+    for n in range(len(parts)):
+        local(n).wait()
+        for j in range(1, peers):
+            remote(n, j, lax.rem(me + j, peers), me).wait_send()
+            remote(n, j, me, lax.rem(me + peers - j, peers)).wait_recv()
+
+
+PARTS = ((0, 16), (16, 32), (48, 16))
+
+
+def attend_and_return(queries, limits, history, start, gain, peers, key_rows):
+    rows, width = queries.shape
+    kernel = functools.partial(fused_kernel, peers, key_rows, PARTS)
+    return pl.pallas_call(
+        kernel,
+        out_shape=jax.ShapeDtypeStruct((rows, width), jnp.bfloat16),
+        in_specs=[
+            pl.BlockSpec(memory_space=pltpu.VMEM),
+            pl.BlockSpec(memory_space=pltpu.VMEM),
+            pl.BlockSpec(memory_space=pltpu.VMEM),
+            pl.BlockSpec(memory_space=pl.ANY),
+            pl.BlockSpec(memory_space=pl.ANY),
+        ],
+        out_specs=pl.BlockSpec(memory_space=pl.ANY),
+        scratch_shapes=[
+            pltpu.VMEM((2, key_rows, 2 * width), jnp.bfloat16),
+            pltpu.SemaphoreType.DMA((2,)),
+            pltpu.VMEM((rows, width), jnp.float32),
+            pltpu.VMEM((rows, width), jnp.bfloat16),
+            pltpu.SemaphoreType.DMA((len(PARTS), peers)),
+            pltpu.SemaphoreType.DMA((len(PARTS), peers)),
+            pltpu.SemaphoreType.DMA((len(PARTS),)),
+            pltpu.SemaphoreType.DMA((len(PARTS),)),
+        ],
+        compiler_params=pltpu.CompilerParams(
+            collective_id=0, has_side_effects=True, vmem_limit_bytes=60 * 1024 * 1024
+        ),
+        cost_estimate=pl.CostEstimate(
+            flops=8 * rows * history.shape[0] * width,
+            transcendentals=rows * history.shape[0] * HEADS,
+            bytes_accessed=2 * history.size * 2 + rows * width * 6,
+        ),
+    )(queries, limits, gain.reshape(1, width), history, start)
+
+
 def per_device(cand_x, cand_user, visible, hist_len, kv_cache, w_in, w_out, ln_gain):
     rows, width = cand_x.shape
     columns = lax.axis_size("cand")
@@ -123,24 +271,24 @@
     got_vis = got_vis.reshape(slots)
     user_length = hist_len[0].astype(jnp.float32)
     limits = jnp.minimum(user_length, BLK * got_vis.astype(jnp.float32)).astype(jnp.int32)
-    limits = limits.reshape(slots, 1)
+    def halves(x):
+        x = x.reshape(columns, capacity, -1)
+        pieces = [x[:, first : first + count].reshape(-1, x.shape[-1]) for first, count in PARTS]
+        return jnp.concatenate(pieces, axis=0)
 
     segment = kv_cache[0]
-    seg_rows = segment.shape[0]
-    me = lax.axis_index("user").astype(jnp.int32)
-    acc = jnp.zeros((slots, width), jnp.float32)
-    acc = attend(got_rows, limits, segment, acc, me.reshape(1), seg_rows, False)
+    me = lax.axis_index("user").astype(jnp.int32).reshape(1)
+    queries_h = halves(got_rows)
+    limits_h = halves(limits.reshape(slots, 1))
+    start = attend(
+        queries_h, limits_h, segment, jnp.zeros((slots, width), jnp.float32), me, segment.shape[0], False
+    )
     history = lax.all_gather(segment, "user", axis=0, tiled=True)
-    acc = attend(got_rows, limits, history, acc, me.reshape(1), seg_rows, True)
-    partial_value = acc
-    mean_row = jnp.mean(partial_value, axis=1, keepdims=True)
-    centered = partial_value - mean_row
-    variance = jnp.mean(centered * centered, axis=1, keepdims=True)
-    normed = (centered * lax.rsqrt(variance + norm_eps) * ln_gain).astype(jnp.bfloat16)
-    returned = lax.all_to_all(
-        normed.reshape(columns, capacity, width), "cand", split_axis=0, concat_axis=0, tiled=True
-    ).reshape(slots, width)
-    home_rows = returned[slot_of]
+    returned = attend_and_return(
+        queries_h, limits_h, history, start, ln_gain, columns, segment.shape[0]
+    )
+    pick = (slot_of[:, None] == jnp.arange(slots, dtype=jnp.int32)[None, :]).astype(jnp.bfloat16)
+    home_rows = jnp.dot(pick, returned, preferred_element_type=jnp.float32)
     mixed_rows = (home_rows.astype(jnp.float32) * gate.astype(jnp.float32)).astype(jnp.bfloat16)
     projected = jnp.dot(mixed_rows, w_out, preferred_element_type=jnp.float32)
     return (cand_x.astype(jnp.float32) + projected).astype(jnp.bfloat16)

time: 210 us -> 192 us (0.914)
  waiting for transfers between devices: 105 us -> 73.4 us
  Pallas kernels: 31.1 us -> 55.2 us
  other arithmetic: 11.2 us -> 5.53 us
  starting transfers between devices: 17.5 us -> 12.6 us
  local copies, waits for them, and re-layouts: 18.4 us -> 16 us
    pallas_call x0 -> x1, Pallas kernels: none -> 47.4 us  [attend_and_return(): pl.pallas_call(kernel, out_shape=jax.ShapeDtypeStruct((rows, width), jnp....]
    all_to_all x1 -> x0, waiting for transfers between devices: 27.1 us -> none  [per_device(): lax.all_to_all(normed.reshape(columns, capacity, width), 'cand', split_ax...]
    pallas_call x2 -> x1, Pallas kernels: 31.1 us -> 7.8 us  [attend(): pl.pallas_call(kernel, out_shape=jax.ShapeDtypeStruct((rows, width), jnp....]
    reduce_sum x2 -> x0, other arithmetic: 5.33 us -> none  [the longest x1 2.89 us: per_device(): variance = jnp.mean(centered * centered, axis=1, keepdims=True)]
    all_to_all x1 -> x0, starting transfers between devices: 4.98 us -> none  [per_device(): lax.all_to_all(normed.reshape(columns, capacity, width), 'cand', split_ax...]
    gather x1 -> x0, local copies, waits for them, and re-layouts: 4.59 us -> none  [per_device(): home_rows = returned[slot_of]]
    all_gather x1, waiting for transfers between devices: 51.8 us -> 47.7 us  [per_device(): history = lax.all_gather(segment, 'user', axis=0, tiled=True)]
    slice x1 -> x5, local copies, waits for them, and re-layouts: 0.22 us -> 2.96 us  [the longest x4 2.74 us: halves(): x[:, first:first + count].reshape(-1, x.shape[-1])]
  transfers between devices with their start and end apart: 4 -> 3, of which waited for: 3 -> 2; matrix products, arithmetic and copies ran while one was open for 11% -> 15% of each run, Pallas kernels for 4% -> 4%
where the time goes in v7:
time: 192 us; the launch traced here: 189 us
  waiting for transfers between devices  73.4 us (38%)
  Pallas kernels  55.2 us (29%)
  local copies, waits for them, and re-layouts  16 us (8%)
  between operations  14.1 us (7%)
  starting transfers between devices  12.6 us (7%)
  matrix products  12.4 us (6%)
  other arithmetic  5.53 us (3%)
    all_gather x1, waiting for transfers between devices, per_device(): history = lax.all_gather(segment, 'user', axis=0, tiled=True)  47.7 us
    pallas_call x1, Pallas kernels, attend_and_return(): pl.pallas_call(kernel, out_shape=jax.ShapeDtypeStruct((rows, width), jnp....  47.4 us
    all_to_all x1, waiting for transfers between devices, per_device(): lax.all_to_all(send_rows.reshape(columns, capacity, width), 'cand', split...  25 us
    pallas_call x1, Pallas kernels, attend(): pl.pallas_call(kernel, out_shape=jax.ShapeDtypeStruct((rows, width), jnp....  7.8 us
    dot_general x1, matrix products, per_device(): jnp.dot(cand_x, w_in, preferred_element_type=jnp.float32)  7.15 us
    all_to_all x1, starting transfers between devices, per_device(): lax.all_to_all(send_vis.reshape(columns, capacity), 'cand', split_axis=0,...  6.83 us
    all_to_all x1, starting transfers between devices, per_device(): lax.all_to_all(send_rows.reshape(columns, capacity, width), 'cand', split...  5.74 us
    dot_general x1, matrix products, per_device(): projected = jnp.dot(mixed_rows, w_out, preferred_element_type=jnp.float32)  5.22 us
  transfers between devices with their start and end apart: 3, of which 2 were waited for; matrix products, arithmetic and copies ran while one was open for 15% of the time, Pallas kernels for 4%

profile of v7, /device:TPU:1, one launch (start us, length us, event | category | flops | bytes accessed | tf_op | source)
XLA Modules:
  0.0 189.1 jit_solution(13517307944845648193)
XLA Ops:
  6.5 0.0 copy-start
  6.5 0.0 all-gather.3.cloned.1.call-start
  6.5 0.7 all-gather.3.cloned.1.call-update
  7.3 0.7 fusion.8
  7.9 1.1 reduce-window.6
  9.1 0.2 slice_reduce_fusion
  9.3 0.7 convert_element_type.60
  10.0 0.8 fusion.7
  10.8 0.7 compare_select_fusion
  11.5 3.8 %scatter_custom_fusion.1 = bf16[1024]{0:T(1024)(128)(2,1)S(1)} fusion(s32[512]{0:T(512)S(1)} %bitcast.54, bf16[512]{0:T(512)(128)(2,1)S(1)} %convert_element_type.60, bf16[]{:T(256)} %constant.6.clone.1), kind=kCustom, calls=%fused_computation.25 | custom fusion | bytes 2050 | tf_op jit(solution)/shard_map/scatter | solution.py:257
  15.3 0.7 all_to_all.12
  15.9 6.8 %all-to-all-start.1 = ((bf16[16,1,64]{2,1,0:T(2,128)(2,1)}), bf16[16,1,64]{2,1,0:T(2,128)(2,1)S(1)}, u32[]{:S(2)}, u32[]{:S(2)}) async-start(bf16[16,1,64]{2,1,0:T(2,128)(2,1)} %all_to_all.12), calls=%async_computation.1 | async-start | bytes 16384 | tf_op jit(solution)/shard_map/all_to_all | solution.py:266
  22.8 7.1 %multiply_convert_fusion = bf16[512,2048]{1,0:T(8,128)(2,1)} fusion(bf16[512,1024]{1,0:T(8,128)(2,1)} %param.8, bf16[1024,2048]{1,0:T(8,128)(2,1)} %param.13), kind=kOutput, calls=%fused_computation.2 | convolution fusion | flops 2152726528 | bytes 7340032 | tf_op jit(solution)/shard_map/dot_general | solution.py:249
  29.9 4.8 %scatter_custom_fusion = bf16[1024,1024]{1,0:T(8,128)(2,1)} fusion(s32[512]{0:T(512)S(1)} %bitcast.55, bf16[512,2048]{1,0:T(8,128)(2,1)} %multiply_convert_fusion, bf16[]{:T(256)} %constant.6.clone.1), kind=kCustom, calls=%fused_computation.8 | custom fusion | bytes 3146240 | tf_op jit(solution)/shard_map/scatter | solution.py:256
  34.7 0.0 all-to-all-done.1
  34.7 5.7 %all-to-all-start = ((bf16[16,64,1024]{2,1,0:T(8,128)(2,1)}), bf16[16,64,1024]{2,1,0:T(8,128)(2,1)}, u32[]{:S(2)}, u32[]{:S(2)}) async-start(bf16[16,64,1024]{2,1,0:T(8,128)(2,1)} %bitcast.45), calls=%async_computation | async-start | bytes 4194304 | tf_op jit(solution)/shard_map/all_to_all | solution.py:259
  41.1 0.1 slice.48
  41.2 0.1 fusion.12
  41.2 0.1 reshape.82
  41.3 0.1 reshape.84
  41.4 0.1 reshape.83
  41.5 1.0 copy.25.lim_ref
  42.5 25.0 %all-to-all-done = bf16[16,64,1024]{2,1,0:T(8,128)(2,1)} async-done(((bf16[16,64,1024]{2,1,0:T(8,128)(2,1)}), bf16[16,64,1024]{2,1,0:T(8,128)(2,1)}, u32[]{:S(2)}, u32[]{:S(2)}) %all-to-all-start) | async-done | bytes 2097184 | tf_op jit(solution)/shard_map/all_to_all | solution.py:259
  67.5 1.3 slice.45
  68.8 1.3 fusion.11
  70.1 1.5 pad_maximum_fusion.q_ref
  71.6 2.5 %broadcast_in_dim.16.acc_ref = f32[1024,1024]{1,0:T(8,128)} broadcast(f32[]{:T(128)} %constant.26.clone.1), dimensions={} | broadcast | bytes 4194308 | tf_op jit(solution)/shard_map/broadcast_in_dim | solution.py:284
  74.1 7.8 %shard_map.82.start_hbm = f32[1024,1024]{1,0:T(8,128)} custom-call(s32[1]{0:T(128)} %bitcast.14.base_ref, bf16[1024,1024]{1,0:T(8,128)(2,1)} %pad_maximum_fusion.q_ref, s32[1024,1]{1,0:T(8,128)} %copy.25.lim_ref, bf16[256,2048]{1,0:T(8,128)(2,1)} %bitcast.46, f32[1024,1024]{1,0:T(8,128)} %broadcast_in_dim.16.acc_ref), custom_call_target="tpu_custom_call", output_to_operand_aliasing={{}: (4, {})} | custom-call | flops 1073741824 | bytes 11534336 | tf_op jit(solution)/shard_map/pallas_call | solution.py:70
  81.9 47.7 %all-gather.3.cloned.1.call-done = bf16[1,2048,2048]{2,1,0:T(8,128)(2,1)} async-done(((bf16[1,256,2048]{2,1,0:T(8,128)(2,1)}), bf16[1,2048,2048]{2,1,0:T(8,128)(2,1)}) %all-gather.3.cloned.1.call-update) | async-done | bytes 8388624 | tf_op jit(solution)/shard_map/all_gather | solution.py:286
  129.6 0.0 copy-start.1
  129.6 47.4 %shard_map.83 = bf16[1024,1024]{1,0:T(8,128)(2,1)} custom-call(bf16[1024,1024]{1,0:T(8,128)(2,1)} %pad_maximum_fusion.q_ref, s32[1024,1]{1,0:T(8,128)} %copy.25.lim_ref, f32[1,1024]{1,0:T(1,128)} %bitcast.57, bf16[2048,2048]{1,0:T(8,128)(2,1)} %bitcast.56, f32[1024,1024]{1,0:T(8,128)} %shard_map.82.start_hbm), custom_call_target="tpu_custom_call" | custom-call | flops 17179869184 | bytes 23068672 | tf_op jit(solution)/shard_map/pallas_call | solution.py:212
  177.0 0.0 copy-done
  177.0 0.0 copy-done.1
  177.0 5.2 %add_convert_fusion = bf16[512,1024]{1,0:T(8,128)(2,1)} fusion(bf16[512,1024]{1,0:T(8,128)(2,1)S(1)} %copy-done.1, bf16[1024,1024]{1,0:T(8,128)(2,1)S(1)} %copy-done, bf16[1024,1024]{1,0:T(8,128)(2,1)} %shard_map.83, bf16[512,2048]{1,0:T(8,128)(2,1)} %multiply_convert_fusion, s32[512]{0:T(512)S(1)} %bitcast.53), kind=kOutput, calls=%fused_computation.4 | convolution fusion | flops 2151153664 | bytes 7342080 | tf_op jit(solution)/shard_map/dot_general | solution.py:293
  (4 shorter events, 0.1 us)
Async XLA Ops:
  6.5 170.4 %copy-start = (bf16[1024,1024]{1,0:T(8,128)(2,1)S(1)}, bf16[1024,1024]{1,0:T(8,128)(2,1)}, u32[]{:S(2)}) copy-start(bf16[1024,1024]{1,0:T(8,128)(2,1)} %param.14) | copy-start | bytes 6291460
  6.5 123.1 %all-gather.3.cloned.1.call-start = ((), (), s32[]{:S(2)}) async-start(), calls=%async_computation.2 | async-start | bytes 9437184 | tf_op jit(solution)/shard_map/all_gather | solution.py:286
  15.9 18.7 %all-to-all-start.1 = ((bf16[16,1,64]{2,1,0:T(2,128)(2,1)}), bf16[16,1,64]{2,1,0:T(2,128)(2,1)S(1)}, u32[]{:S(2)}, u32[]{:S(2)}) async-start(bf16[16,1,64]{2,1,0:T(2,128)(2,1)} %all_to_all.12), calls=%async_computation.1 | async-start | bytes 16384 | tf_op jit(solution)/shard_map/all_to_all | solution.py:266
  34.7 32.8 %all-to-all-start = ((bf16[16,64,1024]{2,1,0:T(8,128)(2,1)}), bf16[16,64,1024]{2,1,0:T(8,128)(2,1)}, u32[]{:S(2)}, u32[]{:S(2)}) async-start(bf16[16,64,1024]{2,1,0:T(8,128)(2,1)} %bitcast.45), calls=%async_computation | async-start | bytes 4194304 | tf_op jit(solution)/shard_map/all_to_all | solution.py:259
  129.6 47.4 %copy-start.1 = (bf16[512,1024]{1,0:T(8,128)(2,1)S(1)}, bf16[512,1024]{1,0:T(8,128)(2,1)}, u32[]{:S(2)}) copy-start(bf16[512,1024]{1,0:T(8,128)(2,1)} %param.8) | copy-start | bytes 3145732
Sparse Core Ops, SparseCore 0:
  9.7 119.8 all-gather.2

commit v8 on v6

--- a/solution.py
+++ b/solution.py
@@ -93,6 +93,9 @@
     )(base, queries, limits, kv, acc)
 
 
+ORDER = (None, (0,1,0),(1,0,0),(1,1,0),(3,0,0),(3,1,0),(2,0,0),(2,1,0),(0,1,1),(1,0,1),(1,1,1),(3,0,1),(3,1,1),(2,0,1),(2,1,1),(0,0,1))
+
+
 def fused_kernel(peers, key_rows, q_ref, lim_ref, gain_ref, hist_hbm, start_hbm, out_hbm,
                  kv_buf, kv_sem, acc, normed, send_sem, recv_sem, local_sem, start_sem):
     me = lax.axis_index("cand")
@@ -127,8 +130,19 @@
             kv_sem.at[slot],
         )
 
+    def peer(j, sign):
+        dx, dy, dc = ORDER[j]
+        core = lax.rem(me, 2)
+        y_lo = lax.rem(me // 2, 2)
+        x = me // 4
+        return (
+            lax.rem(x + sign * dx + 4, 4) * 4
+            + lax.rem(y_lo + sign * dy + 2, 2) * 2
+            + lax.rem(core + sign * dc + 2, 2)
+        )
+
     def remote(half, j):
-        p = lax.rem(me + j, peers)
+        p = peer(j, 1)
         return pltpu.make_async_remote_copy(
             src_ref=normed.at[half, pl.ds(pl.multiple_of(p * blk, blk), blk)],
             dst_ref=out_hbm.at[pl.ds(pl.multiple_of(me * cap + half * blk, blk), blk)],
@@ -139,7 +153,7 @@
         )
 
     def incoming(half, j):
-        src = lax.rem(me + peers - j, peers)
+        src = peer(j, -1)
         return pltpu.make_async_remote_copy(
             src_ref=normed.at[half, pl.ds(pl.multiple_of(me * blk, blk), blk)],
             dst_ref=out_hbm.at[pl.ds(pl.multiple_of(src * cap + half * blk, blk), blk)],

time: 187 us -> 185 us (0.989)
  no operation moved by 1% of the time
where the time goes in v8:
time: 185 us
  waiting for transfers between devices  74.3 us (40%)
  Pallas kernels  50.8 us (27%)
  local copies, waits for them, and re-layouts  16.6 us (9%)
  between operations  14.1 us (8%)
  starting transfers between devices  12.6 us (7%)
  matrix products  12.4 us (7%)
  other arithmetic  4.02 us (2%)
    all_gather x1, waiting for transfers between devices, per_device(): history = lax.all_gather(segment, 'user', axis=0, tiled=True)  48.6 us
    pallas_call x1, Pallas kernels, attend_and_return(): pl.pallas_call(kernel, out_shape=jax.ShapeDtypeStruct((rows, width), jnp....  43 us
    all_to_all x1, waiting for transfers between devices, per_device(): lax.all_to_all(send_rows.reshape(columns, capacity, width), 'cand', split...  25 us
    pallas_call x1, Pallas kernels, attend(): pl.pallas_call(kernel, out_shape=jax.ShapeDtypeStruct((rows, width), jnp....  7.8 us
    dot_general x1, matrix products, per_device(): jnp.dot(cand_x, w_in, preferred_element_type=jnp.float32)  7.15 us
    all_to_all x1, starting transfers between devices, per_device(): lax.all_to_all(send_vis.reshape(columns, capacity), 'cand', split_axis=0,...  6.83 us
    all_to_all x1, starting transfers between devices, per_device(): lax.all_to_all(send_rows.reshape(columns, capacity, width), 'cand', split...  5.74 us
    dot_general x1, matrix products, per_device(): projected = jnp.dot(mixed_rows, w_out, preferred_element_type=jnp.float32)  5.22 us
  transfers between devices with their start and end apart: 3, of which 2 were waited for; matrix products, arithmetic and copies ran while one was open for 15% of the time, Pallas kernels for 4%

profile of v8, /device:TPU:1, one launch (start us, length us, event | category | flops | bytes accessed | tf_op | source)
XLA Modules:
  0.0 184.7 jit_solution(1314948925053669982)
XLA Ops:
  6.5 0.0 copy-start
  6.5 0.0 all-gather.3.cloned.1.call-start
  6.5 0.7 all-gather.3.cloned.1.call-update
  7.3 0.7 fusion.8
  7.9 1.1 reduce-window.6
  9.1 0.2 slice_reduce_fusion
  9.3 0.7 convert_element_type.60
  10.0 0.8 fusion.7
  10.8 0.7 compare_select_fusion
  11.5 3.8 %scatter_custom_fusion.1 = bf16[1024]{0:T(1024)(128)(2,1)S(1)} fusion(s32[512]{0:T(512)S(1)} %bitcast.54, bf16[512]{0:T(512)(128)(2,1)S(1)} %convert_element_type.60, bf16[]{:T(256)} %constant.6.clone.1), kind=kCustom, calls=%fused_computation.23 | custom fusion | bytes 2050 | tf_op jit(solution)/shard_map/scatter | solution.py:285
  15.3 0.7 all_to_all.12
  15.9 6.8 %all-to-all-start.1 = ((bf16[16,1,64]{2,1,0:T(2,128)(2,1)}), bf16[16,1,64]{2,1,0:T(2,128)(2,1)S(1)}, u32[]{:S(2)}, u32[]{:S(2)}) async-start(bf16[16,1,64]{2,1,0:T(2,128)(2,1)} %all_to_all.12), calls=%async_computation.1 | async-start | bytes 16384 | tf_op jit(solution)/shard_map/all_to_all | solution.py:294
  22.8 7.1 %multiply_convert_fusion = bf16[512,2048]{1,0:T(8,128)(2,1)} fusion(bf16[512,1024]{1,0:T(8,128)(2,1)} %param.8, bf16[1024,2048]{1,0:T(8,128)(2,1)} %param.13), kind=kOutput, calls=%fused_computation.2 | convolution fusion | flops 2152726528 | bytes 7340032 | tf_op jit(solution)/shard_map/dot_general | solution.py:277
  29.9 4.8 %scatter_custom_fusion = bf16[1024,1024]{1,0:T(8,128)(2,1)} fusion(s32[512]{0:T(512)S(1)} %bitcast.55, bf16[512,2048]{1,0:T(8,128)(2,1)} %multiply_convert_fusion, bf16[]{:T(256)} %constant.6.clone.1), kind=kCustom, calls=%fused_computation.7 | custom fusion | bytes 3146240 | tf_op jit(solution)/shard_map/scatter | solution.py:284
  34.7 0.0 all-to-all-done.1
  34.7 5.7 %all-to-all-start = ((bf16[16,64,1024]{2,1,0:T(8,128)(2,1)}), bf16[16,64,1024]{2,1,0:T(8,128)(2,1)}, u32[]{:S(2)}, u32[]{:S(2)}) async-start(bf16[16,64,1024]{2,1,0:T(8,128)(2,1)} %bitcast.45), calls=%async_computation | async-start | bytes 4194304 | tf_op jit(solution)/shard_map/all_to_all | solution.py:287
  41.1 0.1 convert_element_type.63
  41.2 1.3 reshape.88.lim_ref
  42.5 25.0 %all-to-all-done = bf16[16,64,1024]{2,1,0:T(8,128)(2,1)} async-done(((bf16[16,64,1024]{2,1,0:T(8,128)(2,1)}), bf16[16,64,1024]{2,1,0:T(8,128)(2,1)}, u32[]{:S(2)}, u32[]{:S(2)}) %all-to-all-start) | async-done | bytes 2097184 | tf_op jit(solution)/shard_map/all_to_all | solution.py:287
  67.5 3.2 %copy.22 = bf16[2,16,32,1024]{3,2,1,0:T(8,128)(2,1)} copy(bf16[2,16,32,1024]{3,2,0,1:T(8,128)(2,1)} %bitcast.8) | data formatting | bytes 4194304 | tf_op jit(solution)/shard_map/transpose | solution.py:302
  70.7 2.5 %broadcast_in_dim.16.acc_ref = f32[1024,1024]{1,0:T(8,128)} broadcast(f32[]{:T(128)} %constant.26.clone.1), dimensions={} | broadcast | bytes 4194308 | tf_op jit(solution)/shard_map/broadcast_in_dim | solution.py:308
  73.2 7.8 %shard_map.82.start_hbm = f32[1024,1024]{1,0:T(8,128)} custom-call(s32[1]{0:T(128)} %bitcast.14.base_ref, bf16[1024,1024]{1,0:T(8,128)(2,1)} %bitcast.46, s32[1024,1]{1,0:T(8,128)} %reshape.88.lim_ref, bf16[256,2048]{1,0:T(8,128)(2,1)} %bitcast.48, f32[1024,1024]{1,0:T(8,128)} %broadcast_in_dim.16.acc_ref), custom_call_target="tpu_custom_call", output_to_operand_aliasing={{}: (4, {})} | custom-call | flops 1073741824 | bytes 11534336 | tf_op jit(solution)/shard_map/pallas_call | solution.py:70
  81.0 48.6 %all-gather.3.cloned.1.call-done = bf16[1,2048,2048]{2,1,0:T(8,128)(2,1)} async-done(((bf16[1,256,2048]{2,1,0:T(8,128)(2,1)}), bf16[1,2048,2048]{2,1,0:T(8,128)(2,1)}) %all-gather.3.cloned.1.call-update) | async-done | bytes 8388624 | tf_op jit(solution)/shard_map/all_gather | solution.py:310
  129.6 0.0 copy-start.1
  129.6 43.0 %shard_map.83 = bf16[1024,1024]{1,0:T(8,128)(2,1)} custom-call(bf16[1024,1024]{1,0:T(8,128)(2,1)} %bitcast.47, s32[1024,1]{1,0:T(8,128)} %reshape.88.lim_ref, f32[1,1024]{1,0:T(1,128)} %bitcast.57, bf16[2048,2048]{1,0:T(8,128)(2,1)} %bitcast.56, f32[1024,1024]{1,0:T(8,128)} %shard_map.82.start_hbm), custom_call_target="tpu_custom_call" | custom-call | flops 17179869184 | bytes 23068672 | tf_op jit(solution)/shard_map/pallas_call | solution.py:240
  172.6 0.0 copy-done
  172.6 0.0 copy-done.1
  172.6 5.2 %add_convert_fusion = bf16[512,1024]{1,0:T(8,128)(2,1)} fusion(bf16[512,1024]{1,0:T(8,128)(2,1)S(1)} %copy-done.1, bf16[1024,1024]{1,0:T(8,128)(2,1)S(1)} %copy-done, bf16[1024,1024]{1,0:T(8,128)(2,1)} %shard_map.83, bf16[512,2048]{1,0:T(8,128)(2,1)} %multiply_convert_fusion, s32[512]{0:T(512)S(1)} %bitcast.53), kind=kOutput, calls=%fused_computation.3 | convolution fusion | flops 2151153664 | bytes 7342080 | tf_op jit(solution)/shard_map/dot_general | solution.py:317
  (4 shorter events, 0.1 us)
Async XLA Ops:
  6.5 166.1 %copy-start = (bf16[1024,1024]{1,0:T(8,128)(2,1)S(1)}, bf16[1024,1024]{1,0:T(8,128)(2,1)}, u32[]{:S(2)}) copy-start(bf16[1024,1024]{1,0:T(8,128)(2,1)} %param.14) | copy-start | bytes 6291460
  6.5 123.1 %all-gather.3.cloned.1.call-start = ((), (), s32[]{:S(2)}) async-start(), calls=%async_computation.2 | async-start | bytes 9437184 | tf_op jit(solution)/shard_map/all_gather | solution.py:310
  15.9 18.7 %all-to-all-start.1 = ((bf16[16,1,64]{2,1,0:T(2,128)(2,1)}), bf16[16,1,64]{2,1,0:T(2,128)(2,1)S(1)}, u32[]{:S(2)}, u32[]{:S(2)}) async-start(bf16[16,1,64]{2,1,0:T(2,128)(2,1)} %all_to_all.12), calls=%async_computation.1 | async-start | bytes 16384 | tf_op jit(solution)/shard_map/all_to_all | solution.py:294
  34.7 32.8 %all-to-all-start = ((bf16[16,64,1024]{2,1,0:T(8,128)(2,1)}), bf16[16,64,1024]{2,1,0:T(8,128)(2,1)}, u32[]{:S(2)}, u32[]{:S(2)}) async-start(bf16[16,64,1024]{2,1,0:T(8,128)(2,1)} %bitcast.45), calls=%async_computation | async-start | bytes 4194304 | tf_op jit(solution)/shard_map/all_to_all | solution.py:287
  129.6 43.0 %copy-start.1 = (bf16[512,1024]{1,0:T(8,128)(2,1)S(1)}, bf16[512,1024]{1,0:T(8,128)(2,1)}, u32[]{:S(2)}) copy-start(bf16[512,1024]{1,0:T(8,128)(2,1)} %param.8) | copy-start | bytes 3145732
Sparse Core Ops, SparseCore 0:
  9.7 119.8 all-gather.2

commit v9 on v8

--- a/solution.py
+++ b/solution.py
@@ -115,7 +115,6 @@
         pl.semaphore_signal(
             barrier, inc=1, device_id=(uid, lax.rem(me + j, peers)), device_id_type=pl.DeviceIdType.MESH
         )
-    pl.semaphore_wait(barrier, peers - 1)
 
     def start_copy(half):
         return pltpu.make_async_copy(
@@ -174,58 +173,51 @@
     start_copy(0).start()
     start_copy(1).start()
 
-    def step(s, carry):
-        slot = lax.rem(s, 2)
-        half = s // segments
-        i = lax.rem(s, segments)
-        k = lax.rem(own + 1 + i, segments + 1)
-        kv_copy(s, slot).wait()
-
-        @pl.when(s + 1 < steps)
-        def _():
-            kv_copy(s + 1, 1 - slot).start()
-
-        @pl.when(s == 0)
-        def _():
-            start_copy(0).wait()
-
-        @pl.when(s == segments)
-        def _():
-            start_copy(1).wait()
-
+    for half in range(2):
+        start_copy(half).wait()
         total = acc.at[half]
-        q_rows = pl.ds(pl.multiple_of(half * half_rows, half_rows), half_rows)
-        pos = k * key_rows + lax.broadcasted_iota(jnp.int32, (half_rows, key_rows), 1)
-        vis = pos < lim_ref[q_rows, :]
-        block = kv_buf.at[slot]
-        for h in range(HEADS):
-            cols = slice(h * head_size, (h + 1) * head_size)
-            scores = lax.dot_general(
-                q_ref[q_rows, cols],
-                block[:, cols],
-                (((1,), (1,)), ((), ())),
-                preferred_element_type=jnp.float32,
-            )
-            t = scores * half_scale
-            w = jnp.where(vis, t + t * jnp.tanh(t), 0.0).astype(jnp.bfloat16)
-            vh = block[:, width + h * head_size : width + (h + 1) * head_size]
-            total[:, cols] += jnp.dot(w, vh, preferred_element_type=jnp.float32)
-
-        @pl.when(i == segments - 1)
-        def _():
-            value = total[...]
-            mean_row = jnp.mean(value, axis=1, keepdims=True)
-            centered = value - mean_row
-            variance = jnp.mean(centered * centered, axis=1, keepdims=True)
-            scale_row = lax.rsqrt(variance + norm_eps)
-            normed[half] = (centered * scale_row * gain_ref[...]).astype(jnp.bfloat16)
-            local(half).start()
-            for j in range(1, peers):
-                remote(half, j).start()
-
-        return carry
-
-    lax.fori_loop(0, steps, step, 0)
+
+        def step(i, carry, half=half, total=total):
+            s = half * segments + i
+            slot = lax.rem(s, 2)
+            k = lax.rem(own + 1 + i, segments + 1)
+            kv_copy(s, slot).wait()
+
+            @pl.when(s + 1 < steps)
+            def _():
+                kv_copy(s + 1, 1 - slot).start()
+
+            q_rows = pl.ds(half * half_rows, half_rows)
+            pos = k * key_rows + lax.broadcasted_iota(jnp.int32, (half_rows, key_rows), 1)
+            vis = pos < lim_ref[q_rows, :]
+            block = kv_buf.at[slot]
+            for h in range(HEADS):
+                cols = slice(h * head_size, (h + 1) * head_size)
+                scores = lax.dot_general(
+                    q_ref[q_rows, cols],
+                    block[:, cols],
+                    (((1,), (1,)), ((), ())),
+                    preferred_element_type=jnp.float32,
+                )
+                t = scores * half_scale
+                w = jnp.where(vis, t + t * jnp.tanh(t), 0.0).astype(jnp.bfloat16)
+                vh = block[:, width + h * head_size : width + (h + 1) * head_size]
+                total[:, cols] += jnp.dot(w, vh, preferred_element_type=jnp.float32)
+            return carry
+
+        lax.fori_loop(0, segments, step, 0)
+        value = total[...]
+        mean_row = jnp.mean(value, axis=1, keepdims=True)
+        centered = value - mean_row
+        variance = jnp.mean(centered * centered, axis=1, keepdims=True)
+        scale_row = lax.rsqrt(variance + norm_eps)
+        normed[half] = (centered * scale_row * gain_ref[...]).astype(jnp.bfloat16)
+        if half == 0:
+            pl.semaphore_wait(barrier, peers - 1)
+        local(half).start()
+        for j in range(1, peers):
+            remote(half, j).start()
+
 
     for half in range(2):
         local(half).wait()

time: 185 us -> 183 us (0.989)
  Pallas kernels: 50.8 us -> 48.3 us
    pallas_call x1, Pallas kernels: 43 us -> 40.5 us  [attend_and_return(): pl.pallas_call(kernel, out_shape=jax.ShapeDtypeStruct((rows, width), jnp....]
where the time goes in v9:
time: 183 us; the launch traced here: 182 us
  waiting for transfers between devices  74.3 us (41%)
  Pallas kernels  48.3 us (26%)
  local copies, waits for them, and re-layouts  16.6 us (9%)
  between operations  14.1 us (8%)
  starting transfers between devices  12.6 us (7%)
  matrix products  12.4 us (7%)
  other arithmetic  4.02 us (2%)
    all_gather x1, waiting for transfers between devices, per_device(): history = lax.all_gather(segment, 'user', axis=0, tiled=True)  48.6 us
    pallas_call x1, Pallas kernels, attend_and_return(): pl.pallas_call(kernel, out_shape=jax.ShapeDtypeStruct((rows, width), jnp....  40.5 us
    all_to_all x1, waiting for transfers between devices, per_device(): lax.all_to_all(send_rows.reshape(columns, capacity, width), 'cand', split...  25 us
    pallas_call x1, Pallas kernels, attend(): pl.pallas_call(kernel, out_shape=jax.ShapeDtypeStruct((rows, width), jnp....  7.8 us
    dot_general x1, matrix products, per_device(): jnp.dot(cand_x, w_in, preferred_element_type=jnp.float32)  7.15 us
    all_to_all x1, starting transfers between devices, per_device(): lax.all_to_all(send_vis.reshape(columns, capacity), 'cand', split_axis=0,...  6.83 us
    all_to_all x1, starting transfers between devices, per_device(): lax.all_to_all(send_rows.reshape(columns, capacity, width), 'cand', split...  5.74 us
    dot_general x1, matrix products, per_device(): projected = jnp.dot(mixed_rows, w_out, preferred_element_type=jnp.float32)  5.22 us
  transfers between devices with their start and end apart: 3, of which 2 were waited for; matrix products, arithmetic and copies ran while one was open for 15% of the time, Pallas kernels for 4%

profile of v9, /device:TPU:1, one launch (start us, length us, event | category | flops | bytes accessed | tf_op | source)
XLA Modules:
  0.0 182.3 jit_solution(14612007513064992123)
XLA Ops:
  6.5 0.0 copy-start
  6.5 0.0 all-gather.3.cloned.1.call-start
  6.5 0.7 all-gather.3.cloned.1.call-update
  7.3 0.7 fusion.8
  7.9 1.1 reduce-window.6
  9.1 0.2 slice_reduce_fusion
  9.3 0.7 convert_element_type.60
  10.0 0.8 fusion.7
  10.8 0.7 compare_select_fusion
  11.5 3.8 %scatter_custom_fusion.1 = bf16[1024]{0:T(1024)(128)(2,1)S(1)} fusion(s32[512]{0:T(512)S(1)} %bitcast.54, bf16[512]{0:T(512)(128)(2,1)S(1)} %convert_element_type.60, bf16[]{:T(256)} %constant.6.clone.1), kind=kCustom, calls=%fused_computation.23 | custom fusion | bytes 2050 | tf_op jit(solution)/shard_map/scatter | solution.py:277
  15.3 0.7 all_to_all.12
  15.9 6.8 %all-to-all-start.1 = ((bf16[16,1,64]{2,1,0:T(2,128)(2,1)}), bf16[16,1,64]{2,1,0:T(2,128)(2,1)S(1)}, u32[]{:S(2)}, u32[]{:S(2)}) async-start(bf16[16,1,64]{2,1,0:T(2,128)(2,1)} %all_to_all.12), calls=%async_computation.1 | async-start | bytes 16384 | tf_op jit(solution)/shard_map/all_to_all | solution.py:286
  22.8 7.1 %multiply_convert_fusion = bf16[512,2048]{1,0:T(8,128)(2,1)} fusion(bf16[512,1024]{1,0:T(8,128)(2,1)} %param.8, bf16[1024,2048]{1,0:T(8,128)(2,1)} %param.13), kind=kOutput, calls=%fused_computation.2 | convolution fusion | flops 2152726528 | bytes 7340032 | tf_op jit(solution)/shard_map/dot_general | solution.py:269
  29.9 4.8 %scatter_custom_fusion = bf16[1024,1024]{1,0:T(8,128)(2,1)} fusion(s32[512]{0:T(512)S(1)} %bitcast.55, bf16[512,2048]{1,0:T(8,128)(2,1)} %multiply_convert_fusion, bf16[]{:T(256)} %constant.6.clone.1), kind=kCustom, calls=%fused_computation.7 | custom fusion | bytes 3146240 | tf_op jit(solution)/shard_map/scatter | solution.py:276
  34.7 0.0 all-to-all-done.1
  34.7 5.7 %all-to-all-start = ((bf16[16,64,1024]{2,1,0:T(8,128)(2,1)}), bf16[16,64,1024]{2,1,0:T(8,128)(2,1)}, u32[]{:S(2)}, u32[]{:S(2)}) async-start(bf16[16,64,1024]{2,1,0:T(8,128)(2,1)} %bitcast.45), calls=%async_computation | async-start | bytes 4194304 | tf_op jit(solution)/shard_map/all_to_all | solution.py:279
  41.1 0.1 convert_element_type.63
  41.2 1.3 reshape.88.lim_ref
  42.5 25.0 %all-to-all-done = bf16[16,64,1024]{2,1,0:T(8,128)(2,1)} async-done(((bf16[16,64,1024]{2,1,0:T(8,128)(2,1)}), bf16[16,64,1024]{2,1,0:T(8,128)(2,1)}, u32[]{:S(2)}, u32[]{:S(2)}) %all-to-all-start) | async-done | bytes 2097184 | tf_op jit(solution)/shard_map/all_to_all | solution.py:279
  67.5 3.2 %copy.22 = bf16[2,16,32,1024]{3,2,1,0:T(8,128)(2,1)} copy(bf16[2,16,32,1024]{3,2,0,1:T(8,128)(2,1)} %bitcast.8) | data formatting | bytes 4194304 | tf_op jit(solution)/shard_map/transpose | solution.py:294
  70.7 2.5 %broadcast_in_dim.16.acc_ref = f32[1024,1024]{1,0:T(8,128)} broadcast(f32[]{:T(128)} %constant.26.clone.1), dimensions={} | broadcast | bytes 4194308 | tf_op jit(solution)/shard_map/broadcast_in_dim | solution.py:300
  73.2 7.8 %shard_map.82.start_hbm = f32[1024,1024]{1,0:T(8,128)} custom-call(s32[1]{0:T(128)} %bitcast.14.base_ref, bf16[1024,1024]{1,0:T(8,128)(2,1)} %bitcast.46, s32[1024,1]{1,0:T(8,128)} %reshape.88.lim_ref, bf16[256,2048]{1,0:T(8,128)(2,1)} %bitcast.48, f32[1024,1024]{1,0:T(8,128)} %broadcast_in_dim.16.acc_ref), custom_call_target="tpu_custom_call", output_to_operand_aliasing={{}: (4, {})} | custom-call | flops 1073741824 | bytes 11534336 | tf_op jit(solution)/shard_map/pallas_call | solution.py:70
  81.0 48.6 %all-gather.3.cloned.1.call-done = bf16[1,2048,2048]{2,1,0:T(8,128)(2,1)} async-done(((bf16[1,256,2048]{2,1,0:T(8,128)(2,1)}), bf16[1,2048,2048]{2,1,0:T(8,128)(2,1)}) %all-gather.3.cloned.1.call-update) | async-done | bytes 8388624 | tf_op jit(solution)/shard_map/all_gather | solution.py:302
  129.6 0.0 copy-start.1
  129.6 40.5 %shard_map.83 = bf16[1024,1024]{1,0:T(8,128)(2,1)} custom-call(bf16[1024,1024]{1,0:T(8,128)(2,1)} %bitcast.47, s32[1024,1]{1,0:T(8,128)} %reshape.88.lim_ref, f32[1,1024]{1,0:T(1,128)} %bitcast.57, bf16[2048,2048]{1,0:T(8,128)(2,1)} %bitcast.56, f32[1024,1024]{1,0:T(8,128)} %shard_map.82.start_hbm), custom_call_target="tpu_custom_call" | custom-call | flops 17179869184 | bytes 23068672 | tf_op jit(solution)/shard_map/pallas_call | solution.py:232
  170.2 0.0 copy-done
  170.2 0.0 copy-done.1
  170.2 5.2 %add_convert_fusion = bf16[512,1024]{1,0:T(8,128)(2,1)} fusion(bf16[512,1024]{1,0:T(8,128)(2,1)S(1)} %copy-done.1, bf16[1024,1024]{1,0:T(8,128)(2,1)S(1)} %copy-done, bf16[1024,1024]{1,0:T(8,128)(2,1)} %shard_map.83, bf16[512,2048]{1,0:T(8,128)(2,1)} %multiply_convert_fusion, s32[512]{0:T(512)S(1)} %bitcast.53), kind=kOutput, calls=%fused_computation.3 | convolution fusion | flops 2151153664 | bytes 7342080 | tf_op jit(solution)/shard_map/dot_general | solution.py:309
  (4 shorter events, 0.1 us)
Async XLA Ops:
  6.5 163.6 %copy-start = (bf16[1024,1024]{1,0:T(8,128)(2,1)S(1)}, bf16[1024,1024]{1,0:T(8,128)(2,1)}, u32[]{:S(2)}) copy-start(bf16[1024,1024]{1,0:T(8,128)(2,1)} %param.14) | copy-start | bytes 6291460
  6.5 123.1 %all-gather.3.cloned.1.call-start = ((), (), s32[]{:S(2)}) async-start(), calls=%async_computation.2 | async-start | bytes 9437184 | tf_op jit(solution)/shard_map/all_gather | solution.py:302
  15.9 18.7 %all-to-all-start.1 = ((bf16[16,1,64]{2,1,0:T(2,128)(2,1)}), bf16[16,1,64]{2,1,0:T(2,128)(2,1)S(1)}, u32[]{:S(2)}, u32[]{:S(2)}) async-start(bf16[16,1,64]{2,1,0:T(2,128)(2,1)} %all_to_all.12), calls=%async_computation.1 | async-start | bytes 16384 | tf_op jit(solution)/shard_map/all_to_all | solution.py:286
  34.7 32.8 %all-to-all-start = ((bf16[16,64,1024]{2,1,0:T(8,128)(2,1)}), bf16[16,64,1024]{2,1,0:T(8,128)(2,1)}, u32[]{:S(2)}, u32[]{:S(2)}) async-start(bf16[16,64,1024]{2,1,0:T(8,128)(2,1)} %bitcast.45), calls=%async_computation | async-start | bytes 4194304 | tf_op jit(solution)/shard_map/all_to_all | solution.py:279
  129.6 40.6 %copy-start.1 = (bf16[512,1024]{1,0:T(8,128)(2,1)S(1)}, bf16[512,1024]{1,0:T(8,128)(2,1)}, u32[]{:S(2)}) copy-start(bf16[512,1024]{1,0:T(8,128)(2,1)} %param.8) | copy-start | bytes 3145732
Sparse Core Ops, SparseCore 0:
  9.7 119.8 all-gather.2

commit v10 on v9

--- a/solution.py
+++ b/solution.py
@@ -96,8 +96,9 @@
 ORDER = (None, (0,1,0),(1,0,0),(1,1,0),(3,0,0),(3,1,0),(2,0,0),(2,1,0),(0,1,1),(1,0,1),(1,1,1),(3,0,1),(3,1,1),(2,0,1),(2,1,1),(0,0,1))
 
 
-def fused_kernel(peers, key_rows, q_ref, lim_ref, gain_ref, hist_hbm, start_hbm, out_hbm,
-                 kv_buf, kv_sem, acc, normed, send_sem, recv_sem, local_sem, start_sem):
+def fused_kernel(peers, key_rows, q_ref, lim_ref, gain_ref, cola_ref, colb_ref, hist_hbm, start_hbm,
+                 x_hbm, gate_hbm, wout_hbm, out_ref, kv_buf, kv_sem, acc, normed, ret, part, xv, gv, wv,
+                 send_sem, recv_sem, local_sem, start_sem, misc_sem):
     me = lax.axis_index("cand")
     uid = lax.axis_index("user")
     rows, width = q_ref.shape
@@ -144,7 +145,7 @@
         p = peer(j, 1)
         return pltpu.make_async_remote_copy(
             src_ref=normed.at[half, pl.ds(pl.multiple_of(p * blk, blk), blk)],
-            dst_ref=out_hbm.at[pl.ds(pl.multiple_of(me * cap + half * blk, blk), blk)],
+            dst_ref=ret.at[half, pl.ds(pl.multiple_of(me * blk, blk), blk)],
             send_sem=send_sem.at[half, j],
             recv_sem=recv_sem.at[half, j],
             device_id=(uid, p),
@@ -155,7 +156,7 @@
         src = peer(j, -1)
         return pltpu.make_async_remote_copy(
             src_ref=normed.at[half, pl.ds(pl.multiple_of(me * blk, blk), blk)],
-            dst_ref=out_hbm.at[pl.ds(pl.multiple_of(src * cap + half * blk, blk), blk)],
+            dst_ref=ret.at[half, pl.ds(pl.multiple_of(src * blk, blk), blk)],
             send_sem=send_sem.at[half, j],
             recv_sem=recv_sem.at[half, j],
             device_id=(uid, src),
@@ -165,13 +166,26 @@
     def local(half):
         return pltpu.make_async_copy(
             normed.at[half, pl.ds(pl.multiple_of(me * blk, blk), blk)],
-            out_hbm.at[pl.ds(pl.multiple_of(me * cap + half * blk, blk), blk)],
+            ret.at[half, pl.ds(pl.multiple_of(me * blk, blk), blk)],
             local_sem.at[half],
         )
 
     kv_copy(0, 0).start()
     start_copy(0).start()
     start_copy(1).start()
+    misc = [
+        pltpu.make_async_copy(src, dst, misc_sem.at[n])
+        for n, (src, dst) in enumerate(((x_hbm, xv), (gate_hbm, gv), (wout_hbm, wv)))
+    ]
+    for copy in misc:
+        copy.start()
+
+    def tail(half, col_ref):
+        homes = col_ref.shape[0]
+        pick = lax.broadcasted_iota(jnp.int32, (homes, half_rows), 1) == col_ref[...]
+        home = jnp.dot(pick.astype(jnp.bfloat16), ret[half], preferred_element_type=jnp.float32)
+        mixed = (home * gv[...].astype(jnp.float32)).astype(jnp.bfloat16)
+        return jnp.dot(mixed, wv[...], preferred_element_type=jnp.float32)
 
     for half in range(2):
         start_copy(half).wait()
@@ -219,46 +233,57 @@
             remote(half, j).start()
 
 
+    for copy in misc:
+        copy.wait()
+    local(0).wait()
+    for j in range(1, peers):
+        incoming(0, j).wait_recv()
+    part[...] = tail(0, cola_ref)
+    local(1).wait()
+    for j in range(1, peers):
+        incoming(1, j).wait_recv()
     for half in range(2):
-        local(half).wait()
         for j in range(1, peers):
             remote(half, j).wait_send()
-            incoming(half, j).wait_recv()
-
-
-def attend_and_return(queries, limits, history, start, gain, peers, key_rows):
+    out_ref[...] = (xv[...].astype(jnp.float32) + part[...] + tail(1, colb_ref)).astype(out_ref.dtype)
+
+
+def attend_and_return(queries, limits, history, start, gain, cols, cand_x, gate, w_out, peers, key_rows):
     rows, width = queries.shape
+    homes = cand_x.shape[0]
     kernel = functools.partial(fused_kernel, peers, key_rows)
+    vmem = pl.BlockSpec(memory_space=pltpu.VMEM)
+    hbm = pl.BlockSpec(memory_space=pl.ANY)
     return pl.pallas_call(
         kernel,
-        out_shape=jax.ShapeDtypeStruct((rows, width), jnp.bfloat16),
-        in_specs=[
-            pl.BlockSpec(memory_space=pltpu.VMEM),
-            pl.BlockSpec(memory_space=pltpu.VMEM),
-            pl.BlockSpec(memory_space=pltpu.VMEM),
-            pl.BlockSpec(memory_space=pl.ANY),
-            pl.BlockSpec(memory_space=pl.ANY),
-        ],
-        out_specs=pl.BlockSpec(memory_space=pl.ANY),
+        out_shape=jax.ShapeDtypeStruct((homes, width), jnp.bfloat16),
+        in_specs=[vmem, vmem, vmem, vmem, vmem, hbm, hbm, hbm, hbm, hbm],
+        out_specs=vmem,
         scratch_shapes=[
             pltpu.VMEM((2, key_rows, 2 * width), jnp.bfloat16),
             pltpu.SemaphoreType.DMA((2,)),
             pltpu.VMEM((2, rows // 2, width), jnp.float32),
             pltpu.VMEM((2, rows // 2, width), jnp.bfloat16),
+            pltpu.VMEM((2, rows // 2, width), jnp.bfloat16),
+            pltpu.VMEM((homes, width), jnp.float32),
+            pltpu.VMEM((homes, width), jnp.bfloat16),
+            pltpu.VMEM((homes, width), jnp.bfloat16),
+            pltpu.VMEM(w_out.shape, jnp.bfloat16),
             pltpu.SemaphoreType.DMA((2, peers)),
             pltpu.SemaphoreType.DMA((2, peers)),
             pltpu.SemaphoreType.DMA((2,)),
             pltpu.SemaphoreType.DMA((2,)),
+            pltpu.SemaphoreType.DMA((3,)),
         ],
         compiler_params=pltpu.CompilerParams(
             collective_id=0, has_side_effects=True, vmem_limit_bytes=60 * 1024 * 1024
         ),
         cost_estimate=pl.CostEstimate(
-            flops=8 * rows * history.shape[0] * width,
+            flops=8 * rows * history.shape[0] * width + 4 * homes * width * (rows + width),
             transcendentals=rows * history.shape[0] * HEADS,
             bytes_accessed=2 * history.size * 2 + rows * width * 6,
         ),
-    )(queries, limits, gain.reshape(1, width), history, start)
+    )(queries, limits, gain.reshape(1, width), cols[0], cols[1], history, start, cand_x, gate, w_out)
 
 
 def per_device(cand_x, cand_user, visible, hist_len, kv_cache, w_in, w_out, ln_gain):
@@ -300,14 +325,15 @@
         queries_h, limits_h, segment, jnp.zeros((slots, width), jnp.float32), me, segment.shape[0], False
     )
     history = lax.all_gather(segment, "user", axis=0, tiled=True)
-    returned = attend_and_return(
-        queries_h, limits_h, history, start, ln_gain, columns, segment.shape[0]
-    )
-    pick = (slot_of[:, None] == jnp.arange(slots, dtype=jnp.int32)[None, :]).astype(jnp.bfloat16)
-    home_rows = jnp.dot(pick, returned, preferred_element_type=jnp.float32)
-    mixed_rows = (home_rows.astype(jnp.float32) * gate.astype(jnp.float32)).astype(jnp.bfloat16)
-    projected = jnp.dot(mixed_rows, w_out, preferred_element_type=jnp.float32)
-    return (cand_x.astype(jnp.float32) + projected).astype(jnp.bfloat16)
+    rank = slot_of - owner * capacity
+    half_cap = capacity // 2
+    cols = (
+        jnp.where(rank < half_cap, owner * half_cap + rank, -1).reshape(rows, 1),
+        jnp.where(rank >= half_cap, owner * half_cap + rank - half_cap, -1).reshape(rows, 1),
+    )
+    return attend_and_return(
+        queries_h, limits_h, history, start, ln_gain, cols, cand_x, gate, w_out, columns, segment.shape[0]
+    )
 
 
 def solution(mesh):

time: 183 us -> 182 us (level)
  matrix products: 12.4 us -> 5.77 us
  Pallas kernels: 48.3 us -> 51.5 us
  local copies, waits for them, and re-layouts: 16.6 us -> 19.2 us
    dot_general x1 -> x0, matrix products: 5.22 us -> none  [per_device(): projected = jnp.dot(mixed_rows, w_out, preferred_element_type=jnp.float32)]
    all_to_all x1, waiting for transfers between devices: 25 us -> 21.5 us  [per_device(): lax.all_to_all(send_rows.reshape(columns, capacity, width), 'cand', split...]
    pallas_call x1, Pallas kernels: 40.5 us -> 43.7 us  [attend_and_return(): pl.pallas_call(kernel, out_shape=jax.ShapeDtypeStruct((homes, width), jnp...]
    all_gather x1, waiting for transfers between devices: 48.6 us -> 51.2 us  [per_device(): history = lax.all_gather(segment, 'user', axis=0, tiled=True)]
    slice x1 -> x2, local copies, waits for them, and re-layouts: 0.22 us -> 2.48 us  [the longest x1 2.27 us: per_device(): gate = hidden[:, width:].astype(jnp.bfloat16)]
    unnamed x4 -> x3, local copies, waits for them, and re-layouts: 0.01 us -> 2.27 us
where the time goes in v10:
time: 182 us; the launch traced here: 181 us
  waiting for transfers between devices  73.4 us (40%)
  Pallas kernels  51.5 us (28%)
  local copies, waits for them, and re-layouts  19.2 us (11%)
  between operations  14.1 us (8%)
  starting transfers between devices  12.6 us (7%)
  matrix products  5.77 us (3%)
  other arithmetic  4.89 us (3%)
    all_gather x1, waiting for transfers between devices, per_device(): history = lax.all_gather(segment, 'user', axis=0, tiled=True)  51.2 us
    pallas_call x1, Pallas kernels, attend_and_return(): pl.pallas_call(kernel, out_shape=jax.ShapeDtypeStruct((homes, width), jnp...  43.7 us
    all_to_all x1, waiting for transfers between devices, per_device(): lax.all_to_all(send_rows.reshape(columns, capacity, width), 'cand', split...  21.5 us
    pallas_call x1, Pallas kernels, attend(): pl.pallas_call(kernel, out_shape=jax.ShapeDtypeStruct((rows, width), jnp....  7.8 us
    all_to_all x1, starting transfers between devices, per_device(): lax.all_to_all(send_vis.reshape(columns, capacity), 'cand', split_axis=0,...  6.83 us
    dot_general x1, matrix products, per_device(): jnp.dot(cand_x, w_in, preferred_element_type=jnp.float32)  5.77 us
    all_to_all x1, starting transfers between devices, per_device(): lax.all_to_all(send_rows.reshape(columns, capacity, width), 'cand', split...  5.72 us
    scatter x1, local copies, waits for them, and re-layouts, per_device(): send_rows = jnp.zeros((slots, width), jnp.bfloat16).at[slot_of].set(queries)  4.2 us
  transfers between devices with their start and end apart: 3, of which 2 were waited for; matrix products, arithmetic and copies ran while one was open for 15% of the time, Pallas kernels for 4%

profile of v10, /device:TPU:1, one launch (start us, length us, event | category | flops | bytes accessed | tf_op | source)
XLA Modules:
  0.0 181.4 jit_solution(10781983386563237869)
XLA Ops:
  6.5 0.0 all-gather.3.cloned.1.call-start
  6.5 0.7 all-gather.3.cloned.1.call-update
  7.3 0.7 fusion.6
  7.9 1.1 reduce-window.6
  9.1 0.2 slice_reduce_fusion
  9.3 0.7 convert_element_type.46
  10.0 0.8 fusion.5
  10.8 0.7 broadcast_multiply_fusion
  11.5 3.8 %scatter_custom_fusion.1 = bf16[1024]{0:T(1024)(128)(2,1)S(1)} fusion(s32[512]{0:T(512)S(1)} %bitcast.51, bf16[512]{0:T(512)(128)(2,1)S(1)} %convert_element_type.46, bf16[]{:T(256)} %constant.12.clone.1), kind=kCustom, calls=%fused_computation.20 | custom fusion | bytes 2050 | tf_op jit(solution)/shard_map/scatter | solution.py:302
  15.3 0.7 all_to_all.12
  15.9 6.8 %all-to-all-start.1 = ((bf16[16,1,64]{2,1,0:T(2,128)(2,1)}), bf16[16,1,64]{2,1,0:T(2,128)(2,1)S(1)}, u32[]{:S(2)}, u32[]{:S(2)}) async-start(bf16[16,1,64]{2,1,0:T(2,128)(2,1)} %all_to_all.12), calls=%async_computation.1 | async-start | bytes 16384 | tf_op jit(solution)/shard_map/all_to_all | solution.py:311
  22.8 5.8 %multiply_convert_fusion = bf16[512,2048]{1,0:T(8,128)(2,1)S(1)} fusion(bf16[512,1024]{1,0:T(8,128)(2,1)} %x_hbm.1, bf16[1024,2048]{1,0:T(8,128)(2,1)} %param.13), kind=kOutput, calls=%fused_computation.2 | convolution fusion | flops 2152726528 | bytes 7340032 | tf_op jit(solution)/shard_map/dot_general | solution.py:294
  28.5 0.0 copy-start
  28.6 4.2 %scatter_custom_fusion = bf16[1024,1024]{1,0:T(8,128)(2,1)} fusion(s32[512]{0:T(512)S(1)} %bitcast.52, bf16[512,2048]{1,0:T(8,128)(2,1)S(1)} %multiply_convert_fusion, bf16[]{:T(256)} %constant.12.clone.1), kind=kCustom, calls=%fused_computation.3 | custom fusion | bytes 3145730 | tf_op jit(solution)/shard_map/scatter | solution.py:301
  32.8 0.0 all-to-all-done.1
  32.8 0.0 copy-done
  32.8 5.7 %all-to-all-start = ((bf16[16,64,1024]{2,1,0:T(8,128)(2,1)}), bf16[16,64,1024]{2,1,0:T(8,128)(2,1)S(1)}, u32[]{:S(2)}, u32[]{:S(2)}) async-start(bf16[16,64,1024]{2,1,0:T(8,128)(2,1)} %bitcast.5), calls=%async_computation | async-start | bytes 4194304 | tf_op jit(solution)/shard_map/all_to_all | solution.py:304
  38.5 0.1 copy.40
  38.6 2.3 %slice.20.gate_hbm = bf16[512,1024]{1,0:T(8,128)(2,1)} slice(bf16[512,2048]{1,0:T(8,128)(2,1)} %copy-done), slice={[0:512], [1024:2048]} | slice | bytes 2097152 | tf_op jit(solution)/shard_map/slice | solution.py:296
  41.6 0.1 copy.42
  41.7 0.9 add_select_fusion
  42.6 0.1 convert_element_type.49
  42.7 1.3 reshape.103.lim_ref
  44.0 21.5 %all-to-all-done = bf16[16,64,1024]{2,1,0:T(8,128)(2,1)S(1)} async-done(((bf16[16,64,1024]{2,1,0:T(8,128)(2,1)}), bf16[16,64,1024]{2,1,0:T(8,128)(2,1)S(1)}, u32[]{:S(2)}, u32[]{:S(2)}) %all-to-all-start) | async-done | bytes 2097184 | tf_op jit(solution)/shard_map/all_to_all | solution.py:304
  65.5 1.6 copy.36
  67.1 2.5 %broadcast_in_dim.20.acc_ref = f32[1024,1024]{1,0:T(8,128)} broadcast(f32[]{:T(128)} %constant.32.clone.1), dimensions={} | broadcast | bytes 4194308 | tf_op jit(solution)/shard_map/broadcast_in_dim | solution.py:325
  69.6 7.8 %shard_map.82.start_hbm = f32[1024,1024]{1,0:T(8,128)} custom-call(s32[1]{0:T(128)} %bitcast.13.base_ref, bf16[1024,1024]{1,0:T(8,128)(2,1)} %bitcast.43, s32[1024,1]{1,0:T(8,128)} %reshape.103.lim_ref, bf16[256,2048]{1,0:T(8,128)(2,1)} %bitcast.45, f32[1024,1024]{1,0:T(8,128)} %broadcast_in_dim.20.acc_ref), custom_call_target="tpu_custom_call", output_to_operand_aliasing={{}: (4, {})} | custom-call | flops 1073741824 | bytes 11534336 | tf_op jit(solution)/shard_map/pallas_call | solution.py:70
  77.4 51.2 %all-gather.3.cloned.1.call-done = bf16[1,2048,2048]{2,1,0:T(8,128)(2,1)} async-done(((bf16[1,256,2048]{2,1,0:T(8,128)(2,1)}), bf16[1,2048,2048]{2,1,0:T(8,128)(2,1)}) %all-gather.3.cloned.1.call-update) | async-done | bytes 8388624 | tf_op jit(solution)/shard_map/all_gather | solution.py:327
  128.6 43.7 %shard_map.83 = bf16[512,1024]{1,0:T(8,128)(2,1)} custom-call(bf16[1024,1024]{1,0:T(8,128)(2,1)} %bitcast.44, s32[1024,1]{1,0:T(8,128)} %reshape.103.lim_ref, f32[1,1024]{1,0:T(1,128)} %bitcast.54, s32[512,1]{1,0:T(8,128)} %get-tuple-element.6.cola_ref, s32[512,1]{1,0:T(8,128)} %get-tuple-element.5.colb_ref, bf16[2048,2048]{1,0:T(8,128)(2,1)} %bitcast.53, ...), custom_call_target="tpu_custom_call" | custom-call | flops 21474836480 | bytes 23068672 | tf_op jit(solution)/shard_map/pallas_call | solution.py:257
  172.3 2.3 %copy.53 = bf16[512,1024]{1,0:T(8,128)(2,1)} copy(bf16[512,1024]{1,0:T(8,128)(2,1)} %shard_map.83) | data formatting | bytes 2097152
  (4 shorter events, 0.1 us)
Async XLA Ops:
  6.5 122.0 %all-gather.3.cloned.1.call-start = ((), (), s32[]{:S(2)}) async-start(), calls=%async_computation.2 | async-start | bytes 9437184 | tf_op jit(solution)/shard_map/all_gather | solution.py:327
  15.9 16.8 %all-to-all-start.1 = ((bf16[16,1,64]{2,1,0:T(2,128)(2,1)}), bf16[16,1,64]{2,1,0:T(2,128)(2,1)S(1)}, u32[]{:S(2)}, u32[]{:S(2)}) async-start(bf16[16,1,64]{2,1,0:T(2,128)(2,1)} %all_to_all.12), calls=%async_computation.1 | async-start | bytes 16384 | tf_op jit(solution)/shard_map/all_to_all | solution.py:311
  28.5 4.2 %copy-start = (bf16[512,2048]{1,0:T(8,128)(2,1)}, bf16[512,2048]{1,0:T(8,128)(2,1)S(1)}, u32[]{:S(2)}) copy-start(bf16[512,2048]{1,0:T(8,128)(2,1)S(1)} %multiply_convert_fusion) | copy-start | bytes 6291460
  32.8 32.8 %all-to-all-start = ((bf16[16,64,1024]{2,1,0:T(8,128)(2,1)}), bf16[16,64,1024]{2,1,0:T(8,128)(2,1)S(1)}, u32[]{:S(2)}, u32[]{:S(2)}) async-start(bf16[16,64,1024]{2,1,0:T(8,128)(2,1)} %bitcast.5), calls=%async_computation | async-start | bytes 4194304 | tf_op jit(solution)/shard_map/all_to_all | solution.py:304
Sparse Core Ops, SparseCore 0:
  9.7 118.8 all-gather.2

commit v11 on v10

--- a/solution.py
+++ b/solution.py
@@ -97,7 +97,7 @@
 
 
 def fused_kernel(peers, key_rows, q_ref, lim_ref, gain_ref, cola_ref, colb_ref, hist_hbm, start_hbm,
-                 x_hbm, gate_hbm, wout_hbm, out_ref, kv_buf, kv_sem, acc, normed, ret, part, xv, gv, wv,
+                 gate_hbm, wout_hbm, out_ref, kv_buf, kv_sem, acc, normed, ret, part, gv, wv,
                  send_sem, recv_sem, local_sem, start_sem, misc_sem):
     me = lax.axis_index("cand")
     uid = lax.axis_index("user")
@@ -175,7 +175,7 @@
     start_copy(1).start()
     misc = [
         pltpu.make_async_copy(src, dst, misc_sem.at[n])
-        for n, (src, dst) in enumerate(((x_hbm, xv), (gate_hbm, gv), (wout_hbm, wv)))
+        for n, (src, dst) in enumerate(((gate_hbm, gv), (wout_hbm, wv)))
     ]
     for copy in misc:
         copy.start()
@@ -245,7 +245,7 @@
     for half in range(2):
         for j in range(1, peers):
             remote(half, j).wait_send()
-    out_ref[...] = (xv[...].astype(jnp.float32) + part[...] + tail(1, colb_ref)).astype(out_ref.dtype)
+    out_ref[...] = part[...] + tail(1, colb_ref)
 
 
 def attend_and_return(queries, limits, history, start, gain, cols, cand_x, gate, w_out, peers, key_rows):
@@ -256,8 +256,8 @@
     hbm = pl.BlockSpec(memory_space=pl.ANY)
     return pl.pallas_call(
         kernel,
-        out_shape=jax.ShapeDtypeStruct((homes, width), jnp.bfloat16),
-        in_specs=[vmem, vmem, vmem, vmem, vmem, hbm, hbm, hbm, hbm, hbm],
+        out_shape=jax.ShapeDtypeStruct((homes, width), jnp.float32),
+        in_specs=[vmem, vmem, vmem, vmem, vmem, hbm, hbm, hbm, hbm],
         out_specs=vmem,
         scratch_shapes=[
             pltpu.VMEM((2, key_rows, 2 * width), jnp.bfloat16),
@@ -267,13 +267,12 @@
             pltpu.VMEM((2, rows // 2, width), jnp.bfloat16),
             pltpu.VMEM((homes, width), jnp.float32),
             pltpu.VMEM((homes, width), jnp.bfloat16),
-            pltpu.VMEM((homes, width), jnp.bfloat16),
             pltpu.VMEM(w_out.shape, jnp.bfloat16),
             pltpu.SemaphoreType.DMA((2, peers)),
             pltpu.SemaphoreType.DMA((2, peers)),
             pltpu.SemaphoreType.DMA((2,)),
             pltpu.SemaphoreType.DMA((2,)),
-            pltpu.SemaphoreType.DMA((3,)),
+            pltpu.SemaphoreType.DMA((2,)),
         ],
         compiler_params=pltpu.CompilerParams(
             collective_id=0, has_side_effects=True, vmem_limit_bytes=60 * 1024 * 1024
@@ -283,7 +282,7 @@
             transcendentals=rows * history.shape[0] * HEADS,
             bytes_accessed=2 * history.size * 2 + rows * width * 6,
         ),
-    )(queries, limits, gain.reshape(1, width), cols[0], cols[1], history, start, cand_x, gate, w_out)
+    )(queries, limits, gain.reshape(1, width), cols[0], cols[1], history, start, gate, w_out)
 
 
 def per_device(cand_x, cand_user, visible, hist_len, kv_cache, w_in, w_out, ln_gain):
@@ -331,9 +330,10 @@
         jnp.where(rank < half_cap, owner * half_cap + rank, -1).reshape(rows, 1),
         jnp.where(rank >= half_cap, owner * half_cap + rank - half_cap, -1).reshape(rows, 1),
     )
-    return attend_and_return(
+    projected = attend_and_return(
         queries_h, limits_h, history, start, ln_gain, cols, cand_x, gate, w_out, columns, segment.shape[0]
     )
+    return (cand_x.astype(jnp.float32) + projected).astype(jnp.bfloat16)
 
 
 def solution(mesh):

time: 182 us -> 183 us (level)
  other arithmetic: 4.89 us -> 7.81 us
  local copies, waits for them, and re-layouts: 19.2 us -> 16.9 us
    convert_element_type x0 -> x1, other arithmetic: none -> 2.91 us  [per_device(): return (cand_x.astype(jnp.float32) + projected).astype(jnp.bfloat16)]
    unnamed x3 -> x4, local copies, waits for them, and re-layouts: 2.27 us -> 0.01 us
where the time goes in v11:
time: 183 us; the launch traced here: 182 us
  waiting for transfers between devices  73.4 us (40%)
  Pallas kernels  51.7 us (28%)
  local copies, waits for them, and re-layouts  16.9 us (9%)
  between operations  14.1 us (8%)
  starting transfers between devices  12.6 us (7%)
  other arithmetic  7.81 us (4%)
  matrix products  5.77 us (3%)
    all_gather x1, waiting for transfers between devices, per_device(): history = lax.all_gather(segment, 'user', axis=0, tiled=True)  51.2 us
    pallas_call x1, Pallas kernels, attend_and_return(): pl.pallas_call(kernel, out_shape=jax.ShapeDtypeStruct((homes, width), jnp...  43.9 us
    all_to_all x1, waiting for transfers between devices, per_device(): lax.all_to_all(send_rows.reshape(columns, capacity, width), 'cand', split...  21.5 us
    pallas_call x1, Pallas kernels, attend(): pl.pallas_call(kernel, out_shape=jax.ShapeDtypeStruct((rows, width), jnp....  7.8 us
    all_to_all x1, starting transfers between devices, per_device(): lax.all_to_all(send_vis.reshape(columns, capacity), 'cand', split_axis=0,...  6.83 us
    dot_general x1, matrix products, per_device(): jnp.dot(cand_x, w_in, preferred_element_type=jnp.float32)  5.77 us
    all_to_all x1, starting transfers between devices, per_device(): lax.all_to_all(send_rows.reshape(columns, capacity, width), 'cand', split...  5.72 us
    scatter x1, local copies, waits for them, and re-layouts, per_device(): send_rows = jnp.zeros((slots, width), jnp.bfloat16).at[slot_of].set(queries)  4.2 us
  transfers between devices with their start and end apart: 3, of which 2 were waited for; matrix products, arithmetic and copies ran while one was open for 15% of the time, Pallas kernels for 4%

profile of v11, /device:TPU:1, one launch (start us, length us, event | category | flops | bytes accessed | tf_op | source)
XLA Modules:
  0.0 182.2 jit_solution(11372719890208068060)
XLA Ops:
  6.5 0.0 all-gather.3.cloned.1.call-start
  6.5 0.7 all-gather.3.cloned.1.call-update
  7.3 0.7 fusion.6
  7.9 1.1 reduce-window.6
  9.1 0.2 slice_reduce_fusion
  9.3 0.7 convert_element_type.53
  10.0 0.8 fusion.5
  10.8 0.7 broadcast_multiply_fusion
  11.5 3.8 %scatter_custom_fusion.1 = bf16[1024]{0:T(1024)(128)(2,1)S(1)} fusion(s32[512]{0:T(512)S(1)} %bitcast.51, bf16[512]{0:T(512)(128)(2,1)S(1)} %convert_element_type.53, bf16[]{:T(256)} %constant.12.clone.1), kind=kCustom, calls=%fused_computation.21 | custom fusion | bytes 2050 | tf_op jit(solution)/shard_map/scatter | solution.py:301
  15.3 0.7 all_to_all.12
  15.9 6.8 %all-to-all-start.1 = ((bf16[16,1,64]{2,1,0:T(2,128)(2,1)}), bf16[16,1,64]{2,1,0:T(2,128)(2,1)S(1)}, u32[]{:S(2)}, u32[]{:S(2)}) async-start(bf16[16,1,64]{2,1,0:T(2,128)(2,1)} %all_to_all.12), calls=%async_computation.1 | async-start | bytes 16384 | tf_op jit(solution)/shard_map/all_to_all | solution.py:310
  22.8 5.8 %multiply_convert_fusion = bf16[512,2048]{1,0:T(8,128)(2,1)S(1)} fusion(bf16[512,1024]{1,0:T(8,128)(2,1)} %param.8, bf16[1024,2048]{1,0:T(8,128)(2,1)} %param.13), kind=kOutput, calls=%fused_computation.2 | convolution fusion | flops 2152726528 | bytes 7340032 | tf_op jit(solution)/shard_map/dot_general | solution.py:293
  28.5 0.0 copy-start
  28.6 4.2 %scatter_custom_fusion = bf16[1024,1024]{1,0:T(8,128)(2,1)} fusion(s32[512]{0:T(512)S(1)} %bitcast.52, bf16[512,2048]{1,0:T(8,128)(2,1)S(1)} %multiply_convert_fusion, bf16[]{:T(256)} %constant.12.clone.1), kind=kCustom, calls=%fused_computation.4 | custom fusion | bytes 3145730 | tf_op jit(solution)/shard_map/scatter | solution.py:300
  32.8 0.0 all-to-all-done.1
  32.8 0.0 copy-done
  32.8 5.7 %all-to-all-start = ((bf16[16,64,1024]{2,1,0:T(8,128)(2,1)}), bf16[16,64,1024]{2,1,0:T(8,128)(2,1)S(1)}, u32[]{:S(2)}, u32[]{:S(2)}) async-start(bf16[16,64,1024]{2,1,0:T(8,128)(2,1)} %bitcast.5), calls=%async_computation | async-start | bytes 4194304 | tf_op jit(solution)/shard_map/all_to_all | solution.py:303
  38.5 0.1 copy.40
  38.6 2.3 %slice.20.gate_hbm = bf16[512,1024]{1,0:T(8,128)(2,1)} slice(bf16[512,2048]{1,0:T(8,128)(2,1)} %copy-done), slice={[0:512], [1024:2048]} | slice | bytes 2097152 | tf_op jit(solution)/shard_map/slice | solution.py:295
  41.6 0.1 copy.42
  41.7 0.9 add_select_fusion
  42.6 0.1 convert_element_type.56
  42.7 1.3 reshape.103.lim_ref
  44.0 21.5 %all-to-all-done = bf16[16,64,1024]{2,1,0:T(8,128)(2,1)S(1)} async-done(((bf16[16,64,1024]{2,1,0:T(8,128)(2,1)}), bf16[16,64,1024]{2,1,0:T(8,128)(2,1)S(1)}, u32[]{:S(2)}, u32[]{:S(2)}) %all-to-all-start) | async-done | bytes 2097184 | tf_op jit(solution)/shard_map/all_to_all | solution.py:303
  65.5 1.6 copy.36
  67.1 2.5 %broadcast_in_dim.20.acc_ref = f32[1024,1024]{1,0:T(8,128)} broadcast(f32[]{:T(128)} %constant.32.clone.1), dimensions={} | broadcast | bytes 4194308 | tf_op jit(solution)/shard_map/broadcast_in_dim | solution.py:324
  69.6 7.8 %shard_map.82.start_hbm = f32[1024,1024]{1,0:T(8,128)} custom-call(s32[1]{0:T(128)} %bitcast.13.base_ref, bf16[1024,1024]{1,0:T(8,128)(2,1)} %bitcast.43, s32[1024,1]{1,0:T(8,128)} %reshape.103.lim_ref, bf16[256,2048]{1,0:T(8,128)(2,1)} %bitcast.45, f32[1024,1024]{1,0:T(8,128)} %broadcast_in_dim.20.acc_ref), custom_call_target="tpu_custom_call", output_to_operand_aliasing={{}: (4, {})} | custom-call | flops 1073741824 | bytes 11534336 | tf_op jit(solution)/shard_map/pallas_call | solution.py:70
  77.4 51.2 %all-gather.3.cloned.1.call-done = bf16[1,2048,2048]{2,1,0:T(8,128)(2,1)} async-done(((bf16[1,256,2048]{2,1,0:T(8,128)(2,1)}), bf16[1,2048,2048]{2,1,0:T(8,128)(2,1)}) %all-gather.3.cloned.1.call-update) | async-done | bytes 8388624 | tf_op jit(solution)/shard_map/all_gather | solution.py:326
  128.6 0.0 copy-start.1
  128.6 43.9 %shard_map.83 = f32[512,1024]{1,0:T(8,128)} custom-call(bf16[1024,1024]{1,0:T(8,128)(2,1)} %bitcast.44, s32[1024,1]{1,0:T(8,128)} %reshape.103.lim_ref, f32[1,1024]{1,0:T(1,128)} %bitcast.54, s32[512,1]{1,0:T(8,128)} %get-tuple-element.6.cola_ref, s32[512,1]{1,0:T(8,128)} %get-tuple-element.5.colb_ref, bf16[2048,2048]{1,0:T(8,128)(2,1)} %bitcast.53, ...), custom_call_target="tpu_custom_call" | custom-call | flops 21474836480 | bytes 23068672 | tf_op jit(solution)/shard_map/pallas_call | solution.py:257
  172.4 0.0 copy-done.1
  172.5 2.9 %add_convert_fusion = bf16[512,1024]{1,0:T(8,128)(2,1)} fusion(f32[512,1024]{1,0:T(8,128)} %shard_map.83, bf16[512,1024]{1,0:T(8,128)(2,1)S(1)} %copy-done.1), kind=kLoop, calls=%fused_computation.3 | loop fusion | flops 1572864 | bytes 4194304 | tf_op jit(solution)/shard_map/convert_element_type | solution.py:336
  (4 shorter events, 0.1 us)
Async XLA Ops:
  6.5 122.0 %all-gather.3.cloned.1.call-start = ((), (), s32[]{:S(2)}) async-start(), calls=%async_computation.2 | async-start | bytes 9437184 | tf_op jit(solution)/shard_map/all_gather | solution.py:326
  15.9 16.8 %all-to-all-start.1 = ((bf16[16,1,64]{2,1,0:T(2,128)(2,1)}), bf16[16,1,64]{2,1,0:T(2,128)(2,1)S(1)}, u32[]{:S(2)}, u32[]{:S(2)}) async-start(bf16[16,1,64]{2,1,0:T(2,128)(2,1)} %all_to_all.12), calls=%async_computation.1 | async-start | bytes 16384 | tf_op jit(solution)/shard_map/all_to_all | solution.py:310
  28.5 4.2 %copy-start = (bf16[512,2048]{1,0:T(8,128)(2,1)}, bf16[512,2048]{1,0:T(8,128)(2,1)S(1)}, u32[]{:S(2)}) copy-start(bf16[512,2048]{1,0:T(8,128)(2,1)S(1)} %multiply_convert_fusion) | copy-start | bytes 6291460
  32.8 32.8 %all-to-all-start = ((bf16[16,64,1024]{2,1,0:T(8,128)(2,1)}), bf16[16,64,1024]{2,1,0:T(8,128)(2,1)S(1)}, u32[]{:S(2)}, u32[]{:S(2)}) async-start(bf16[16,64,1024]{2,1,0:T(8,128)(2,1)} %bitcast.5), calls=%async_computation | async-start | bytes 4194304 | tf_op jit(solution)/shard_map/all_to_all | solution.py:303
  128.6 43.9 %copy-start.1 = (bf16[512,1024]{1,0:T(8,128)(2,1)S(1)}, bf16[512,1024]{1,0:T(8,128)(2,1)}, u32[]{:S(2)}) copy-start(bf16[512,1024]{1,0:T(8,128)(2,1)} %param.8) | copy-start | bytes 3145732
Sparse Core Ops, SparseCore 0:
  9.7 118.8 all-gather.2

commit v12 on v10

--- a/solution.py
+++ b/solution.py
@@ -242,10 +242,10 @@
     local(1).wait()
     for j in range(1, peers):
         incoming(1, j).wait_recv()
+    out_ref[...] = (xv[...].astype(jnp.float32) + part[...] + tail(1, colb_ref)).astype(out_ref.dtype)
     for half in range(2):
         for j in range(1, peers):
             remote(half, j).wait_send()
-    out_ref[...] = (xv[...].astype(jnp.float32) + part[...] + tail(1, colb_ref)).astype(out_ref.dtype)
 
 
 def attend_and_return(queries, limits, history, start, gain, cols, cand_x, gate, w_out, peers, key_rows):

time: 182 us -> 182 us (level)
  no operation moved by 1% of the time
where the time goes in v12:
time: 182 us; the launch traced here: 181 us
  waiting for transfers between devices  73.4 us (40%)
  Pallas kernels  51.5 us (28%)
  local copies, waits for them, and re-layouts  19.2 us (11%)
  between operations  14.1 us (8%)
  starting transfers between devices  12.6 us (7%)
  matrix products  5.77 us (3%)
  other arithmetic  4.89 us (3%)
    all_gather x1, waiting for transfers between devices, per_device(): history = lax.all_gather(segment, 'user', axis=0, tiled=True)  51.2 us
    pallas_call x1, Pallas kernels, attend_and_return(): pl.pallas_call(kernel, out_shape=jax.ShapeDtypeStruct((homes, width), jnp...  43.7 us
    all_to_all x1, waiting for transfers between devices, per_device(): lax.all_to_all(send_rows.reshape(columns, capacity, width), 'cand', split...  21.5 us
    pallas_call x1, Pallas kernels, attend(): pl.pallas_call(kernel, out_shape=jax.ShapeDtypeStruct((rows, width), jnp....  7.8 us
    all_to_all x1, starting transfers between devices, per_device(): lax.all_to_all(send_vis.reshape(columns, capacity), 'cand', split_axis=0,...  6.83 us
    dot_general x1, matrix products, per_device(): jnp.dot(cand_x, w_in, preferred_element_type=jnp.float32)  5.77 us
    all_to_all x1, starting transfers between devices, per_device(): lax.all_to_all(send_rows.reshape(columns, capacity, width), 'cand', split...  5.72 us
    scatter x1, local copies, waits for them, and re-layouts, per_device(): send_rows = jnp.zeros((slots, width), jnp.bfloat16).at[slot_of].set(queries)  4.2 us
  transfers between devices with their start and end apart: 3, of which 2 were waited for; matrix products, arithmetic and copies ran while one was open for 15% of the time, Pallas kernels for 4%

profile of v12, /device:TPU:1, one launch (start us, length us, event | category | flops | bytes accessed | tf_op | source)
XLA Modules:
  0.0 181.4 jit_solution(6679117093186340603)
XLA Ops:
  6.5 0.0 all-gather.3.cloned.1.call-start
  6.5 0.7 all-gather.3.cloned.1.call-update
  7.3 0.7 fusion.6
  7.9 1.1 reduce-window.6
  9.1 0.2 slice_reduce_fusion
  9.3 0.7 convert_element_type.46
  10.0 0.8 fusion.5
  10.8 0.7 broadcast_multiply_fusion
  11.5 3.8 %scatter_custom_fusion.1 = bf16[1024]{0:T(1024)(128)(2,1)S(1)} fusion(s32[512]{0:T(512)S(1)} %bitcast.51, bf16[512]{0:T(512)(128)(2,1)S(1)} %convert_element_type.46, bf16[]{:T(256)} %constant.12.clone.1), kind=kCustom, calls=%fused_computation.20 | custom fusion | bytes 2050 | tf_op jit(solution)/shard_map/scatter | solution.py:302
  15.3 0.7 all_to_all.12
  15.9 6.8 %all-to-all-start.1 = ((bf16[16,1,64]{2,1,0:T(2,128)(2,1)}), bf16[16,1,64]{2,1,0:T(2,128)(2,1)S(1)}, u32[]{:S(2)}, u32[]{:S(2)}) async-start(bf16[16,1,64]{2,1,0:T(2,128)(2,1)} %all_to_all.12), calls=%async_computation.1 | async-start | bytes 16384 | tf_op jit(solution)/shard_map/all_to_all | solution.py:311
  22.8 5.8 %multiply_convert_fusion = bf16[512,2048]{1,0:T(8,128)(2,1)S(1)} fusion(bf16[512,1024]{1,0:T(8,128)(2,1)} %x_hbm.1, bf16[1024,2048]{1,0:T(8,128)(2,1)} %param.13), kind=kOutput, calls=%fused_computation.2 | convolution fusion | flops 2152726528 | bytes 7340032 | tf_op jit(solution)/shard_map/dot_general | solution.py:294
  28.5 0.0 copy-start
  28.6 4.2 %scatter_custom_fusion = bf16[1024,1024]{1,0:T(8,128)(2,1)} fusion(s32[512]{0:T(512)S(1)} %bitcast.52, bf16[512,2048]{1,0:T(8,128)(2,1)S(1)} %multiply_convert_fusion, bf16[]{:T(256)} %constant.12.clone.1), kind=kCustom, calls=%fused_computation.3 | custom fusion | bytes 3145730 | tf_op jit(solution)/shard_map/scatter | solution.py:301
  32.8 0.0 all-to-all-done.1
  32.8 0.0 copy-done
  32.8 5.7 %all-to-all-start = ((bf16[16,64,1024]{2,1,0:T(8,128)(2,1)}), bf16[16,64,1024]{2,1,0:T(8,128)(2,1)S(1)}, u32[]{:S(2)}, u32[]{:S(2)}) async-start(bf16[16,64,1024]{2,1,0:T(8,128)(2,1)} %bitcast.5), calls=%async_computation | async-start | bytes 4194304 | tf_op jit(solution)/shard_map/all_to_all | solution.py:304
  38.5 0.1 copy.40
  38.6 2.3 %slice.20.gate_hbm = bf16[512,1024]{1,0:T(8,128)(2,1)} slice(bf16[512,2048]{1,0:T(8,128)(2,1)} %copy-done), slice={[0:512], [1024:2048]} | slice | bytes 2097152 | tf_op jit(solution)/shard_map/slice | solution.py:296
  41.6 0.1 copy.42
  41.7 0.9 add_select_fusion
  42.6 0.1 convert_element_type.49
  42.7 1.3 reshape.103.lim_ref
  44.0 21.5 %all-to-all-done = bf16[16,64,1024]{2,1,0:T(8,128)(2,1)S(1)} async-done(((bf16[16,64,1024]{2,1,0:T(8,128)(2,1)}), bf16[16,64,1024]{2,1,0:T(8,128)(2,1)S(1)}, u32[]{:S(2)}, u32[]{:S(2)}) %all-to-all-start) | async-done | bytes 2097184 | tf_op jit(solution)/shard_map/all_to_all | solution.py:304
  65.5 1.6 copy.36
  67.1 2.5 %broadcast_in_dim.20.acc_ref = f32[1024,1024]{1,0:T(8,128)} broadcast(f32[]{:T(128)} %constant.32.clone.1), dimensions={} | broadcast | bytes 4194308 | tf_op jit(solution)/shard_map/broadcast_in_dim | solution.py:325
  69.6 7.8 %shard_map.82.start_hbm = f32[1024,1024]{1,0:T(8,128)} custom-call(s32[1]{0:T(128)} %bitcast.13.base_ref, bf16[1024,1024]{1,0:T(8,128)(2,1)} %bitcast.43, s32[1024,1]{1,0:T(8,128)} %reshape.103.lim_ref, bf16[256,2048]{1,0:T(8,128)(2,1)} %bitcast.45, f32[1024,1024]{1,0:T(8,128)} %broadcast_in_dim.20.acc_ref), custom_call_target="tpu_custom_call", output_to_operand_aliasing={{}: (4, {})} | custom-call | flops 1073741824 | bytes 11534336 | tf_op jit(solution)/shard_map/pallas_call | solution.py:70
  77.4 51.2 %all-gather.3.cloned.1.call-done = bf16[1,2048,2048]{2,1,0:T(8,128)(2,1)} async-done(((bf16[1,256,2048]{2,1,0:T(8,128)(2,1)}), bf16[1,2048,2048]{2,1,0:T(8,128)(2,1)}) %all-gather.3.cloned.1.call-update) | async-done | bytes 8388624 | tf_op jit(solution)/shard_map/all_gather | solution.py:327
  128.6 43.7 %shard_map.83 = bf16[512,1024]{1,0:T(8,128)(2,1)} custom-call(bf16[1024,1024]{1,0:T(8,128)(2,1)} %bitcast.44, s32[1024,1]{1,0:T(8,128)} %reshape.103.lim_ref, f32[1,1024]{1,0:T(1,128)} %bitcast.54, s32[512,1]{1,0:T(8,128)} %get-tuple-element.6.cola_ref, s32[512,1]{1,0:T(8,128)} %get-tuple-element.5.colb_ref, bf16[2048,2048]{1,0:T(8,128)(2,1)} %bitcast.53, ...), custom_call_target="tpu_custom_call" | custom-call | flops 21474836480 | bytes 23068672 | tf_op jit(solution)/shard_map/pallas_call | solution.py:257
  172.3 2.3 %copy.53 = bf16[512,1024]{1,0:T(8,128)(2,1)} copy(bf16[512,1024]{1,0:T(8,128)(2,1)} %shard_map.83) | data formatting | bytes 2097152
  (4 shorter events, 0.1 us)
Async XLA Ops:
  6.5 122.0 %all-gather.3.cloned.1.call-start = ((), (), s32[]{:S(2)}) async-start(), calls=%async_computation.2 | async-start | bytes 9437184 | tf_op jit(solution)/shard_map/all_gather | solution.py:327
  15.9 16.8 %all-to-all-start.1 = ((bf16[16,1,64]{2,1,0:T(2,128)(2,1)}), bf16[16,1,64]{2,1,0:T(2,128)(2,1)S(1)}, u32[]{:S(2)}, u32[]{:S(2)}) async-start(bf16[16,1,64]{2,1,0:T(2,128)(2,1)} %all_to_all.12), calls=%async_computation.1 | async-start | bytes 16384 | tf_op jit(solution)/shard_map/all_to_all | solution.py:311
  28.5 4.2 %copy-start = (bf16[512,2048]{1,0:T(8,128)(2,1)}, bf16[512,2048]{1,0:T(8,128)(2,1)S(1)}, u32[]{:S(2)}) copy-start(bf16[512,2048]{1,0:T(8,128)(2,1)S(1)} %multiply_convert_fusion) | copy-start | bytes 6291460
  32.8 32.8 %all-to-all-start = ((bf16[16,64,1024]{2,1,0:T(8,128)(2,1)}), bf16[16,64,1024]{2,1,0:T(8,128)(2,1)S(1)}, u32[]{:S(2)}, u32[]{:S(2)}) async-start(bf16[16,64,1024]{2,1,0:T(8,128)(2,1)} %bitcast.5), calls=%async_computation | async-start | bytes 4194304 | tf_op jit(solution)/shard_map/all_to_all | solution.py:304
Sparse Core Ops, SparseCore 0:
  9.7 118.8 all-gather.2

commit v13 on v10

--- a/solution.py
+++ b/solution.py
@@ -177,8 +177,6 @@
         pltpu.make_async_copy(src, dst, misc_sem.at[n])
         for n, (src, dst) in enumerate(((x_hbm, xv), (gate_hbm, gv), (wout_hbm, wv)))
     ]
-    for copy in misc:
-        copy.start()
 
     def tail(half, col_ref):
         homes = col_ref.shape[0]
@@ -220,6 +218,9 @@
             return carry
 
         lax.fori_loop(0, segments, step, 0)
+        if half == 0:
+            for copy in misc:
+                copy.start()
         value = total[...]
         mean_row = jnp.mean(value, axis=1, keepdims=True)
         centered = value - mean_row

time: 182 us -> 181 us (level)
  no operation moved by 1% of the time
where the time goes in v13:
time: 181 us
  waiting for transfers between devices  73.4 us (41%)
  Pallas kernels  50.6 us (28%)
  local copies, waits for them, and re-layouts  19.2 us (11%)
  between operations  14.1 us (8%)
  starting transfers between devices  12.6 us (7%)
  matrix products  5.77 us (3%)
  other arithmetic  4.89 us (3%)
    all_gather x1, waiting for transfers between devices, per_device(): history = lax.all_gather(segment, 'user', axis=0, tiled=True)  51.2 us
    pallas_call x1, Pallas kernels, attend_and_return(): pl.pallas_call(kernel, out_shape=jax.ShapeDtypeStruct((homes, width), jnp...  42.8 us
    all_to_all x1, waiting for transfers between devices, per_device(): lax.all_to_all(send_rows.reshape(columns, capacity, width), 'cand', split...  21.5 us
    pallas_call x1, Pallas kernels, attend(): pl.pallas_call(kernel, out_shape=jax.ShapeDtypeStruct((rows, width), jnp....  7.8 us
    all_to_all x1, starting transfers between devices, per_device(): lax.all_to_all(send_vis.reshape(columns, capacity), 'cand', split_axis=0,...  6.83 us
    dot_general x1, matrix products, per_device(): jnp.dot(cand_x, w_in, preferred_element_type=jnp.float32)  5.77 us
    all_to_all x1, starting transfers between devices, per_device(): lax.all_to_all(send_rows.reshape(columns, capacity, width), 'cand', split...  5.72 us
    scatter x1, local copies, waits for them, and re-layouts, per_device(): send_rows = jnp.zeros((slots, width), jnp.bfloat16).at[slot_of].set(queries)  4.2 us
  transfers between devices with their start and end apart: 3, of which 2 were waited for; matrix products, arithmetic and copies ran while one was open for 15% of the time, Pallas kernels for 4%

profile of v13, /device:TPU:1, one launch (start us, length us, event | category | flops | bytes accessed | tf_op | source)
XLA Modules:
  0.0 180.5 jit_solution(2348978795814775730)
XLA Ops:
  6.5 0.0 all-gather.3.cloned.1.call-start
  6.5 0.7 all-gather.3.cloned.1.call-update
  7.3 0.7 fusion.6
  7.9 1.1 reduce-window.6
  9.1 0.2 slice_reduce_fusion
  9.3 0.7 convert_element_type.46
  10.0 0.8 fusion.5
  10.8 0.7 broadcast_multiply_fusion
  11.5 3.8 %scatter_custom_fusion.1 = bf16[1024]{0:T(1024)(128)(2,1)S(1)} fusion(s32[512]{0:T(512)S(1)} %bitcast.51, bf16[512]{0:T(512)(128)(2,1)S(1)} %convert_element_type.46, bf16[]{:T(256)} %constant.12.clone.1), kind=kCustom, calls=%fused_computation.20 | custom fusion | bytes 2050 | tf_op jit(solution)/shard_map/scatter | solution.py:303
  15.3 0.7 all_to_all.12
  15.9 6.8 %all-to-all-start.1 = ((bf16[16,1,64]{2,1,0:T(2,128)(2,1)}), bf16[16,1,64]{2,1,0:T(2,128)(2,1)S(1)}, u32[]{:S(2)}, u32[]{:S(2)}) async-start(bf16[16,1,64]{2,1,0:T(2,128)(2,1)} %all_to_all.12), calls=%async_computation.1 | async-start | bytes 16384 | tf_op jit(solution)/shard_map/all_to_all | solution.py:312
  22.8 5.8 %multiply_convert_fusion = bf16[512,2048]{1,0:T(8,128)(2,1)S(1)} fusion(bf16[512,1024]{1,0:T(8,128)(2,1)} %x_hbm.1, bf16[1024,2048]{1,0:T(8,128)(2,1)} %param.13), kind=kOutput, calls=%fused_computation.2 | convolution fusion | flops 2152726528 | bytes 7340032 | tf_op jit(solution)/shard_map/dot_general | solution.py:295
  28.5 0.0 copy-start
  28.6 4.2 %scatter_custom_fusion = bf16[1024,1024]{1,0:T(8,128)(2,1)} fusion(s32[512]{0:T(512)S(1)} %bitcast.52, bf16[512,2048]{1,0:T(8,128)(2,1)S(1)} %multiply_convert_fusion, bf16[]{:T(256)} %constant.12.clone.1), kind=kCustom, calls=%fused_computation.3 | custom fusion | bytes 3145730 | tf_op jit(solution)/shard_map/scatter | solution.py:302
  32.8 0.0 all-to-all-done.1
  32.8 0.0 copy-done
  32.8 5.7 %all-to-all-start = ((bf16[16,64,1024]{2,1,0:T(8,128)(2,1)}), bf16[16,64,1024]{2,1,0:T(8,128)(2,1)S(1)}, u32[]{:S(2)}, u32[]{:S(2)}) async-start(bf16[16,64,1024]{2,1,0:T(8,128)(2,1)} %bitcast.5), calls=%async_computation | async-start | bytes 4194304 | tf_op jit(solution)/shard_map/all_to_all | solution.py:305
  38.5 0.1 copy.40
  38.6 2.3 %slice.20.gate_hbm = bf16[512,1024]{1,0:T(8,128)(2,1)} slice(bf16[512,2048]{1,0:T(8,128)(2,1)} %copy-done), slice={[0:512], [1024:2048]} | slice | bytes 2097152 | tf_op jit(solution)/shard_map/slice | solution.py:297
  41.6 0.1 copy.42
  41.7 0.9 add_select_fusion
  42.6 0.1 convert_element_type.49
  42.7 1.3 reshape.103.lim_ref
  44.0 21.5 %all-to-all-done = bf16[16,64,1024]{2,1,0:T(8,128)(2,1)S(1)} async-done(((bf16[16,64,1024]{2,1,0:T(8,128)(2,1)}), bf16[16,64,1024]{2,1,0:T(8,128)(2,1)S(1)}, u32[]{:S(2)}, u32[]{:S(2)}) %all-to-all-start) | async-done | bytes 2097184 | tf_op jit(solution)/shard_map/all_to_all | solution.py:305
  65.5 1.6 copy.36
  67.1 2.5 %broadcast_in_dim.20.acc_ref = f32[1024,1024]{1,0:T(8,128)} broadcast(f32[]{:T(128)} %constant.32.clone.1), dimensions={} | broadcast | bytes 4194308 | tf_op jit(solution)/shard_map/broadcast_in_dim | solution.py:326
  69.6 7.8 %shard_map.82.start_hbm = f32[1024,1024]{1,0:T(8,128)} custom-call(s32[1]{0:T(128)} %bitcast.13.base_ref, bf16[1024,1024]{1,0:T(8,128)(2,1)} %bitcast.43, s32[1024,1]{1,0:T(8,128)} %reshape.103.lim_ref, bf16[256,2048]{1,0:T(8,128)(2,1)} %bitcast.45, f32[1024,1024]{1,0:T(8,128)} %broadcast_in_dim.20.acc_ref), custom_call_target="tpu_custom_call", output_to_operand_aliasing={{}: (4, {})} | custom-call | flops 1073741824 | bytes 11534336 | tf_op jit(solution)/shard_map/pallas_call | solution.py:70
  77.4 51.2 %all-gather.3.cloned.1.call-done = bf16[1,2048,2048]{2,1,0:T(8,128)(2,1)} async-done(((bf16[1,256,2048]{2,1,0:T(8,128)(2,1)}), bf16[1,2048,2048]{2,1,0:T(8,128)(2,1)}) %all-gather.3.cloned.1.call-update) | async-done | bytes 8388624 | tf_op jit(solution)/shard_map/all_gather | solution.py:328
  128.6 42.8 %shard_map.83 = bf16[512,1024]{1,0:T(8,128)(2,1)} custom-call(bf16[1024,1024]{1,0:T(8,128)(2,1)} %bitcast.44, s32[1024,1]{1,0:T(8,128)} %reshape.103.lim_ref, f32[1,1024]{1,0:T(1,128)} %bitcast.54, s32[512,1]{1,0:T(8,128)} %get-tuple-element.6.cola_ref, s32[512,1]{1,0:T(8,128)} %get-tuple-element.5.colb_ref, bf16[2048,2048]{1,0:T(8,128)(2,1)} %bitcast.53, ...), custom_call_target="tpu_custom_call" | custom-call | flops 21474836480 | bytes 23068672 | tf_op jit(solution)/shard_map/pallas_call | solution.py:258
  171.4 2.3 %copy.53 = bf16[512,1024]{1,0:T(8,128)(2,1)} copy(bf16[512,1024]{1,0:T(8,128)(2,1)} %shard_map.83) | data formatting | bytes 2097152
  (4 shorter events, 0.1 us)
Async XLA Ops:
  6.5 122.0 %all-gather.3.cloned.1.call-start = ((), (), s32[]{:S(2)}) async-start(), calls=%async_computation.2 | async-start | bytes 9437184 | tf_op jit(solution)/shard_map/all_gather | solution.py:328
  15.9 16.8 %all-to-all-start.1 = ((bf16[16,1,64]{2,1,0:T(2,128)(2,1)}), bf16[16,1,64]{2,1,0:T(2,128)(2,1)S(1)}, u32[]{:S(2)}, u32[]{:S(2)}) async-start(bf16[16,1,64]{2,1,0:T(2,128)(2,1)} %all_to_all.12), calls=%async_computation.1 | async-start | bytes 16384 | tf_op jit(solution)/shard_map/all_to_all | solution.py:312
  28.5 4.2 %copy-start = (bf16[512,2048]{1,0:T(8,128)(2,1)}, bf16[512,2048]{1,0:T(8,128)(2,1)S(1)}, u32[]{:S(2)}) copy-start(bf16[512,2048]{1,0:T(8,128)(2,1)S(1)} %multiply_convert_fusion) | copy-start | bytes 6291460
  32.8 32.8 %all-to-all-start = ((bf16[16,64,1024]{2,1,0:T(8,128)(2,1)}), bf16[16,64,1024]{2,1,0:T(8,128)(2,1)S(1)}, u32[]{:S(2)}, u32[]{:S(2)}) async-start(bf16[16,64,1024]{2,1,0:T(8,128)(2,1)} %bitcast.5), calls=%async_computation | async-start | bytes 4194304 | tf_op jit(solution)/shard_map/all_to_all | solution.py:305
Sparse Core Ops, SparseCore 0:
  9.7 118.8 all-gather.2

commit v14 on v13

--- a/solution.py
+++ b/solution.py
@@ -98,7 +98,7 @@
 
 def fused_kernel(peers, key_rows, q_ref, lim_ref, gain_ref, cola_ref, colb_ref, hist_hbm, start_hbm,
                  x_hbm, gate_hbm, wout_hbm, out_ref, kv_buf, kv_sem, acc, normed, ret, part, xv, gv, wv,
-                 send_sem, recv_sem, local_sem, start_sem, misc_sem):
+                 sbuf, send_sem, recv_sem, local_sem, start_sem, misc_sem):
     me = lax.axis_index("cand")
     uid = lax.axis_index("user")
     rows, width = q_ref.shape
@@ -119,7 +119,9 @@
 
     def start_copy(half):
         return pltpu.make_async_copy(
-            start_hbm.at[pl.ds(half * half_rows, half_rows)], acc.at[half], start_sem.at[half]
+            start_hbm.at[pl.ds(half * half_rows, half_rows)],
+            sbuf if half == 0 else acc.at[half],
+            start_sem.at[half],
         )
 
     def kv_copy(s, slot):
@@ -186,8 +188,11 @@
         return jnp.dot(mixed, wv[...], preferred_element_type=jnp.float32)
 
     for half in range(2):
-        start_copy(half).wait()
         total = acc.at[half]
+        if half == 0:
+            total[...] = jnp.zeros_like(total)
+        else:
+            start_copy(half).wait()
 
         def step(i, carry, half=half, total=total):
             s = half * segments + i
@@ -221,7 +226,11 @@
         if half == 0:
             for copy in misc:
                 copy.start()
-        value = total[...]
+        if half == 0:
+            start_copy(0).wait()
+            value = total[...] + sbuf[...]
+        else:
+            value = total[...]
         mean_row = jnp.mean(value, axis=1, keepdims=True)
         centered = value - mean_row
         variance = jnp.mean(centered * centered, axis=1, keepdims=True)
@@ -270,6 +279,7 @@
             pltpu.VMEM((homes, width), jnp.bfloat16),
             pltpu.VMEM((homes, width), jnp.bfloat16),
             pltpu.VMEM(w_out.shape, jnp.bfloat16),
+            pltpu.VMEM((rows // 2, width), jnp.float32),
             pltpu.SemaphoreType.DMA((2, peers)),
             pltpu.SemaphoreType.DMA((2, peers)),
             pltpu.SemaphoreType.DMA((2,)),

time: 181 us -> 182 us (level)
  no operation moved by 1% of the time
where the time goes in v14:
time: 182 us; the launch traced here: 181 us
  waiting for transfers between devices  73.4 us (40%)
  Pallas kernels  51.4 us (28%)
  local copies, waits for them, and re-layouts  19.2 us (11%)
  between operations  14.1 us (8%)
  starting transfers between devices  12.6 us (7%)
  matrix products  5.77 us (3%)
  other arithmetic  4.89 us (3%)
    all_gather x1, waiting for transfers between devices, per_device(): history = lax.all_gather(segment, 'user', axis=0, tiled=True)  51.2 us
    pallas_call x1, Pallas kernels, attend_and_return(): pl.pallas_call(kernel, out_shape=jax.ShapeDtypeStruct((homes, width), jnp...  43.6 us
    all_to_all x1, waiting for transfers between devices, per_device(): lax.all_to_all(send_rows.reshape(columns, capacity, width), 'cand', split...  21.5 us
    pallas_call x1, Pallas kernels, attend(): pl.pallas_call(kernel, out_shape=jax.ShapeDtypeStruct((rows, width), jnp....  7.8 us
    all_to_all x1, starting transfers between devices, per_device(): lax.all_to_all(send_vis.reshape(columns, capacity), 'cand', split_axis=0,...  6.83 us
    dot_general x1, matrix products, per_device(): jnp.dot(cand_x, w_in, preferred_element_type=jnp.float32)  5.77 us
    all_to_all x1, starting transfers between devices, per_device(): lax.all_to_all(send_rows.reshape(columns, capacity, width), 'cand', split...  5.72 us
    scatter x1, local copies, waits for them, and re-layouts, per_device(): send_rows = jnp.zeros((slots, width), jnp.bfloat16).at[slot_of].set(queries)  4.2 us
  transfers between devices with their start and end apart: 3, of which 2 were waited for; matrix products, arithmetic and copies ran while one was open for 15% of the time, Pallas kernels for 4%

profile of v14, /device:TPU:1, one launch (start us, length us, event | category | flops | bytes accessed | tf_op | source)
XLA Modules:
  0.0 181.3 jit_solution(1811729935236250070)
XLA Ops:
  6.5 0.0 all-gather.3.cloned.1.call-start
  6.5 0.7 all-gather.3.cloned.1.call-update
  7.3 0.7 fusion.6
  7.9 1.1 reduce-window.6
  9.1 0.2 slice_reduce_fusion
  9.3 0.7 convert_element_type.46
  10.0 0.8 fusion.5
  10.8 0.7 broadcast_multiply_fusion
  11.5 3.8 %scatter_custom_fusion.1 = bf16[1024]{0:T(1024)(128)(2,1)S(1)} fusion(s32[512]{0:T(512)S(1)} %bitcast.51, bf16[512]{0:T(512)(128)(2,1)S(1)} %convert_element_type.46, bf16[]{:T(256)} %constant.12.clone.1), kind=kCustom, calls=%fused_computation.20 | custom fusion | bytes 2050 | tf_op jit(solution)/shard_map/scatter | solution.py:313
  15.3 0.7 all_to_all.12
  15.9 6.8 %all-to-all-start.1 = ((bf16[16,1,64]{2,1,0:T(2,128)(2,1)}), bf16[16,1,64]{2,1,0:T(2,128)(2,1)S(1)}, u32[]{:S(2)}, u32[]{:S(2)}) async-start(bf16[16,1,64]{2,1,0:T(2,128)(2,1)} %all_to_all.12), calls=%async_computation.1 | async-start | bytes 16384 | tf_op jit(solution)/shard_map/all_to_all | solution.py:322
  22.8 5.8 %multiply_convert_fusion = bf16[512,2048]{1,0:T(8,128)(2,1)S(1)} fusion(bf16[512,1024]{1,0:T(8,128)(2,1)} %x_hbm.1, bf16[1024,2048]{1,0:T(8,128)(2,1)} %param.13), kind=kOutput, calls=%fused_computation.2 | convolution fusion | flops 2152726528 | bytes 7340032 | tf_op jit(solution)/shard_map/dot_general | solution.py:305
  28.5 0.0 copy-start
  28.6 4.2 %scatter_custom_fusion = bf16[1024,1024]{1,0:T(8,128)(2,1)} fusion(s32[512]{0:T(512)S(1)} %bitcast.52, bf16[512,2048]{1,0:T(8,128)(2,1)S(1)} %multiply_convert_fusion, bf16[]{:T(256)} %constant.12.clone.1), kind=kCustom, calls=%fused_computation.3 | custom fusion | bytes 3145730 | tf_op jit(solution)/shard_map/scatter | solution.py:312
  32.8 0.0 all-to-all-done.1
  32.8 0.0 copy-done
  32.8 5.7 %all-to-all-start = ((bf16[16,64,1024]{2,1,0:T(8,128)(2,1)}), bf16[16,64,1024]{2,1,0:T(8,128)(2,1)S(1)}, u32[]{:S(2)}, u32[]{:S(2)}) async-start(bf16[16,64,1024]{2,1,0:T(8,128)(2,1)} %bitcast.5), calls=%async_computation | async-start | bytes 4194304 | tf_op jit(solution)/shard_map/all_to_all | solution.py:315
  38.5 0.1 copy.40
  38.6 2.3 %slice.20.gate_hbm = bf16[512,1024]{1,0:T(8,128)(2,1)} slice(bf16[512,2048]{1,0:T(8,128)(2,1)} %copy-done), slice={[0:512], [1024:2048]} | slice | bytes 2097152 | tf_op jit(solution)/shard_map/slice | solution.py:307
  41.6 0.1 copy.42
  41.7 0.9 add_select_fusion
  42.6 0.1 convert_element_type.49
  42.7 1.3 reshape.103.lim_ref
  44.0 21.5 %all-to-all-done = bf16[16,64,1024]{2,1,0:T(8,128)(2,1)S(1)} async-done(((bf16[16,64,1024]{2,1,0:T(8,128)(2,1)}), bf16[16,64,1024]{2,1,0:T(8,128)(2,1)S(1)}, u32[]{:S(2)}, u32[]{:S(2)}) %all-to-all-start) | async-done | bytes 2097184 | tf_op jit(solution)/shard_map/all_to_all | solution.py:315
  65.5 1.6 copy.36
  67.1 2.5 %broadcast_in_dim.20.acc_ref = f32[1024,1024]{1,0:T(8,128)} broadcast(f32[]{:T(128)} %constant.32.clone.1), dimensions={} | broadcast | bytes 4194308 | tf_op jit(solution)/shard_map/broadcast_in_dim | solution.py:336
  69.6 7.8 %shard_map.82.start_hbm = f32[1024,1024]{1,0:T(8,128)} custom-call(s32[1]{0:T(128)} %bitcast.13.base_ref, bf16[1024,1024]{1,0:T(8,128)(2,1)} %bitcast.43, s32[1024,1]{1,0:T(8,128)} %reshape.103.lim_ref, bf16[256,2048]{1,0:T(8,128)(2,1)} %bitcast.45, f32[1024,1024]{1,0:T(8,128)} %broadcast_in_dim.20.acc_ref), custom_call_target="tpu_custom_call", output_to_operand_aliasing={{}: (4, {})} | custom-call | flops 1073741824 | bytes 11534336 | tf_op jit(solution)/shard_map/pallas_call | solution.py:70
  77.4 51.2 %all-gather.3.cloned.1.call-done = bf16[1,2048,2048]{2,1,0:T(8,128)(2,1)} async-done(((bf16[1,256,2048]{2,1,0:T(8,128)(2,1)}), bf16[1,2048,2048]{2,1,0:T(8,128)(2,1)}) %all-gather.3.cloned.1.call-update) | async-done | bytes 8388624 | tf_op jit(solution)/shard_map/all_gather | solution.py:338
  128.6 43.6 %shard_map.83 = bf16[512,1024]{1,0:T(8,128)(2,1)} custom-call(bf16[1024,1024]{1,0:T(8,128)(2,1)} %bitcast.44, s32[1024,1]{1,0:T(8,128)} %reshape.103.lim_ref, f32[1,1024]{1,0:T(1,128)} %bitcast.54, s32[512,1]{1,0:T(8,128)} %get-tuple-element.6.cola_ref, s32[512,1]{1,0:T(8,128)} %get-tuple-element.5.colb_ref, bf16[2048,2048]{1,0:T(8,128)(2,1)} %bitcast.53, ...), custom_call_target="tpu_custom_call" | custom-call | flops 21474836480 | bytes 23068672 | tf_op jit(solution)/shard_map/pallas_call | solution.py:267
  172.2 2.3 %copy.53 = bf16[512,1024]{1,0:T(8,128)(2,1)} copy(bf16[512,1024]{1,0:T(8,128)(2,1)} %shard_map.83) | data formatting | bytes 2097152
  (4 shorter events, 0.1 us)
Async XLA Ops:
  6.5 122.0 %all-gather.3.cloned.1.call-start = ((), (), s32[]{:S(2)}) async-start(), calls=%async_computation.2 | async-start | bytes 9437184 | tf_op jit(solution)/shard_map/all_gather | solution.py:338
  15.9 16.8 %all-to-all-start.1 = ((bf16[16,1,64]{2,1,0:T(2,128)(2,1)}), bf16[16,1,64]{2,1,0:T(2,128)(2,1)S(1)}, u32[]{:S(2)}, u32[]{:S(2)}) async-start(bf16[16,1,64]{2,1,0:T(2,128)(2,1)} %all_to_all.12), calls=%async_computation.1 | async-start | bytes 16384 | tf_op jit(solution)/shard_map/all_to_all | solution.py:322
  28.5 4.2 %copy-start = (bf16[512,2048]{1,0:T(8,128)(2,1)}, bf16[512,2048]{1,0:T(8,128)(2,1)S(1)}, u32[]{:S(2)}) copy-start(bf16[512,2048]{1,0:T(8,128)(2,1)S(1)} %multiply_convert_fusion) | copy-start | bytes 6291460
  32.8 32.8 %all-to-all-start = ((bf16[16,64,1024]{2,1,0:T(8,128)(2,1)}), bf16[16,64,1024]{2,1,0:T(8,128)(2,1)S(1)}, u32[]{:S(2)}, u32[]{:S(2)}) async-start(bf16[16,64,1024]{2,1,0:T(8,128)(2,1)} %bitcast.5), calls=%async_computation | async-start | bytes 4194304 | tf_op jit(solution)/shard_map/all_to_all | solution.py:315
Sparse Core Ops, SparseCore 0:
  9.7 118.8 all-gather.2
